TPU v7x, 32 devices: a whole 2x2x4 slice. The times are simulated.
32 devices in a mesh: dp: 8 (over z, x), ctx: 4 (over y, core).
Axes of the slice: x: 2, y: 2, z: 4, core: 2. Of those that a mesh axis runs over, the one named last changes fastest.
Arguments:
- states: bfloat16 [32, 1024, 960], P('dp', 'ctx'), may hold values from -6 to 6
- teacher: bfloat16 [32, 1024, 960], P('dp', 'ctx'), may hold values from -6 to 6
- validity: int32 [32, 1024], P('dp', 'ctx'), may hold values from 0 to 1, as said below
- chosen: int32 [32, 1024], P('dp', 'ctx'), may hold values from 0 to 1, as said below
- attn_pack: bfloat16 [960, 2560], P(None, ('dp', 'ctx')), may hold values from -1 to 1
- gate_up: bfloat16 [960, 5120], P(None, ('dp', 'ctx')), may hold values from -0.1875 to 0.1875
- down_proj: bfloat16 [960, 2560], P(None, ('dp', 'ctx')), may hold values from -0.125 to 0.125
- norm_gains: float32 [2, 960], replicated, may hold values from 0.25 to 1.75
- router: float32 [960], replicated, may hold values from -0.12 to 0.12
Outputs:
- states_out: bfloat16 [32, 1024, 960], P('dp', 'ctx')
- mse_loss: float32 [], replicated
- states_grad: float32 [32, 1024, 960], P('dp', 'ctx')
- attn_pack_grad: float32 [960, 2560], P(None, ('dp', 'ctx'))
- gate_up_grad: float32 [960, 5120], P(None, ('dp', 'ctx'))
- down_proj_grad: float32 [960, 2560], P(None, ('dp', 'ctx'))
- norm_gains_grad: float32 [2, 960], replicated
- router_grad: float32 [960], replicated
Inputs may be any that keep to these rules, and one draw needn't show every extreme that they name: `validity`: the first token of every sequence is valid. `chosen`: each sequence has 640 or 641 selected tokens, the first token always among them.
All inputs are finite; a program needn't handle non-finite values.
Results may differ from a plain program's by a relative error of at most 0.012.
Values may be sent and summed in bfloat16 or wider, within the bound.
No kernel may reach another device: no remote copies, remote signals or barrier semaphores. Data moves between devices by JAX's collectives and lax.ppermute only.
A program may use at most 320 MiB of HBM per device.

v0:
```python
import jax
import jax.numpy as jnp
from jax import lax
from jax.sharding import PartitionSpec as P

D = 960
HEADS = 15
KV_HEADS = 5
HEAD = 64
FF = 2560
MICRO = 2


EPS = 1e-05
THETA = 10000.0


def shortened(x):
    return jax.tree.map(lambda a: a.astype(jnp.bfloat16) if a.dtype == jnp.float32 else a, x)


def rope_tables(positions):
    half_head = HEAD // 2
    freqs = THETA ** (-(jnp.arange(half_head).astype(jnp.float32) * 2.0 / HEAD))
    angles = positions.astype(jnp.float32)[:, None] * freqs[None, :]
    return (jnp.cos(angles)[:, None, :], jnp.sin(angles)[:, None, :])


def rotate(values, cosine, sine):
    half_head = HEAD // 2
    first = values[..., :half_head]
    second = values[..., half_head:]
    return jnp.concatenate(
        [first * cosine - second * sine, second * cosine + first * sine], axis=-1
    )


def rotate_back(values, cosine, sine):
    half_head = HEAD // 2
    first = values[..., :half_head]
    second = values[..., half_head:]
    return jnp.concatenate(
        [first * cosine + second * sine, second * cosine - first * sine], axis=-1
    )


def norm_back(grad_out, values, inv_rms, gain_row):
    scaled = grad_out * gain_row
    return inv_rms * scaled - values * inv_rms**3 * jnp.mean(
        scaled * values, axis=-1, keepdims=True
    )


def scores_of(queries, keys, allowed):
    scores = (
        jnp.einsum("bqgrh,bkgh->bgrqk", queries, keys, preferred_element_type=jnp.float32) * 0.125
    )
    return jnp.where(allowed, scores, -jnp.inf)


def over_rows(left, right):
    return lax.dot_general(
        left, right, (((0, 1), (0, 1)), ((), ())), preferred_element_type=jnp.float32
    )


def by_columns(left, right):
    return lax.dot_general(
        left, right, (((2,), (1,)), ((), ())), preferred_element_type=jnp.float32
    )


def on_device(states, teacher, validity, chosen, attn_pack, gate_up, down_proj, norm_gains, router):
    seq_count, block_rows, width = states.shape
    seq_micro = seq_count // MICRO
    ctx_count = lax.axis_size("ctx")
    dp_count = lax.axis_size("dp")
    ctx_spot = lax.axis_index("ctx")
    seq_length = block_rows * ctx_count
    qkv_cols = D + 2 * KV_HEADS * HEAD
    kv_width = KV_HEADS * HEAD
    per_kv = HEADS // KV_HEADS
    cosine, sine = rope_tables(ctx_spot * block_rows + jnp.arange(block_rows))
    early_block = jnp.arange(seq_length) // block_rows <= ctx_spot
    valid_all = validity.astype(jnp.float32)
    chosen_all = chosen.astype(jnp.float32)
    key_flags = (validity * chosen).astype(jnp.bfloat16)
    gain_one = norm_gains[0]
    gain_two = norm_gains[1]
    packs = (attn_pack, gate_up, down_proj)
    valid_total = lax.psum(jnp.sum(valid_all), ("dp", "ctx"))
    grad_attn = jnp.zeros((D, qkv_cols + D), jnp.float32)
    grad_gu = jnp.zeros((D, 2 * FF), jnp.float32)
    grad_down = jnp.zeros((D, FF), jnp.float32)
    grad_gain_one = jnp.zeros((D,), jnp.float32)
    grad_gain_two = jnp.zeros((D,), jnp.float32)
    grad_router = jnp.zeros((D,), jnp.float32)
    energy = jnp.zeros((), jnp.float32)
    out_parts = []
    input_grads = []
    for micro_index in range(MICRO):
        lower = micro_index * seq_micro
        upper = lower + seq_micro
        x_float = states[lower:upper].astype(jnp.float32)
        teacher_rows = teacher[lower:upper].astype(jnp.float32)
        valid_rows = valid_all[lower:upper]
        chosen_rows = chosen_all[lower:upper]
        fresh = (
            lax.all_gather(packs[0], ("dp", "ctx"), axis=1, tiled=True),
            lax.all_gather(packs[1], ("dp", "ctx"), axis=1, tiled=True),
            lax.all_gather(packs[2], ("dp", "ctx"), axis=1, tiled=True),
        )
        w_attn, w_gu, w_down = fresh
        inv_one = lax.rsqrt(jnp.mean(x_float * x_float, axis=-1, keepdims=True) + EPS)
        normed = (x_float * inv_one * gain_one).astype(jnp.bfloat16)
        mixed = jnp.dot(normed, w_attn[:, :qkv_cols], preferred_element_type=jnp.float32)
        queries = mixed[..., :D].reshape(seq_micro, block_rows, HEADS, HEAD)
        keys = mixed[..., D : D + kv_width].reshape(seq_micro, block_rows, KV_HEADS, HEAD)
        values_in = mixed[..., D + kv_width :].reshape(seq_micro, block_rows, KV_HEADS, HEAD)
        rot_queries = (
            rotate(queries, cosine, sine)
            .astype(jnp.bfloat16)
            .reshape(seq_micro, block_rows, KV_HEADS, per_kv, HEAD)
        )
        rot_keys = rotate(keys, cosine, sine).astype(jnp.bfloat16)
        value_low = values_in.astype(jnp.bfloat16)
        keys_all, values_all, flags_all = (
            lax.all_gather(rot_keys, "ctx", axis=1, tiled=True),
            lax.all_gather(value_low, "ctx", axis=1, tiled=True),
            lax.all_gather(key_flags[lower:upper], "ctx", axis=1, tiled=True),
        )
        allowed = (early_block[None, :] & (flags_all > 0.5))[:, None, None, None, :]
        scores = scores_of(rot_queries, keys_all, allowed)
        row_max = jnp.max(scores, axis=-1, keepdims=True)
        expd = jnp.exp(scores - row_max)
        row_total = jnp.sum(expd, axis=-1, keepdims=True)
        log_total = row_max + jnp.log(row_total)
        probs_low = (expd / row_total).astype(jnp.bfloat16)
        heads_out = jnp.einsum(
            "bgrqk,bkgh->bqgrh", probs_low, values_all, preferred_element_type=jnp.float32
        )
        heads_low = heads_out.reshape(seq_micro, block_rows, D).astype(jnp.bfloat16)
        attn_out = by_columns(heads_low, w_attn[:, qkv_cols:])
        inner = x_float + attn_out
        inv_two = lax.rsqrt(jnp.mean(inner * inner, axis=-1, keepdims=True) + EPS)
        normed_two = (inner * inv_two * gain_two).astype(jnp.bfloat16)
        gate_both = jnp.dot(normed_two, w_gu, preferred_element_type=jnp.float32)
        gate_part = gate_both[..., :FF]
        up_part = gate_both[..., FF:]
        gate_sig = jax.nn.sigmoid(gate_part)
        hidden = (gate_part * gate_sig * up_part).astype(jnp.bfloat16)
        ffn_out = by_columns(hidden, w_down)
        gate_prob = jax.nn.sigmoid(jnp.dot(x_float, router, precision=lax.Precision.HIGHEST))
        weight_mix = chosen_rows * gate_prob
        branch = attn_out + ffn_out
        result = x_float + weight_mix[..., None] * branch
        out_parts.append(result.astype(jnp.bfloat16))
        diff = valid_rows[..., None] * (result - teacher_rows)
        energy = energy + 0.5 * jnp.sum(diff * diff)
        w_attn, w_gu, w_down = (
            lax.all_gather(packs[0], ("dp", "ctx"), axis=1, tiled=True),
            lax.all_gather(packs[1], ("dp", "ctx"), axis=1, tiled=True),
            lax.all_gather(packs[2], ("dp", "ctx"), axis=1, tiled=True),
        )
        d_branch = weight_mix[..., None] * diff
        d_logit = chosen_rows * jnp.sum(diff * branch, axis=-1) * gate_prob * (1.0 - gate_prob)
        grad_router = grad_router + jnp.einsum(
            "bt,btd->d", d_logit, x_float, precision=lax.Precision.HIGHEST
        )
        d_states = diff + d_logit[..., None] * router
        d_ffn = d_branch.astype(jnp.bfloat16)
        d_hidden = jnp.dot(d_ffn, w_down, preferred_element_type=jnp.float32)
        grad_down = grad_down + over_rows(d_ffn, hidden)
        d_gate = d_hidden * up_part * gate_sig * (1.0 + gate_part * (1.0 - gate_sig))
        d_up = d_hidden * gate_part * gate_sig
        d_gu_low = jnp.concatenate([d_gate, d_up], axis=-1).astype(jnp.bfloat16)
        d_normed_two = by_columns(d_gu_low, w_gu)
        grad_gu = grad_gu + over_rows(normed_two, d_gu_low)
        grad_gain_two = grad_gain_two + jnp.sum(d_normed_two * inner * inv_two, axis=(0, 1))
        d_inner = norm_back(d_normed_two, inner, inv_two, gain_two)
        d_states = d_states + d_inner
        d_attn_low = (d_branch + d_inner).astype(jnp.bfloat16)
        d_heads = jnp.dot(d_attn_low, w_attn[:, qkv_cols:], preferred_element_type=jnp.float32)
        d_heads_low = d_heads.astype(jnp.bfloat16).reshape(
            seq_micro, block_rows, KV_HEADS, per_kv, HEAD
        )
        grad_out_proj = over_rows(d_attn_low, heads_low)
        probs = jnp.exp(scores_of(rot_queries, keys_all, allowed) - log_total)
        d_probs = jnp.einsum(
            "bqgrh,bkgh->bgrqk", d_heads_low, values_all, preferred_element_type=jnp.float32
        )
        d_scores = (probs * (d_probs - jnp.sum(probs * d_probs, axis=-1, keepdims=True))).astype(
            jnp.bfloat16
        )
        d_queries = (
            jnp.einsum("bgrqk,bkgh->bqgrh", d_scores, keys_all, preferred_element_type=jnp.float32)
            * 0.125
        )
        d_keys_all = (
            jnp.einsum(
                "bgrqk,bqgrh->bkgh", d_scores, rot_queries, preferred_element_type=jnp.float32
            )
            * 0.125
        )
        d_values_all = jnp.einsum(
            "bgrqk,bqgrh->bkgh",
            probs.astype(jnp.bfloat16),
            d_heads_low,
            preferred_element_type=jnp.float32,
        )
        d_keys, d_values = (
            lax.psum_scatter(
                d_keys_all.astype(jnp.bfloat16), "ctx", scatter_dimension=1, tiled=True
            ).astype(jnp.float32),
            lax.psum_scatter(
                d_values_all.astype(jnp.bfloat16), "ctx", scatter_dimension=1, tiled=True
            ).astype(jnp.float32),
        )
        d_queries = rotate_back(d_queries.reshape(seq_micro, block_rows, HEADS, HEAD), cosine, sine)
        d_keys = rotate_back(d_keys, cosine, sine)
        d_mixed = jnp.concatenate(
            [
                d_queries.reshape(seq_micro, block_rows, D),
                d_keys.reshape(seq_micro, block_rows, kv_width),
                d_values.reshape(seq_micro, block_rows, kv_width),
            ],
            axis=-1,
        ).astype(jnp.bfloat16)
        d_normed = by_columns(d_mixed, w_attn[:, :qkv_cols])
        grad_attn = grad_attn + jnp.concatenate([over_rows(normed, d_mixed), grad_out_proj], axis=1)
        grad_gain_one = grad_gain_one + jnp.sum(d_normed * x_float * inv_one, axis=(0, 1))
        d_states = d_states + norm_back(d_normed, x_float, inv_one, gain_one)
        input_grads.append(d_states)

    def owner_layout(grad_whole):
        return grad_whole.reshape(
            D, dp_count, ctx_count, grad_whole.shape[1] // (dp_count * ctx_count)
        )

    by_ctx = (
        lax.all_to_all(
            owner_layout(grad_attn).astype(jnp.bfloat16),
            "ctx",
            split_axis=2,
            concat_axis=2,
            tiled=True,
        ).astype(jnp.float32),
        lax.all_to_all(
            owner_layout(grad_gu).astype(jnp.bfloat16),
            "ctx",
            split_axis=2,
            concat_axis=2,
            tiled=True,
        ).astype(jnp.float32),
        lax.all_to_all(
            owner_layout(grad_down).astype(jnp.bfloat16),
            "ctx",
            split_axis=2,
            concat_axis=2,
            tiled=True,
        ).astype(jnp.float32),
    )
    attn_ctx, gu_ctx, down_ctx = [jnp.sum(piece, axis=2) for piece in by_ctx]
    by_dp = (
        lax.all_to_all(shortened(attn_ctx), "dp", split_axis=1, concat_axis=1, tiled=True).astype(
            attn_ctx.dtype
        ),
        lax.all_to_all(shortened(gu_ctx), "dp", split_axis=1, concat_axis=1, tiled=True).astype(
            gu_ctx.dtype
        ),
        lax.all_to_all(shortened(down_ctx), "dp", split_axis=1, concat_axis=1, tiled=True).astype(
            down_ctx.dtype
        ),
    )
    attn_grad_part, gu_grad_part, down_grad_part = [jnp.sum(piece, axis=1) for piece in by_dp]
    grad_gains = jnp.stack([grad_gain_one, grad_gain_two], axis=0)
    energy_all, gains_all, router_all = lax.psum((energy, grad_gains, grad_router), ("dp", "ctx"))
    mse_loss = 2.0 * energy_all / (valid_total * D)
    return (
        jnp.concatenate(out_parts, axis=0),
        mse_loss,
        jnp.concatenate(input_grads, axis=0),
        attn_grad_part,
        gu_grad_part,
        down_grad_part,
        gains_all,
        router_all,
    )


def solution(mesh):
    placed = (
        P("dp", "ctx", None),
        P("dp", "ctx", None),
        P("dp", "ctx"),
        P("dp", "ctx"),
        P(None, ("dp", "ctx")),
        P(None, ("dp", "ctx")),
        P(None, ("dp", "ctx")),
        P(),
        P(),
    )
    return jax.shard_map(
        on_device,
        mesh=mesh,
        in_specs=placed,
        out_specs=(
            P("dp", "ctx", None),
            P(),
            P("dp", "ctx", None),
            P(None, ("dp", "ctx")),
            P(None, ("dp", "ctx")),
            P(None, ("dp", "ctx")),
            P(),
            P(),
        ),
        check_vma=False,
    )
```

profile of v0, /device:TPU:0, one launch (start us, length us, event | category | flops | bytes accessed | tf_op | source)
XLA Modules:
  0.0 1026.6 jit_solution(13568377429993740406)
XLA Ops:
  10.8 68.1 %all-gather.8.cloned.1.call-done = bf16[960,2560]{0,1:T(8,128)(2,1)} async-done(((bf16[960,80]{0,1:T(8,128)(2,1)}), bf16[960,2560]{0,1:T(8,128)(2,1)}) %all-gather.8.cloned.1.call-update) | async-done | bytes 4915216 | tf_op jit(solution)/shard_map/all_gather | solution.py:109
  78.9 4.1 fusion.97
  95.4 5.2 all_gather.38
  100.6 5.2 all_gather.43
  110.1 15.0 %bitcast_reduce_fusion = (f32[2,5,3,256]{3,2,1,0:T(4,128)S(1)}, f32[2,5,1024,256,3]{3,2,4,1,0:T(8,128)}) fusion(bf16[2,256,5,3,32]{1,4,3,2,0:T(8,128)(2,1)S(1)} %bitcast.322, bf16[2,256,5,3,32]{1,4,3,2,0:T(8,128)(2,1)} %bitcast.324, bf16[2,1024,5,64]{1,3,2,0:T(8,128)(2,1)} %all-gather.20.cloned.1.call-done, pred[2,1024]{1,0:T(4,128)(4,1)S(1)} %get-tuple-element.98), kind=kOutput, calls=%fused_computation.12 | convolution fusion | flops 1032184320 | bytes 33783808 | tf_op jit(solution)/shard_map/bqgrh,bkgh->bgrqk/dot_general | solution.py:56
  125.1 13.0 %fusion.11 = f32[2,5,3,256]{3,2,1,0:T(4,128)S(1)} fusion(f32[2,5,1024,256,3]{3,2,4,1,0:T(8,128)} %get-tuple-element.100, f32[2,5,3,256]{3,2,1,0:T(4,128)S(1)} %get-tuple-element.99), kind=kLoop, calls=%fused_computation.25 | loop fusion | flops 15720960 | bytes 31518720 | tf_op jit(solution)/shard_map/reduce_sum | solution.py:136
  138.1 14.3 %bitcast_reduce_fusion.1 = (f32[2,5,3,256]{3,2,1,0:T(4,128)S(1)}, f32[2,5,1024,256,3]{3,2,4,1,0:T(8,128)}) fusion(bf16[2,256,5,3,32]{1,4,3,2,0:T(8,128)(2,1)S(1)} %bitcast.320, bf16[2,256,5,3,32]{1,4,3,2,0:T(8,128)(2,1)S(1)} %bitcast.318, bf16[2,1024,5,64]{1,3,2,0:T(8,128)(2,1)} %all-gather.12.cloned.1.call-done, pred[2,1024]{1,0:T(4,128)(4,1)S(1)} %get-tuple-element.97), kind=kOutput, calls=%fused_computation.17 | convolution fusion | flops 1032184320 | bytes 33783808 | tf_op jit(solution)/shard_map/bqgrh,bkgh->bgrqk/dot_general | solution.py:56
  152.4 13.1 %fusion.10 = f32[2,5,3,256]{3,2,1,0:T(4,128)S(1)} fusion(f32[2,5,1024,256,3]{3,2,4,1,0:T(8,128)} %get-tuple-element.102, f32[2,5,3,256]{3,2,1,0:T(4,128)S(1)} %get-tuple-element.101), kind=kLoop, calls=%fused_computation.24 | loop fusion | flops 15720960 | bytes 31518720 | tf_op jit(solution)/shard_map/reduce_sum | solution.py:136
  165.5 13.3 %fusion.72 = bf16[2,5,64,3,256]{4,2,3,1,0:T(8,128)(2,1)S(1)} fusion(f32[2,5,1024,256,3]{3,2,4,1,0:T(8,128)} %get-tuple-element.100, f32[2,5,3,256]{3,2,1,0:T(4,128)S(1)} %fusion.11, f32[2,5,3,256]{3,2,1,0:T(4,128)S(1)} %get-tuple-element.99, bf16[2,1024,5,64]{1,3,2,0:T(8,128)(2,1)} %all-gather.18.cloned.1.call-done), kind=kOutput, calls=%fused_computation.144 | convolution fusion | flops 1030717440 | bytes 33812480 | tf_op jit(solution)/shard_map/bgrqk,bkgh->bqgrh/dot_general | solution.py:139
  178.8 4.4 fusion.98
  183.2 13.5 %fusion.73 = bf16[2,5,64,3,256]{4,2,3,1,0:T(8,128)(2,1)S(1)} fusion(f32[2,5,1024,256,3]{3,2,4,1,0:T(8,128)} %get-tuple-element.102, f32[2,5,3,256]{3,2,1,0:T(4,128)S(1)} %fusion.10, f32[2,5,3,256]{3,2,1,0:T(4,128)S(1)} %get-tuple-element.101, bf16[2,1024,5,64]{1,3,2,0:T(8,128)(2,1)} %all-gather.10.cloned.1.call-done), kind=kOutput, calls=%fused_computation.145 | convolution fusion | flops 1030717440 | bytes 33812480 | tf_op jit(solution)/shard_map/bgrqk,bkgh->bqgrh/dot_general | solution.py:139
  196.8 5.7 multiply_reduce_fusion.9
  203.2 51.0 %all-gather.14.cloned.1.call-done = bf16[960,5120]{0,1:T(8,128)(2,1)} async-done(((bf16[960,160]{0,1:T(8,128)(2,1)}), bf16[960,5120]{0,1:T(8,128)(2,1)}) %all-gather.14.cloned.1.call-update) | async-done | bytes 9830416 | tf_op jit(solution)/shard_map/all_gather | solution.py:110
  254.2 9.5 fusion.27
  268.7 8.9 fusion.29
  277.6 3.9 copy-done.6
  284.6 36.3 %all-gather.16.cloned.1.call-done = bf16[960,2560]{0,1:T(8,128)(2,1)} async-done(((bf16[960,80]{0,1:T(8,128)(2,1)}), bf16[960,2560]{0,1:T(8,128)(2,1)}) %all-gather.16.cloned.1.call-update) | async-done | bytes 4915216 | tf_op jit(solution)/shard_map/all_gather | solution.py:111
  320.9 8.0 fusion.66
  329.0 10.3 multiply_reduce_fusion.3
  339.3 11.5 %multiply_convert_fusion.3 = (bf16[2,256,2560]{2,1,0:T(8,128)(2,1)S(1)}, bf16[2,256,2560]{2,1,0:T(8,128)(2,1)}) fusion(f32[2,256,5120]{2,1,0:T(8,128)} %copy-done.6, bf16[960,2560]{0,1:T(8,128)(2,1)} %all-gather.16.cloned.1.call-done, f32[2,256,960]{1,2,0:T(8,128)S(1)} %get-tuple-element.43, f32[2,256]{1,0:T(2,128)S(1)} %copy-done.48), kind=kOutput, calls=%fused_computation.62 | convolution fusion | flops 2534604800 | bytes 22611968 | tf_op jit(solution)/shard_map/dot_general | solution.py:172
  350.9 10.2 multiply_convert_fusion.1
  361.0 13.7 %fusion.25 = f32[2,256,960]{1,2,0:T(8,128)} fusion(bf16[960,5120]{0,1:T(8,128)(2,1)} %all-gather.14.cloned.1.call-done, bf16[2,256,2560]{2,1,0:T(8,128)(2,1)} %get-tuple-element.37, bf16[2,256,2560]{2,1,0:T(8,128)(2,1)S(1)} %get-tuple-element.36), kind=kOutput, calls=%fused_computation.38 | convolution fusion | flops 5043650560 | bytes 17039360 | tf_op jit(solution)/shard_map/dot_general | solution.py:68
  374.7 15.0 %multiply_reduce_fusion = (f32[960]{0:T(1024)}, f32[2,256]{1,0:T(2,128)S(1)}, f32[2,256]{1,0:T(2,128)S(1)}, f32[960]{0:T(1024)}, f32[2,256,960]{1,2,0:T(8,128)}) fusion(f32[2,256,960]{1,2,0:T(8,128)} %get-tuple-element.53, f32[2,256]{1,0:T(2,128)S(1)} %get-tuple-element.90, f32[960]{0:T(1024)S(1)} %bitcast.340, f32[2,256,960]{1,2,0:T(8,128)} %get-tuple-element.31, ...), kind=kOutput, calls=%fused_computation.116 | convolution fusion | flops 5049545728 | bytes 22957312 | tf_op jit(solution)/shard_map/dot_general | solution.py:68
  389.7 5.9 add_convert_fusion
  398.8 24.2 %fusion = (f32[2,5,3,256]{3,2,1,0:T(4,128)S(1)}, f32[2,5,1024,256,3]{3,2,4,1,0:T(8,128)}) fusion(f32[2,5,1024,256,3]{3,2,4,1,0:T(8,128)} %get-tuple-element.100, f32[2,5,3,256]{3,2,1,0:T(4,128)S(1)} %log_add_fusion, bf16[2,256,5,3,64]{1,4,3,2,0:T(8,128)(2,1)S(1)} %bitcast.312, bf16[2,1024,5,64]{1,3,2,0:T(8,128)(2,1)S(1)} %copy-done.26), kind=kOutput, calls=%fused_computation.2 | convolution fusion | flops 1030218240 | bytes 65269760 | tf_op jit(solution)/shard_map/bqgrh,bkgh->bgrqk/dot_general | solution.py:189
  423.1 26.8 %fusion.2 = bf16[2,5,3,256,1024]{3,4,2,1,0:T(8,128)(2,1)} fusion(f32[2,5,1024,256,3]{3,2,4,1,0:T(8,128)} %get-tuple-element.106, f32[2,5,1024,256,3]{3,2,4,1,0:T(8,128)} %get-tuple-element.100, f32[2,5,3,256]{3,2,1,0:T(4,128)S(1)} %get-tuple-element.105, f32[2,5,3,256]{3,2,1,0:T(4,128)S(1)} %log_add_fusion), kind=kLoop, calls=%fused_computation.4 | loop fusion | flops 31457280 | bytes 78704640 | tf_op jit(solution)/shard_map/convert_element_type | solution.py:192
  449.9 11.4 %fusion.81 = bf16[2,1024,5,64]{1,3,2,0:T(8,128)(2,1)} fusion(bf16[2,5,3,256,1024]{3,4,2,1,0:T(8,128)(2,1)} %fusion.2, bf16[2,256,5,3,32]{1,4,3,2,0:T(8,128)(2,1)S(1)} %bitcast.323, bf16[2,256,5,3,32]{1,4,3,2,0:T(8,128)(2,1)S(1)} %bitcast.325), kind=kOutput, calls=%fused_computation.149 | convolution fusion | flops 1009909760 | bytes 18022400 | tf_op jit(solution)/shard_map/bgrqk,bqgrh->bkgh/dot_general | solution.py:200
  464.5 24.4 %fusion.3 = (f32[2,5,3,256]{3,2,1,0:T(4,128)S(1)}, f32[2,5,1024,256,3]{3,2,4,1,0:T(8,128)}) fusion(f32[2,5,1024,256,3]{3,2,4,1,0:T(8,128)} %get-tuple-element.102, f32[2,5,3,256]{3,2,1,0:T(4,128)S(1)} %copy-done.30, bf16[2,256,5,3,64]{1,4,3,2,0:T(8,128)(2,1)S(1)} %bitcast.310, bf16[2,1024,5,64]{1,3,2,0:T(8,128)(2,1)S(1)} %copy-done.25), kind=kOutput, calls=%fused_computation.7 | convolution fusion | flops 1030218240 | bytes 65269760 | tf_op jit(solution)/shard_map/bqgrh,bkgh->bgrqk/dot_general | solution.py:189
  488.9 26.6 %fusion.5 = bf16[2,5,3,256,1024]{3,4,2,1,0:T(8,128)(2,1)} fusion(f32[2,5,1024,256,3]{3,2,4,1,0:T(8,128)} %get-tuple-element.108, f32[2,5,1024,256,3]{3,2,4,1,0:T(8,128)} %get-tuple-element.102, f32[2,5,3,256]{3,2,1,0:T(4,128)S(1)} %get-tuple-element.107, f32[2,5,3,256]{3,2,1,0:T(4,128)S(1)} %copy-done.30), kind=kLoop, calls=%fused_computation.9 | loop fusion | flops 31457280 | bytes 78704640 | tf_op jit(solution)/shard_map/convert_element_type | solution.py:192
  515.5 11.5 %fusion.80 = bf16[2,1024,5,64]{1,3,2,0:T(8,128)(2,1)} fusion(bf16[2,5,3,256,1024]{3,4,2,1,0:T(8,128)(2,1)} %fusion.5, bf16[2,256,5,3,32]{1,4,3,2,0:T(8,128)(2,1)} %bitcast.321, bf16[2,256,5,3,32]{1,4,3,2,0:T(8,128)(2,1)S(1)} %bitcast.319), kind=kOutput, calls=%fused_computation.148 | convolution fusion | flops 1009909760 | bytes 18022400 | tf_op jit(solution)/shard_map/bgrqk,bqgrh->bkgh/dot_general | solution.py:200
  527.1 14.7 %fusion.77 = bf16[2,1024,5,64]{1,3,2,0:T(8,128)(2,1)} fusion(bf16[2,256,5,3,64]{1,4,3,2,0:T(8,128)(2,1)} %bitcast.313, f32[2,5,1024,256,3]{3,2,4,1,0:T(8,128)} %get-tuple-element.100, f32[2,5,3,256]{3,2,1,0:T(4,128)S(1)} %log_add_fusion), kind=kOutput, calls=%fused_computation.147 | convolution fusion | flops 1023016960 | bytes 33781760 | tf_op jit(solution)/shard_map/bgrqk,bqgrh->bkgh/dot_general | solution.py:205
  541.9 4.6 fusion.100
  546.5 4.4 fusion.32
  550.9 7.9 copy.60
  558.8 5.9 copy.61
  564.7 5.1 all-to-all-start.4
  569.8 14.1 %fusion.74 = bf16[2,1024,5,64]{1,3,2,0:T(8,128)(2,1)} fusion(bf16[2,256,5,3,64]{1,4,3,2,0:T(8,128)(2,1)S(1)} %bitcast.311, f32[2,5,1024,256,3]{3,2,4,1,0:T(8,128)} %get-tuple-element.102, f32[2,5,3,256]{3,2,1,0:T(4,128)S(1)} %copy-done.30), kind=kOutput, calls=%fused_computation.146 | convolution fusion | flops 1023016960 | bytes 33781760 | tf_op jit(solution)/shard_map/bgrqk,bqgrh->bkgh/dot_general | solution.py:205
  585.2 8.3 convolution_multiply_fusion
  593.6 8.8 convolution_multiply_fusion.1
  608.1 35.2 %all-to-all-done.4 = bf16[960,8,4,80]{0,3,1,2:T(8,128)(2,1)} async-done(((bf16[960,8,4,80]{0,3,1,2:T(8,128)(2,1)}), bf16[960,8,4,80]{0,3,1,2:T(8,128)(2,1)}, u32[]{:S(2)}, u32[]{:S(2)}) %all-to-all-start.4) | async-done | bytes 4915232 | tf_op jit(solution)/shard_map/all_to_all | solution.py:255
  643.2 5.2 reduce_sum.273
  648.4 4.3 all-to-all-start.5
  663.4 6.1 convolution_bitcast_fusion
  669.5 3.6 convolution_bitcast_fusion.1
  673.9 6.9 fusion.31
  680.9 7.8 copy.54
  688.7 5.7 copy.55
  694.4 5.5 all-to-all-start
  699.9 12.3 %fusion.41 = f32[960,5120,1]{1,0,2:T(8,128)} fusion(bf16[2,256,2560]{2,1,0:T(8,128)(2,1)} %get-tuple-element.37, bf16[2,256,2560]{2,1,0:T(8,128)(2,1)} %copy-done.95, f32[2,256,960]{1,2,0:T(8,128)} %get-tuple-element.31, f32[960]{0:T(1024)S(1)} %bitcast.342, f32[2,256]{1,0:T(2,128)S(1)} %copy-done.56), kind=kOutput, calls=%fused_computation.84 | convolution fusion | flops 5045125120 | bytes 26875648 | tf_op jit(solution)/shard_map/dot_general | solution.py:62
  712.1 13.8 %fusion.14 = bf16[960,5120]{1,0:T(8,128)(2,1)} fusion(f32[960,5120,1]{1,0,2:T(8,128)} %fusion.41, bf16[2,256,2560]{2,1,0:T(8,128)(2,1)} %get-tuple-element.35, bf16[2,256,2560]{2,1,0:T(8,128)(2,1)} %get-tuple-element.34, f32[2,256,960]{1,2,0:T(8,128)} %get-tuple-element.53, f32[2,256]{1,0:T(2,128)S(1)} %copy-done.60, f32[960]{0:T(1024)S(1)} %bitcast.343), kind=kOutput, calls=%fused_computation.29 | convolution fusion | flops 5054955520 | bytes 36706048 | tf_op jit(solution)/shard_map/dot_general | solution.py:62
  725.9 14.2 %copy.57 = bf16[960,5120]{0,1:T(8,128)(2,1)} copy(bf16[960,5120]{1,0:T(8,128)(2,1)} %fusion.14) | data formatting | bytes 19660800 | tf_op jit(solution)/shard_map/convert_element_type | solution.py:249
  740.2 9.9 copy.58
  750.0 9.2 all-to-all-done
  759.2 6.0 all-to-all-start.2
  765.2 5.2 reduce_sum.269
  770.4 110.4 %all-to-all-done.2 = bf16[960,8,4,160]{0,3,1,2:T(8,128)(2,1)} async-done(((bf16[960,8,4,160]{0,3,1,2:T(8,128)(2,1)}), bf16[960,8,4,160]{0,3,1,2:T(8,128)(2,1)}, u32[]{:S(2)}, u32[]{:S(2)}) %all-to-all-start.2) | async-done | bytes 9830432 | tf_op jit(solution)/shard_map/all_to_all | solution.py:248
  880.8 6.2 all-to-all-start.1
  887.7 9.2 reduce_sum.271
  896.9 21.3 %all-to-all-done.1 = bf16[960,8,80]{0,2,1:T(8,128)(2,1)} async-done(((bf16[960,8,80]{0,2,1:T(8,128)(2,1)}), bf16[960,8,80]{0,2,1:T(8,128)(2,1)}, u32[]{:S(2)}, u32[]{:S(2)}) %all-to-all-start.1) | async-done | bytes 1228832 | tf_op jit(solution)/shard_map/all_to_all | solution.py:265
  918.2 4.4 all-to-all-start.3
  925.9 4.0 fusion.94
  930.0 6.3 fusion.52
  937.8 63.9 %all-reduce = (f32[]{:T(128)}, f32[]{:T(128)}, f32[2,960]{1,0:T(2,128)}, f32[960]{0:T(1024)}) all-reduce(f32[]{:T(128)S(6)} %add.239, f32[]{:T(128)} %convert_reduce_fusion.3, f32[2,960]{1,0:T(2,128)S(1)} %pad_maximum_fusion.26, f32[960]{0:T(1024)S(1)} %add.263), channel_id=1, replica_groups=mesh['dp'=8,'ctx'=4] {'dp','ctx'}, use_global_device_ids=true, to_apply=%region_10.11 | all-reduce | flops 2882 | bytes 23056 | tf_op jit(solution)/shard_map/psum | solution.py:277
  1003.2 4.1 fusion.58
  (293 shorter events, 69.2 us)
Async XLA Ops:
  7.2 71.7 %copy-start = (bf16[4,256,960]{1,2,0:T(8,128)(2,1)S(1)}, bf16[4,256,960]{1,2,0:T(8,128)(2,1)}, u32[]{:S(2)}) copy-start(bf16[4,256,960]{1,2,0:T(8,128)(2,1)} %param.9) | copy-start | bytes 5898244
  7.2 71.7 %all-gather.8.cloned.1.call-start = ((), (), s32[]{:S(2)}) async-start(), calls=%async_computation.10 | async-start | bytes 5406720 | tf_op jit(solution)/shard_map/all_gather | solution.py:109
  7.9 102.2 %all-gather.20.cloned.1.call-start = ((), (), s32[]{:S(2)}) async-start(), calls=%async_computation.16 | async-start | bytes 1638400 | tf_op jit(solution)/shard_map/all_gather | solution.py:128
  10.5 72.5 %copy-start.75 = (f32[2,256]{1,0:T(2,128)}, f32[2,256]{1,0:T(2,128)S(1)}, u32[]{:S(2)}) copy-start(f32[2,256]{1,0:T(2,128)S(1)} %get-tuple-element.88) | copy-start | bytes 6148
  10.5 72.5 %copy-start.71 = (f32[2,256]{1,0:T(2,128)}, f32[2,256]{1,0:T(2,128)S(1)}, u32[]{:S(2)}) copy-start(f32[2,256]{1,0:T(2,128)S(1)} %get-tuple-element.110) | copy-start | bytes 6148
  10.5 72.5 %copy-start.49 = (f32[1,960]{1,0:T(1,128)}, f32[1,960]{1,0:T(1,128)S(1)}, u32[]{:S(2)}) copy-start(f32[1,960]{1,0:T(1,128)S(1)} %get-tuple-element.71) | copy-start | bytes 11524
  10.5 379.1 %copy-start.44 = (f32[1,960]{1,0:T(1,128)}, f32[1,960]{1,0:T(1,128)S(1)}, u32[]{:S(2)}) copy-start(f32[1,960]{1,0:T(1,128)S(1)} %get-tuple-element.70) | copy-start | bytes 11524
  10.7 95.8 %copy-start.38 = (f32[256,32]{0,1:T(8,128)}, f32[256,32]{0,1:T(8,128)S(1)}, u32[]{:S(2)}) copy-start(f32[256,32]{0,1:T(8,128)S(1)} %get-tuple-element.95) | copy-start | bytes 98308
  10.8 95.8 %copy-start.40 = (f32[256,32]{0,1:T(8,128)}, f32[256,32]{0,1:T(8,128)S(1)}, u32[]{:S(2)}) copy-start(f32[256,32]{0,1:T(8,128)S(1)} %get-tuple-element.96) | copy-start | bytes 98308
  87.7 50.4 %all-gather.12.cloned.1.call-start = ((), (), s32[]{:S(2)}) async-start(), calls=%async_computation.12 | async-start | bytes 1638400 | tf_op jit(solution)/shard_map/all_gather | solution.py:128
  88.5 77.0 %all-gather.18.cloned.1.call-start = ((), (), s32[]{:S(2)}) async-start(), calls=%async_computation.15 | async-start | bytes 1638400 | tf_op jit(solution)/shard_map/all_gather | solution.py:129
  90.5 92.7 %all-gather.10.cloned.1.call-start = ((), (), s32[]{:S(2)}) async-start(), calls=%async_computation.11 | async-start | bytes 1638400 | tf_op jit(solution)/shard_map/all_gather | solution.py:129
  92.4 161.8 %all-gather.14.cloned.1.call-start = ((), (), s32[]{:S(2)}) async-start(), calls=%async_computation.13 | async-start | bytes 10813440 | tf_op jit(solution)/shard_map/all_gather | solution.py:110
  93.0 227.9 %all-gather.16.cloned.1.call-start = ((), (), s32[]{:S(2)}) async-start(), calls=%async_computation.14 | async-start | bytes 5406720 | tf_op jit(solution)/shard_map/all_gather | solution.py:111
  93.7 563.8 %reduce-scatter.9.cloned.1.call-start = ((), (), s32[]{:S(2)}) async-start(), calls=%async_computation.19 | async-start | bytes 1638400 | tf_op jit(solution)/shard_map/reduce_scatter | solution.py:212
  94.3 12.2 %copy-start.65 = (f32[1,2,256]{2,0,1:T(1,128)}, f32[1,2,256]{2,0,1:T(1,128)S(1)}, u32[]{:S(2)}) copy-start(f32[1,2,256]{2,0,1:T(1,128)S(1)} %fusion.142) | copy-start | bytes 6148
  94.8 11.7 %copy-start.67 = (f32[1,2,256]{2,0,1:T(1,128)}, f32[1,2,256]{2,0,1:T(1,128)S(1)}, u32[]{:S(2)}) copy-start(f32[1,2,256]{2,0,1:T(1,128)S(1)} %fusion.141) | copy-start | bytes 6148
  94.8 11.7 %copy-start.51 = (f32[4,256]{1,0:T(4,128)}, f32[4,256]{1,0:T(4,128)S(1)}, u32[]{:S(2)}) copy-start(f32[4,256]{1,0:T(4,128)S(1)} %get-tuple-element.82) | copy-start | bytes 12292
  110.1 15.0 %copy-start.21 = (bf16[2,256,15,32]{1,3,2,0:T(8,128)(2,1)}, bf16[2,256,15,32]{1,3,2,0:T(8,128)(2,1)S(1)}, u32[]{:S(2)}) copy-start(bf16[2,256,15,32]{1,3,2,0:T(8,128)(2,1)S(1)} %get-tuple-element.66) | copy-start | bytes 1474564
  110.1 28.0 %copy-start.18 = (bf16[2,256,15,32]{1,3,2,0:T(8,128)(2,1)}, bf16[2,256,15,32]{1,3,2,0:T(8,128)(2,1)S(1)}, u32[]{:S(2)}) copy-start(bf16[2,256,15,32]{1,3,2,0:T(8,128)(2,1)S(1)} %get-tuple-element.48) | copy-start | bytes 1474564
  110.1 28.0 %copy-start.20 = (bf16[2,256,15,32]{1,3,2,0:T(8,128)(2,1)}, bf16[2,256,15,32]{1,3,2,0:T(8,128)(2,1)S(1)}, u32[]{:S(2)}) copy-start(bf16[2,256,15,32]{1,3,2,0:T(8,128)(2,1)S(1)} %get-tuple-element.49) | copy-start | bytes 1474564
  183.2 13.6 %copy-start.94 = (f32[2,256,960]{1,2,0:T(8,128)S(1)}, f32[2,256,960]{1,2,0:T(8,128)}, u32[]{:S(2)}) copy-start(f32[2,256,960]{1,2,0:T(8,128)} %fusion.98) | copy-start | bytes 5898244
  202.5 187.2 %copy-start.53 = (f32[2,256]{1,0:T(2,128)}, f32[2,256]{1,0:T(2,128)S(1)}, u32[]{:S(2)}) copy-start(f32[2,256]{1,0:T(2,128)S(1)} %get-tuple-element.91) | copy-start | bytes 6148
  202.5 187.2 %copy-start.55 = (f32[2,256]{1,0:T(2,128)}, f32[2,256]{1,0:T(2,128)S(1)}, u32[]{:S(2)}) copy-start(f32[2,256]{1,0:T(2,128)S(1)} %get-tuple-element.92) | copy-start | bytes 6148
  202.5 187.2 %copy-start.57 = (f32[2,256]{1,0:T(2,128)}, f32[2,256]{1,0:T(2,128)S(1)}, u32[]{:S(2)}) copy-start(f32[2,256]{1,0:T(2,128)S(1)} %get-tuple-element.89) | copy-start | bytes 6148
  202.5 187.2 %copy-start.59 = (f32[2,256]{1,0:T(2,128)}, f32[2,256]{1,0:T(2,128)S(1)}, u32[]{:S(2)}) copy-start(f32[2,256]{1,0:T(2,128)S(1)} %get-tuple-element.90) | copy-start | bytes 6148
  320.9 8.1 copy-start.77
  320.9 8.1 copy-start.82
  320.9 8.1 copy-start.83
  320.9 8.1 copy-start.87
  329.0 21.8 %slice-start = ((s8[10485760]{0:T(1024)(128)(4,1)}), s8[4194304]{0:T(1024)(128)(4,1)S(1)}, s32[]{:S(2)}) async-start(s8[10485760]{0:T(1024)(128)(4,1)} %bitcast.308), calls=%async_computation.21 | async-start | bytes 8388608
  329.0 21.8 %slice-start.1 = ((s8[10485760]{0:T(1024)(128)(4,1)}), s8[4194304]{0:T(1024)(128)(4,1)S(1)}, s32[]{:S(2)}) async-start(s8[10485760]{0:T(1024)(128)(4,1)} %bitcast.308), calls=%async_computation.22 | async-start | bytes 8388608
  339.3 11.6 %copy-start.2 = (f32[2,256,960]{1,2,0:T(8,128)}, f32[2,256,960]{1,2,0:T(8,128)S(1)}, u32[]{:S(2)}) copy-start(f32[2,256,960]{1,2,0:T(8,128)S(1)} %get-tuple-element.43) | copy-start | bytes 5898244
  339.3 11.6 %copy-start.13 = (f32[2,256,960]{1,2,0:T(8,128)}, f32[2,256,960]{1,2,0:T(8,128)S(1)}, u32[]{:S(2)}) copy-start(f32[2,256,960]{1,2,0:T(8,128)S(1)} %get-tuple-element.28) | copy-start | bytes 5898244
  339.3 11.6 %slice-start.2 = ((s8[10485760]{0:T(1024)(128)(4,1)}), s8[2097152]{0:T(1024)(128)(4,1)S(1)}, s32[]{:S(2)}) async-start(s8[10485760]{0:T(1024)(128)(4,1)} %bitcast.308), calls=%async_computation.23 | async-start | bytes 4194304
  350.8 10.2 copy-start.95
  374.7 15.0 %copy-start.3 = (f32[2,256,960]{1,2,0:T(8,128)S(1)}, f32[2,256,960]{1,2,0:T(8,128)}, u32[]{:S(2)}) copy-start(f32[2,256,960]{1,2,0:T(8,128)} %copy-done.2) | copy-start | bytes 5898244
  398.8 24.3 %copy-start.9 = (bf16[2,256,960]{1,2,0:T(8,128)(2,1)}, bf16[2,256,960]{1,2,0:T(8,128)(2,1)S(1)}, u32[]{:S(2)}) copy-start(bf16[2,256,960]{1,2,0:T(8,128)(2,1)S(1)} %convolution_convert_fusion) | copy-start | bytes 2949124
  423.1 26.8 %copy-start.22 = (bf16[2,256,15,32]{1,3,2,0:T(8,128)(2,1)S(1)}, bf16[2,256,15,32]{1,3,2,0:T(8,128)(2,1)}, u32[]{:S(2)}) copy-start(bf16[2,256,15,32]{1,3,2,0:T(8,128)(2,1)} %copy-done.21) | copy-start | bytes 1474564
  423.1 26.8 %copy-start.23 = (bf16[2,256,15,32]{1,3,2,0:T(8,128)(2,1)S(1)}, bf16[2,256,15,32]{1,3,2,0:T(8,128)(2,1)}, u32[]{:S(2)}) copy-start(bf16[2,256,15,32]{1,3,2,0:T(8,128)(2,1)} %get-tuple-element.67) | copy-start | bytes 1474564
  461.3 198.1 %reduce-scatter.5.cloned.1.call-start = ((), (), s32[]{:S(2)}) async-start(), calls=%async_computation.17 | async-start | bytes 1638400 | tf_op jit(solution)/shard_map/reduce_scatter | solution.py:212
  488.9 26.6 %copy-start.19 = (bf16[2,256,15,32]{1,3,2,0:T(8,128)(2,1)S(1)}, bf16[2,256,15,32]{1,3,2,0:T(8,128)(2,1)}, u32[]{:S(2)}) copy-start(bf16[2,256,15,32]{1,3,2,0:T(8,128)(2,1)} %copy-done.18) | copy-start | bytes 1474564
  527.0 136.3 %reduce-scatter.11.cloned.1.call-start = ((), (), s32[]{:S(2)}) async-start(), calls=%async_computation.20 | async-start | bytes 1638400 | tf_op jit(solution)/shard_map/reduce_scatter | solution.py:215
  564.7 78.5 %all-to-all-start.4 = ((bf16[960,8,4,80]{0,3,1,2:T(8,128)(2,1)}), bf16[960,8,4,80]{0,3,1,2:T(8,128)(2,1)}, u32[]{:S(2)}, u32[]{:S(2)}) async-start(bf16[960,8,4,80]{0,3,1,2:T(8,128)(2,1)} %copy.61), calls=%async_computation.8 | async-start | bytes 10485760 | tf_op jit(solution)/shard_map/all_to_all | solution.py:255
  569.8 99.7 %reduce-scatter.7.cloned.1.call-start = ((), (), s32[]{:S(2)}) async-start(), calls=%async_computation.18 | async-start | bytes 1638400 | tf_op jit(solution)/shard_map/reduce_scatter | solution.py:215
  585.2 8.3 copy-start.8
  593.5 8.8 copy-start.39
  593.6 8.8 copy-start.41
  648.4 45.9 %all-to-all-start.5 = ((bf16[960,8,80]{0,2,1:T(8,128)(2,1)}), bf16[960,8,80]{0,2,1:T(8,128)(2,1)S(1)}, u32[]{:S(2)}, u32[]{:S(2)}) async-start(bf16[960,8,80]{0,2,1:T(8,128)(2,1)} %reduce_sum.273), calls=%async_computation.9 | async-start | bytes 2621440 | tf_op jit(solution)/shard_map/all_to_all | solution.py:271
  694.4 64.9 %all-to-all-start = ((bf16[960,8,4,80]{0,3,1,2:T(8,128)(2,1)}), bf16[960,8,4,80]{0,3,1,2:T(8,128)(2,1)}, u32[]{:S(2)}, u32[]{:S(2)}) async-start(bf16[960,8,4,80]{0,3,1,2:T(8,128)(2,1)} %copy.55), calls=%async_computation.4 | async-start | bytes 10485760 | tf_op jit(solution)/shard_map/all_to_all | solution.py:241
  699.8 12.3 %copy-start.60 = (f32[2,256]{1,0:T(2,128)S(1)}, f32[2,256]{1,0:T(2,128)}, u32[]{:S(2)}) copy-start(f32[2,256]{1,0:T(2,128)} %copy-done.59) | copy-start | bytes 6148
  759.2 121.6 %all-to-all-start.2 = ((bf16[960,8,4,160]{0,3,1,2:T(8,128)(2,1)}), bf16[960,8,4,160]{0,3,1,2:T(8,128)(2,1)}, u32[]{:S(2)}, u32[]{:S(2)}) async-start(bf16[960,8,4,160]{0,3,1,2:T(8,128)(2,1)} %copy.58), calls=%async_computation.6 | async-start | bytes 20971520 | tf_op jit(solution)/shard_map/all_to_all | solution.py:248
  770.4 116.6 %copy-start.70 = (s32[4,256]{1,0:T(4,128)S(1)}, s32[4,256]{1,0:T(4,128)}, u32[]{:S(2)}) copy-start(s32[4,256]{1,0:T(4,128)} %param.11) | copy-start | bytes 12292
  880.8 37.3 %all-to-all-start.1 = ((bf16[960,8,80]{0,2,1:T(8,128)(2,1)}), bf16[960,8,80]{0,2,1:T(8,128)(2,1)}, u32[]{:S(2)}, u32[]{:S(2)}) async-start(bf16[960,8,80]{0,2,1:T(8,128)(2,1)} %reduce_sum.269), calls=%async_computation.5 | async-start | bytes 2621440 | tf_op jit(solution)/shard_map/all_to_all | solution.py:265
  896.9 25.7 %copy-start.52 = (f32[4,256]{1,0:T(4,128)S(1)}, f32[4,256]{1,0:T(4,128)}, u32[]{:S(2)}) copy-start(f32[4,256]{1,0:T(4,128)} %copy-done.51) | copy-start | bytes 12292
  896.9 25.7 %copy-start.66 = (f32[1,2,256]{2,0,1:T(1,128)S(1)}, f32[1,2,256]{2,0,1:T(1,128)}, u32[]{:S(2)}) copy-start(f32[1,2,256]{2,0,1:T(1,128)} %copy-done.65) | copy-start | bytes 6148
  896.9 25.7 %copy-start.68 = (f32[1,2,256]{2,0,1:T(1,128)S(1)}, f32[1,2,256]{2,0,1:T(1,128)}, u32[]{:S(2)}) copy-start(f32[1,2,256]{2,0,1:T(1,128)} %copy-done.67) | copy-start | bytes 6148
  896.9 25.8 %copy-start.84 = (f32[2,256]{1,0:T(2,128)S(1)}, f32[2,256]{1,0:T(2,128)}, u32[]{:S(2)}) copy-start(f32[2,256]{1,0:T(2,128)} %get-tuple-element.20) | copy-start | bytes 6148
  896.9 25.8 %copy-start.85 = (f32[2,256]{1,0:T(2,128)S(1)}, f32[2,256]{1,0:T(2,128)}, u32[]{:S(2)}) copy-start(f32[2,256]{1,0:T(2,128)} %get-tuple-element.42) | copy-start | bytes 6148
  918.2 97.5 %all-to-all-start.3 = ((bf16[960,8,160]{0,2,1:T(8,128)(2,1)}), bf16[960,8,160]{0,2,1:T(8,128)(2,1)}, u32[]{:S(2)}, u32[]{:S(2)}) async-start(bf16[960,8,160]{0,2,1:T(8,128)(2,1)} %reduce_sum.271), calls=%async_computation.7 | async-start | bytes 5242880 | tf_op jit(solution)/shard_map/all_to_all | solution.py:268
  936.3 66.7 %copy-start.47 = (f32[960]{0:T(1024)S(1)}, f32[960]{0:T(1024)}, u32[]{:S(2)}) copy-start(f32[960]{0:T(1024)} %param.17) | copy-start | bytes 11524
  936.3 66.7 %copy-start.58 = (f32[2,256]{1,0:T(2,128)S(1)}, f32[2,256]{1,0:T(2,128)}, u32[]{:S(2)}) copy-start(f32[2,256]{1,0:T(2,128)} %copy-done.57) | copy-start | bytes 6148
  936.3 66.7 %copy-start.64 = (f32[2,256]{1,0:T(2,128)S(1)}, f32[2,256]{1,0:T(2,128)}, u32[]{:S(2)}) copy-start(f32[2,256]{1,0:T(2,128)} %copy-done.63) | copy-start | bytes 6148
  936.4 66.7 %copy-start.74 = (f32[2,256]{1,0:T(2,128)S(1)}, f32[2,256]{1,0:T(2,128)}, u32[]{:S(2)}) copy-start(f32[2,256]{1,0:T(2,128)} %get-tuple-element.87) | copy-start | bytes 6148
  (54 other events, 219.6 us)
Sparse Core Ops, SparseCore 0:
  10.8 68.0 all-gather.7
  87.8 16.8 all-gather.19
  106.9 18.3 all-gather.11
  127.2 18.3 all-gather.17
  146.9 18.3 all-gather.9
  168.0 86.1 all-gather.13
  257.0 63.8 all-gather.15
  461.4 24.9 reduce-scatter.8
  527.2 24.8 reduce-scatter.4
  555.0 33.5 reduce-scatter.10
  591.2 33.5 reduce-scatter.6
where the time goes:
time: 1030 us
  matrix products  347 us (34%)
  waiting for transfers between devices  334 us (32%)
  other arithmetic  150 us (15%)
  blocking collectives  74.3 us (7%)
  local copies, waits for them, and re-layouts  71.1 us (7%)
  starting transfers between devices  31.9 us (3%)
  between operations  19.2 us (2%)
    all_to_all x1, waiting for transfers between devices, on_device(): lax.all_to_all(owner_layout(grad_gu).astype(jnp.bfloat16), 'ctx', split_a...  110 us
    all_gather x1, waiting for transfers between devices, on_device(): lax.all_gather(packs[0], ('dp', 'ctx'), axis=1, tiled=True)  68.1 us
    dot_general x8, matrix products, by_columns(): lax.dot_general(left, right, (((2,), (1,)), ((), ())), preferred_element_...  67.4 us
    psum x1, blocking collectives, on_device(): lax.psum((energy, grad_gains, grad_router), ('dp', 'ctx'))  63.9 us
    convert_element_type x2, other arithmetic, on_device(): (probs * (d_probs - jnp.sum(probs * d_probs, axis=-1, keepdims=True))).as...  53.3 us
    dot_general x8, matrix products, over_rows(): lax.dot_general(left, right, (((0, 1), (0, 1)), ((), ())), preferred_elem...  51.1 us
    all_gather x1, waiting for transfers between devices, on_device(): lax.all_gather(packs[1], ('dp', 'ctx'), axis=1, tiled=True)  51 us
    dot_general x2, matrix products, on_device(): jnp.einsum('bqgrh,bkgh->bgrqk', d_heads_low, values_all, preferred_elemen...  48.7 us
  transfers between devices with their start and end apart: 17, of which 7 were waited for; matrix products, arithmetic and copies ran while one was open for 39% of the time, Pallas kernels for 0%

commit v1 on v0

v1 whole, which is shorter than its diff:
```python
import functools

import jax
import jax.numpy as jnp
from jax import lax
from jax.experimental import pallas as pl
from jax.experimental.pallas import tpu as pltpu
from jax.sharding import PartitionSpec as P

D = 960
HEADS = 15
KV_HEADS = 5
HEAD = 64
FF = 2560
CHOSEN = 640
PER_KV = HEADS // KV_HEADS
KV_WIDTH = KV_HEADS * HEAD
QKV_COLS = D + 2 * KV_WIDTH
ROWS = 656
TILE = 256
WIDE = 768
SLAB = 1280
CHUNK = 640
TILES = ((0, 256, 512), (256, 512, 768), (512, ROWS, 768))
NEG = -1e30
VMEM_LIMIT = 62 * 1024 * 1024

EPS = 1e-05
THETA = 10000.0
F32 = jnp.float32
BF16 = jnp.bfloat16


def device_bits():
    found = []
    for name in ("dp", "ctx"):
        count = lax.axis_size(name)
        found += [(name, bit) for bit in reversed(range(count.bit_length() - 1))]
    return found


def swap(value, place):
    name, bit = place
    pairs = [(i, i ^ (1 << bit)) for i in range(lax.axis_size(name))]
    return lax.ppermute(value, name, pairs)


def own_bit(place):
    name, bit = place
    return (lax.axis_index(name) >> bit) & 1


def merge(whole, other, place, ahead):
    low_side = own_bit(place) == 0
    size = whole.shape[0]
    whole, other = [v.reshape(ahead, size // ahead, D) for v in (whole, other)]
    both = [jnp.where(low_side, whole, other), jnp.where(low_side, other, whole)]
    return jnp.stack(both, axis=1).reshape(2 * size, D)


def gather_halves(shard, bits):
    other = swap(shard, bits[0])
    low_side = own_bit(bits[0]) == 0
    halves = [jnp.where(low_side, shard, other), jnp.where(low_side, other, shard)]
    last = len(bits) - 1
    for step in range(1, last + 1):
        moved = []
        for half, spots in zip(halves, routes(bits)):
            spot = spots[step - 1]
            ahead = 1 << sum(1 for s in spots[: step - 1] if s < spot)
            moved.append((half, swap(half, bits[spot]), bits[spot], ahead))
        halves = [merge(*m) for m in moved]
    return halves


def routes(bits):
    count = len(bits)
    far = list(range(1, count - 3))
    return [far + [count - 3, count - 2, count - 1], far + [count - 2, count - 3, count - 1]]


class Scatter:
    def __init__(self, grads, bits):
        self.bits = bits
        self.rows = [g.shape[0] >> (len(bits) - 1) for g in grads]
        self.routes = [r[::-1] for r in routes(bits)]
        self.parts = [[g] for g in grads]
        self.held = [sorted(r) for r in self.routes]
        self.step = 0
        self.part = None
        self.got = []

    def cut(self, parts, held, spot, side, rows):
        ahead = 1 << held.index(spot)
        behind = (1 << (len(held) - held.index(spot) - 1)) * rows
        total = 0.0
        for part in parts:
            cube = part.reshape(ahead, 2, behind, D)
            total = total + lax.dynamic_index_in_dim(cube, side, 1, keepdims=False).astype(F32)
        return total.astype(BF16).reshape(ahead * behind, D)

    def send(self):
        arrive = []
        if self.step < len(self.bits) - 1:
            for i in range(2):
                spot = self.routes[i][self.step]
                mine = own_bit(self.bits[spot])
                parts, held, rows = self.parts[i], self.held[i], self.rows[i]
                out = self.cut(parts, held, spot, 1 - mine, rows)
                self.parts[i] = [self.cut(parts, held, spot, mine, rows)]
                self.held[i] = [h for h in held if h != spot]
                arrive.append(swap(out, self.bits[spot]))
        else:
            low_side = own_bit(self.bits[0]) == 0
            sums = []
            for parts in self.parts:
                sums.append(sum(p.astype(F32) for p in parts))
            out = jnp.where(low_side, sums[1], sums[0]).astype(BF16)
            self.keep = jnp.where(low_side, sums[0], sums[1])
            arrive.append(swap(out, self.bits[0]))
        self.step += 1
        return arrive

    def take(self, arrive):
        if self.step == len(self.bits):
            return self.keep + arrive[0].astype(F32)
        for parts, got in zip(self.parts, arrive):
            parts.append(got)


def advance(scatters, value):
    active = [s for s in scatters if s.part is None]
    if value is not None:
        flat = join(value, *[g for s in active for g in s.got])
        value, flat = flat[0], list(flat[1:])
        for s in active:
            s.got, flat = flat[: len(s.got)], flat[len(s.got) :]
    for s in active:
        s.part = s.take(s.got)
        if s.part is None:
            s.got = s.send()
    return value


def join(*values):
    return lax.optimization_barrier(values)


def all_sum(value, bits):
    for place in bits:
        value = value + swap(value, place)
    return value


def dot(left, right, contract):
    return lax.dot_general(left, right, (contract, ((), ())), preferred_element_type=F32)


def to_sequence(blocks):
    return lax.all_to_all(blocks, "ctx", split_axis=0, concat_axis=0, tiled=True)


def nt(left, right):
    return lax.dot_general(left, right, (((1,), (1,)), ((), ())), preferred_element_type=F32)


def nn(left, right):
    return lax.dot_general(left, right, (((1,), (0,)), ((), ())), preferred_element_type=F32)


def tn(left, right):
    return lax.dot_general(left, right, (((0,), (0,)), ((), ())), preferred_element_type=F32)


def turned(values, cosine, sine):
    half = HEAD // 2
    pieces = []
    for start in range(0, values.shape[1], HEAD):
        head = values[:, start : start + HEAD]
        swapped = jnp.concatenate([head[:, half:], head[:, :half]], axis=1)
        pieces.append(head * cosine + swapped * sine)
    return pieces


def weight_specs(first):
    return [
        pl.BlockSpec((D // KV_HEADS, D), lambda g: (first + g, 0)),
        pl.BlockSpec((HEAD, D), lambda g: (HEADS + first + g, 0)),
        pl.BlockSpec((HEAD, D), lambda g: (first + g, 0)),
    ] + [
        pl.BlockSpec((HEAD, D), lambda g, r=r: (KV_HEADS + PER_KV * (first + g) + r, 0))
        for r in range(PER_KV)
    ]


def attend_kernel(
    x_ref, gain_ref, cos_ref, sin_ref, aux_ref, row_ref, wq_ref, wk_ref, wv_ref, wo0_ref, wo1_ref, wo2_ref,
    n1_ref, q_ref, k_ref, v_ref, o_ref, l_ref, h1_ref,
    bias, keys, vals, lse,
):
    group = pl.program_id(0)

    @pl.when(group == 0)
    def _():
        x = x_ref[...].astype(F32)
        inv = lax.rsqrt(jnp.mean(x * x, axis=-1, keepdims=True) + EPS)
        n1_ref[...] = (x * inv * gain_ref[...]).astype(BF16)
        h1_ref[...] = x
        bias[...] = jnp.where(row_ref[1:2, :] <= aux_ref[:, 2:3], 0.0, NEG)
        keys[...] = jnp.zeros_like(keys)
        vals[...] = jnp.zeros_like(vals)
        lse[...] = jnp.zeros_like(lse)

    packed = jnp.concatenate([wq_ref[...], wk_ref[...], wv_ref[...]], axis=0)
    mixed = nt(n1_ref[...], packed)
    rotated = turned(mixed[:, : D // KV_HEADS + HEAD], cos_ref[...], sin_ref[...])
    key = rotated[PER_KV].astype(BF16)
    value = mixed[:, D // KV_HEADS + HEAD :].astype(BF16)
    k_ref[0] = key
    v_ref[0] = value
    keys[:ROWS] = key
    vals[:ROWS] = value
    for head in range(PER_KV):
        q_ref[head] = rotated[head].astype(BF16)
    lanes = lax.broadcasted_iota(jnp.int32, (1, 128), 1)
    for start, stop, reach in TILES:
        outs = []
        logs = jnp.zeros((stop - start, 128), F32)
        for head in range(PER_KV):
            scores = nt(q_ref[head, start:stop], keys[:reach]) * 0.125 + bias[start:stop, :reach]
            top = jnp.max(scores, axis=-1, keepdims=True)
            expd = jnp.exp(scores - top)
            total = jnp.sum(expd, axis=-1, keepdims=True)
            outs.append(nn(expd.astype(BF16), vals[:reach]) / total)
            logs = jnp.where(lanes == head, top + jnp.log(total), logs)
        o_ref[0, start:stop] = jnp.concatenate(outs, axis=1).astype(BF16)
        lse[start:stop] = logs
    l_ref[0] = lse[...].T[:8]
    h1_ref[...] += nn(o_ref[0], jnp.concatenate([wo0_ref[...], wo1_ref[...], wo2_ref[...]], axis=0))


def attend(x, gain, cosine, sine, aux, row, w_low, w_high):
    whole = lambda *shape: pl.BlockSpec(shape, lambda g: (0,) * len(shape))
    fixed = lambda *shape: pl.BlockSpec(
        shape, lambda g: (0,) * len(shape), pipeline_mode=pl.Buffered(1)
    )
    per = D // KV_HEADS
    return pl.pallas_call(
        attend_kernel,
        grid=(KV_HEADS,),
        in_specs=[
            fixed(ROWS, D),
            fixed(1, D),
            fixed(ROWS, HEAD),
            fixed(ROWS, HEAD),
            fixed(ROWS, 8),
            fixed(8, WIDE),
            *weight_specs(0),
        ],
        out_specs=[
            whole(ROWS, D),
            pl.BlockSpec((PER_KV, ROWS, HEAD), lambda g: (g, 0, 0)),
            pl.BlockSpec((1, ROWS, HEAD), lambda g: (g, 0, 0)),
            pl.BlockSpec((1, ROWS, HEAD), lambda g: (g, 0, 0)),
            pl.BlockSpec((1, ROWS, per), lambda g: (g, 0, 0)),
            pl.BlockSpec((1, 8, WIDE), lambda g: (g, 0, 0)),
            whole(ROWS, D),
        ],
        out_shape=[
            jax.ShapeDtypeStruct((ROWS, D), BF16),
            jax.ShapeDtypeStruct((HEADS, ROWS, HEAD), BF16),
            jax.ShapeDtypeStruct((KV_HEADS, ROWS, HEAD), BF16),
            jax.ShapeDtypeStruct((KV_HEADS, ROWS, HEAD), BF16),
            jax.ShapeDtypeStruct((KV_HEADS, ROWS, per), BF16),
            jax.ShapeDtypeStruct((KV_HEADS, 8, WIDE), F32),
            jax.ShapeDtypeStruct((ROWS, D), F32),
        ],
        scratch_shapes=[
            pltpu.VMEM((ROWS, WIDE), F32),
            pltpu.VMEM((WIDE, HEAD), BF16),
            pltpu.VMEM((WIDE, HEAD), BF16),
            pltpu.VMEM((WIDE, 128), F32),
        ],
        compiler_params=pltpu.CompilerParams(vmem_limit_bytes=VMEM_LIMIT),
        name="attend",
    )(x, gain, cosine, sine, aux, row, w_low, w_low, w_high, w_high, w_high, w_high)


def feed_specs(packs):
    if packs[0].ndim == 2:
        return [
            pl.BlockSpec((SLAB, D), lambda j: (j, 0)),
            pl.BlockSpec((SLAB, D), lambda j: (FF // SLAB + j, 0)),
            pl.BlockSpec((SLAB, D), lambda j: (j, 0)),
        ]
    count, rows, _ = packs[0].shape
    thin = rows // 3
    return [
        pl.BlockSpec((SLAB // (2 * thin), 2 * thin, D), lambda j: (j, 0, 0)),
        pl.BlockSpec((SLAB // (2 * thin), 2 * thin, D), lambda j: (FF // SLAB + j, 0, 0)),
        pl.BlockSpec((SLAB // thin, thin, D), lambda j: (j, 2, 0)),
    ]


def rows_of(ref, start=0, size=SLAB):
    if len(ref.shape) == 2:
        return ref[start : start + size]
    each = ref.shape[1]
    return ref[start // each : (start + size) // each].reshape(size, D)


def feed_kernel(
    h1_ref, x_ref, t_ref, aux_ref, gain_ref, router_ref, wg_ref, wu_ref, wd_ref,
    n2_ref, g_ref, u_ref, hid_ref, y_ref, diff_ref, cols_ref, sums_ref, d_ffn_ref,
):
    step = pl.program_id(0)

    @pl.when(step == 0)
    def _():
        h1 = h1_ref[...]
        inv = lax.rsqrt(jnp.mean(h1 * h1, axis=-1, keepdims=True) + EPS)
        n2_ref[...] = (h1 * inv * gain_ref[...]).astype(BF16)
        diff_ref[...] = h1 - x_ref[...].astype(F32)

    for start in range(0, SLAB, CHUNK):
        span = slice(start, start + CHUNK)
        gate = nt(n2_ref[...], rows_of(wg_ref, start, CHUNK))
        up = nt(n2_ref[...], rows_of(wu_ref, start, CHUNK))
        g_ref[:, span] = gate.astype(BF16)
        u_ref[:, span] = up.astype(BF16)
        hid_ref[:, span] = (gate * jax.nn.sigmoid(gate) * up).astype(BF16)
    diff_ref[...] += nn(hid_ref[...], rows_of(wd_ref))

    @pl.when(step == pl.num_programs(0) - 1)
    def _():
        x = x_ref[...].astype(F32)
        branch = diff_ref[...]
        valid, live = aux_ref[:, 0:1], aux_ref[:, 1:2]
        prob = jax.nn.sigmoid(jnp.sum(x * router_ref[...], axis=-1, keepdims=True))
        mix = live * prob
        result = x + mix * branch
        y_ref[...] = result.astype(BF16)
        diff = valid * (result - t_ref[...].astype(F32))
        d_logit = live * jnp.sum(diff * branch, axis=-1, keepdims=True) * prob * (1.0 - prob)
        diff_ref[...] = diff
        d_ffn_ref[...] = (mix * diff).astype(BF16)
        lanes = lax.broadcasted_iota(jnp.int32, (1, 128), 1)
        cols_ref[...] = jnp.where(lanes == 0, mix, jnp.where(lanes == 1, d_logit, 0.0))
        sums_ref[...] = jnp.concatenate(
            [
                jnp.sum(d_logit * x, axis=0, keepdims=True),
                0.5 * jnp.sum(diff * diff, axis=0, keepdims=True),
                jnp.zeros((6, D), F32),
            ],
            axis=0,
        )


def feed(h1, x, t, aux, gain, router, packs):
    whole = lambda *shape: pl.BlockSpec(shape, lambda j: (0,) * len(shape))
    fixed = lambda *shape: pl.BlockSpec(
        shape, lambda j: (0,) * len(shape), pipeline_mode=pl.Buffered(1)
    )
    return pl.pallas_call(
        feed_kernel,
        grid=(FF // SLAB,),
        in_specs=[
            fixed(ROWS, D),
            fixed(ROWS, D),
            fixed(ROWS, D),
            fixed(ROWS, 8),
            fixed(1, D),
            fixed(1, D),
            *feed_specs(packs),
        ],
        out_specs=[
            whole(ROWS, D),
            pl.BlockSpec((ROWS, SLAB), lambda j: (0, j)),
            pl.BlockSpec((ROWS, SLAB), lambda j: (0, j)),
            pl.BlockSpec((ROWS, SLAB), lambda j: (0, j)),
            whole(ROWS, D),
            whole(ROWS, D),
            whole(ROWS, 128),
            whole(8, D),
            whole(ROWS, D),
        ],
        out_shape=[
            jax.ShapeDtypeStruct((ROWS, D), BF16),
            jax.ShapeDtypeStruct((ROWS, FF), BF16),
            jax.ShapeDtypeStruct((ROWS, FF), BF16),
            jax.ShapeDtypeStruct((ROWS, FF), BF16),
            jax.ShapeDtypeStruct((ROWS, D), BF16),
            jax.ShapeDtypeStruct((ROWS, D), F32),
            jax.ShapeDtypeStruct((ROWS, 128), F32),
            jax.ShapeDtypeStruct((8, D), F32),
            jax.ShapeDtypeStruct((ROWS, D), BF16),
        ],
        compiler_params=pltpu.CompilerParams(vmem_limit_bytes=VMEM_LIMIT),
        name="feed",
    )(h1, x, t, aux, gain, router, *packs)


def down_grad_kernel(hid_ref, d_ffn_ref, out_ref):
    out_ref[...] = tn(hid_ref[...], d_ffn_ref[...]).astype(BF16)


def down_grad(hid, d_ffn):
    return pl.pallas_call(
        down_grad_kernel,
        grid=(FF // CHUNK,),
        in_specs=[
            pl.BlockSpec((ROWS, CHUNK), lambda j: (0, j)),
            pl.BlockSpec((ROWS, D), lambda j: (0, 0)),
        ],
        out_specs=pl.BlockSpec((CHUNK, D), lambda j: (j, 0)),
        out_shape=jax.ShapeDtypeStruct((FF, D), BF16),
        compiler_params=pltpu.CompilerParams(vmem_limit_bytes=VMEM_LIMIT),
        name="down_grad",
    )(hid, d_ffn)


def feed_back_kernel(
    h1_ref, n2_ref, diff_ref, cols_ref, gain_ref, router_ref, g_ref, u_ref, d_ffn_ref,
    wg_ref, wu_ref, wd_ref,
    ggu_ref, da_ref, part_ref, sums_ref,
    d_gate, d_up,
):
    step = pl.program_id(0)

    @pl.when(step == 0)
    def _():
        part_ref[...] = jnp.zeros_like(part_ref)

    for start in range(0, SLAB, CHUNK):
        span = slice(start, start + CHUNK)
        d_hidden = nt(d_ffn_ref[...], rows_of(wd_ref, start, CHUNK))
        gate = g_ref[:, span].astype(F32)
        up = u_ref[:, span].astype(F32)
        sig = jax.nn.sigmoid(gate)
        d_gate[:, span] = (d_hidden * up * sig * (1.0 + gate * (1.0 - sig))).astype(BF16)
        d_up[:, span] = (d_hidden * gate * sig).astype(BF16)
        ggu_ref[0, span] = tn(d_gate[:, span], n2_ref[...]).astype(BF16)
        ggu_ref[1, span] = tn(d_up[:, span], n2_ref[...]).astype(BF16)
    part_ref[...] += nn(d_gate[...], rows_of(wg_ref)) + nn(d_up[...], rows_of(wu_ref))

    @pl.when(step == pl.num_programs(0) - 1)
    def _():
        h1 = h1_ref[...]
        inv = lax.rsqrt(jnp.mean(h1 * h1, axis=-1, keepdims=True) + EPS)
        d_norm = part_ref[...]
        sums_ref[...] = jnp.broadcast_to(
            jnp.sum(d_norm * h1 * inv, axis=0, keepdims=True), sums_ref.shape
        )
        scaled = d_norm * gain_ref[...]
        d_inner = inv * scaled - h1 * inv**3 * jnp.mean(scaled * h1, axis=-1, keepdims=True)
        diff = diff_ref[...]
        da_ref[...] = (cols_ref[:, 0:1] * diff + d_inner).astype(BF16)
        part_ref[...] = diff + cols_ref[:, 1:2] * router_ref[...] + d_inner


def feed_back(h1, n2, diff, cols, gain, router, g, u, d_ffn, packs):
    whole = lambda *shape: pl.BlockSpec(shape, lambda j: (0,) * len(shape))
    fixed = lambda *shape: pl.BlockSpec(
        shape, lambda j: (0,) * len(shape), pipeline_mode=pl.Buffered(1)
    )
    return pl.pallas_call(
        feed_back_kernel,
        grid=(FF // SLAB,),
        in_specs=[
            fixed(ROWS, D),
            fixed(ROWS, D),
            fixed(ROWS, D),
            fixed(ROWS, 128),
            fixed(1, D),
            fixed(1, D),
            pl.BlockSpec((ROWS, SLAB), lambda j: (0, j)),
            pl.BlockSpec((ROWS, SLAB), lambda j: (0, j)),
            fixed(ROWS, D),
            *feed_specs(packs),
        ],
        out_specs=[
            pl.BlockSpec((2, SLAB, D), lambda j: (0, j, 0)),
            whole(ROWS, D),
            whole(ROWS, D),
            whole(8, D),
        ],
        out_shape=[
            jax.ShapeDtypeStruct((2, FF, D), BF16),
            jax.ShapeDtypeStruct((ROWS, D), BF16),
            jax.ShapeDtypeStruct((ROWS, D), F32),
            jax.ShapeDtypeStruct((8, D), F32),
        ],
        scratch_shapes=[
            pltpu.VMEM((ROWS, SLAB), BF16),
            pltpu.VMEM((ROWS, SLAB), BF16),
        ],
        compiler_params=pltpu.CompilerParams(vmem_limit_bytes=VMEM_LIMIT),
        name="feed_back",
    )(h1, n2, diff, cols, gain, router, g, u, d_ffn, *packs)


def attend_back_kernel(
    final, da_ref, part_ref, x_ref, n1_ref, gain_ref, cos_ref, sin_ref, aux_ref, row_ref,
    q_ref, k_ref, v_ref, o_ref, l_ref, wq_ref, wk_ref, wv_ref, wo0_ref, wo1_ref, wo2_ref,
    sofar_ref, _gq, _gk, _gv, _go,
    gq_ref, gk_ref, gv_ref, go_ref, dn1, grad_ref, sums_ref,
    bias, wide_q, wide_do, dq,
):
    group = pl.program_id(0)
    per = D // KV_HEADS

    @pl.when(group == 0)
    def _():
        bias[...] = jnp.where(aux_ref[:, 3:4] <= row_ref[0:1, :], 0.0, NEG)
        wide_q[...] = jnp.zeros_like(wide_q)
        wide_do[...] = jnp.zeros_like(wide_do)
        dn1[...] = sofar_ref[...]

    w_out = jnp.concatenate([wo0_ref[...], wo1_ref[...], wo2_ref[...]], axis=0)
    d_heads = nt(da_ref[...], w_out)
    d_low = d_heads.astype(BF16)
    go_ref[...] = tn(o_ref[0], da_ref[...]).astype(BF16)
    both = d_low.astype(F32) * o_ref[0].astype(F32)
    key, value = k_ref[0], v_ref[0]
    d_key = jnp.zeros((ROWS, HEAD), F32)
    d_value = jnp.zeros((ROWS, HEAD), F32)
    d_queries = []
    ones = jnp.ones((8, HEAD), F32)
    for head in range(PER_KV):
        span = slice(head * HEAD, (head + 1) * HEAD)
        wide_q[:ROWS] = q_ref[head]
        wide_do[:ROWS] = d_low[:, span]
        inside = lax.dot_general(
            ones, both[:, span], (((1,), (1,)), ((), ())),
            preferred_element_type=F32, precision=lax.Precision.HIGHEST,
        )
        inside = jnp.concatenate([inside, jnp.zeros((8, WIDE - ROWS), F32)], axis=1)
        for start, stop, reach in TILES:
            end = start + TILE
            reach = min(reach, ROWS)
            scores = nt(key[:reach], wide_q[start:end]) * 0.125 + bias[:reach, start:end]
            probs = jnp.exp(scores - l_ref[0, head : head + 1, start:end])
            d_probs = nt(value[:reach], wide_do[start:end])
            d_scores = (probs * (d_probs - inside[0:1, start:end])).astype(BF16)
            add_k = nn(d_scores, wide_q[start:end])
            add_v = nn(probs.astype(BF16), wide_do[start:end])
            if reach < ROWS:
                rest = jnp.zeros((ROWS - reach, HEAD), F32)
                add_k = jnp.concatenate([add_k, rest], axis=0)
                add_v = jnp.concatenate([add_v, rest], axis=0)
            d_key += add_k
            d_value += add_v
            dq[start:end] = tn(d_scores, key[:reach]) * 0.125
        d_queries.append(dq[:ROWS])
    turned_back = turned(
        jnp.concatenate(d_queries + [d_key * 0.125], axis=1), cos_ref[...], -sin_ref[...]
    )
    d_mixed = jnp.concatenate(turned_back + [d_value], axis=1).astype(BF16)
    grads = tn(d_mixed, n1_ref[...]).astype(BF16)
    gq_ref[...] = grads[:per]
    gk_ref[...] = grads[per : per + HEAD]
    gv_ref[...] = grads[per + HEAD :]
    packed = jnp.concatenate([wq_ref[...], wk_ref[...], wv_ref[...]], axis=0)
    dn1[...] += nn(d_mixed, packed)

    if not final:
        return

    @pl.when(group == pl.num_programs(0) - 1)
    def _():
        x = x_ref[...].astype(F32)
        inv = lax.rsqrt(jnp.mean(x * x, axis=-1, keepdims=True) + EPS)
        d_norm = dn1[...]
        sums_ref[...] = jnp.broadcast_to(
            jnp.sum(d_norm * x * inv, axis=0, keepdims=True), sums_ref.shape
        )
        scaled = d_norm * gain_ref[...]
        d_x = inv * scaled - x * inv**3 * jnp.mean(scaled * x, axis=-1, keepdims=True)
        grad_ref[...] = (part_ref[...] + d_x).astype(BF16)


def attend_back(first, count, given, so_far):
    whole = lambda *shape: pl.BlockSpec(shape, lambda g: (0,) * len(shape))
    fixed = lambda *shape: pl.BlockSpec(
        shape, lambda g: (0,) * len(shape), pipeline_mode=pl.Buffered(1)
    )
    per = D // KV_HEADS
    final = first + count == KV_HEADS
    kept = pl.BlockSpec(memory_space=pl.ANY)
    return pl.pallas_call(
        functools.partial(attend_back_kernel, final),
        grid=(count,),
        in_specs=[
            fixed(ROWS, D),
            fixed(ROWS, D),
            fixed(ROWS, D),
            fixed(ROWS, D),
            fixed(1, D),
            fixed(ROWS, HEAD),
            fixed(ROWS, HEAD),
            fixed(ROWS, 8),
            fixed(8, WIDE),
            pl.BlockSpec((PER_KV, ROWS, HEAD), lambda g: (first + g, 0, 0)),
            pl.BlockSpec((1, ROWS, HEAD), lambda g: (first + g, 0, 0)),
            pl.BlockSpec((1, ROWS, HEAD), lambda g: (first + g, 0, 0)),
            pl.BlockSpec((1, ROWS, per), lambda g: (first + g, 0, 0)),
            pl.BlockSpec((1, 8, WIDE), lambda g: (first + g, 0, 0)),
            *weight_specs(first),
            fixed(ROWS, D),
            kept,
            kept,
            kept,
            kept,
        ],
        out_specs=[
            pl.BlockSpec((per, D), lambda g: (first + g, 0)),
            pl.BlockSpec((HEAD, D), lambda g: (first + g, 0)),
            pl.BlockSpec((HEAD, D), lambda g: (first + g, 0)),
            pl.BlockSpec((per, D), lambda g: (first + g, 0)),
            whole(ROWS, D),
            whole(ROWS, D),
            whole(8, D),
        ],
        out_shape=[
            jax.ShapeDtypeStruct((D, D), BF16),
            jax.ShapeDtypeStruct((KV_WIDTH, D), BF16),
            jax.ShapeDtypeStruct((KV_WIDTH, D), BF16),
            jax.ShapeDtypeStruct((D, D), BF16),
            jax.ShapeDtypeStruct((ROWS, D), F32),
            jax.ShapeDtypeStruct((ROWS, D), BF16),
            jax.ShapeDtypeStruct((8, D), F32),
        ],
        scratch_shapes=[
            pltpu.VMEM((ROWS, WIDE), F32),
            pltpu.VMEM((WIDE, HEAD), BF16),
            pltpu.VMEM((WIDE, HEAD), BF16),
            pltpu.VMEM((WIDE, HEAD), F32),
        ],
        input_output_aliases={21: 0, 22: 1, 23: 2, 24: 3},
        compiler_params=pltpu.CompilerParams(vmem_limit_bytes=VMEM_LIMIT),
        name="attend_back",
    )(*given, *so_far)


def on_device(states, teacher, validity, chosen, attn_pack, gate_up, down_proj, norm_gains, router):
    seq_count, block_rows, width = states.shape
    ctx_count = lax.axis_size("ctx")
    if seq_count != ctx_count:
        raise ValueError("seq_count")
    seq_length = block_rows * ctx_count
    bits = device_bits()
    gain_one, gain_two = norm_gains[0:1], norm_gains[1:2]

    flags = to_sequence((validity + 2 * chosen).reshape(seq_count, 1, block_rows))
    x_seq = to_sequence(states).reshape(seq_length, width)
    feed_rows = jnp.concatenate([gate_up.T, down_proj.T], axis=0)
    packs = lax.all_gather(feed_rows, ("dp", "ctx"), axis=0)
    w_low, w_high = gather_halves(attn_pack.T, bits)
    teacher_late, w_low, w_high = join(teacher, w_low, w_high)
    t_seq = to_sequence(teacher_late).reshape(seq_length, width)
    thin = down_proj.shape[1]
    if thin % 16:
        wide = packs[:, : 2 * thin].reshape(2 * FF, width)
        packs = (wide, wide, packs[:, 2 * thin :].reshape(FF, width))
    else:
        packs = (packs, packs, packs)

    flags = flags.reshape(seq_length)
    chosen_seq, valid_seq = flags >> 1, flags & 1
    place = jnp.arange(seq_length)
    rank = jnp.sum(jnp.where(place[:, None] < place[None, :], chosen_seq[:, None], 0), axis=0)
    slot = jnp.where(chosen_seq > 0, rank, -1)
    pick = (jnp.arange(ROWS)[:, None] == slot[None, :]).astype(BF16)
    picked = pick.astype(F32)
    pos = jnp.sum(picked * place.astype(F32)[None, :], axis=1)
    valid = jnp.sum(picked * valid_seq.astype(F32)[None, :], axis=1)
    live = (jnp.arange(ROWS) < jnp.sum(chosen_seq)).astype(F32)

    x_low = dot(pick, x_seq, ((1,), (0,))).astype(BF16)
    t_low = dot(pick, t_seq, ((1,), (0,))).astype(BF16)

    half = HEAD // 2
    freqs = THETA ** (-(jnp.arange(half).astype(F32) * 2.0 / HEAD))
    angles = pos[:, None] * freqs[None, :]
    cosine, sine = jnp.cos(angles), jnp.sin(angles)
    cosine = jnp.concatenate([cosine, cosine], axis=1)
    sine = jnp.concatenate([-sine, sine], axis=1)
    block = jnp.floor(pos / block_rows)
    key_block = jnp.where(valid * live > 0.5, block, 1e6)
    aux = jnp.stack([valid, live, block, key_block] + [jnp.zeros_like(pos)] * 4, axis=1)
    row = jnp.stack([block, key_block] + [jnp.zeros_like(pos)] * 6, axis=0)
    row = jnp.pad(row, ((0, 0), (0, WIDE - ROWS)), constant_values=1e6)
    router_row = router[None, :]

    n1, q, k, v, o, lse, h1 = attend(x_low, gain_one, cosine, sine, aux, row, w_low, w_high)
    n2, g, u, hid, y, diff, cols, sums, d_ffn = feed(
        h1, x_low, t_low, aux, gain_two, router_row, packs
    )
    energy = jnp.sum(sums[1])

    def to_home(compact):
        whole = dot(pick, compact, ((0,), (0,))).astype(BF16)
        return to_sequence(whole.reshape(ctx_count, block_rows, width))

    out_home = to_home(y)
    down_half = down_grad(hid, d_ffn).reshape(2, FF // 2, width)
    down = Scatter([down_half[0], down_half[1]], bits)
    got = down.send()
    got = join(*got)
    down.take(got)
    got = down.send()
    grad_gu, da, part, two = feed_back(
        h1, n2, diff, cols, gain_two, router_row, g, u, d_ffn, packs
    )
    da, out_home, *got = join(da, out_home, *got)
    down.take(got)
    wide = Scatter([grad_gu[0], grad_gu[1]], bits)
    got, got_wide = down.send(), wide.send()

    given = (da, part, x_low, n1, gain_one, cosine, sine, aux, row, q, k, v, o, lse)
    given += (w_low, w_low, w_high, w_high, w_high, w_high)
    room = [jnp.zeros((D, width), BF16), jnp.zeros((KV_WIDTH, width), BF16)]
    so_far = [jnp.zeros((ROWS, width), F32), room[0], room[1], room[1], room[0]]
    down.got, wide.got = got, got_wide
    for first, count in ((0, 2), (2, 2), (4, 1)):
        gq, gk, gv, go, dn1, d_states, one = attend_back(first, count, given, so_far)
        dn1 = advance([down, wide], dn1)
        so_far = [dn1, gq, gk, gv, go]
    attn = Scatter(
        [jnp.concatenate([gq, gk], axis=0), jnp.concatenate([gv, go], axis=0)], bits
    )
    grad_home = to_home(d_states)
    attn.got = attn.send()
    while attn.part is None or wide.part is None or down.part is None:
        advance([attn, wide, down], None)
    attn_part, gu_part, down_part = attn.part, wide.part, down.part
    grad_gain_one, grad_gain_two, grad_router = one[0], two[0], sums[0]

    x_home = states.astype(F32)
    still = (chosen == 0)[..., None]
    valid_home = validity.astype(F32)[..., None]
    apart = valid_home * (x_home - teacher.astype(F32))
    energy = energy + 0.5 * jnp.sum(jnp.where(still, apart * apart, 0.0))
    states_out = jnp.where(still, states, out_home)
    states_grad = jnp.where(still, apart, grad_home.astype(F32))

    scalars = jnp.concatenate(
        [energy[None], jnp.sum(validity).astype(F32)[None], jnp.zeros((D - 2,), F32)]
    )
    small = jnp.stack([grad_gain_one, grad_gain_two, grad_router, scalars], axis=0)
    small = all_sum(small, bits)
    mse_loss = 2.0 * small[3, 0] / (small[3, 1] * D)
    return (
        states_out,
        mse_loss,
        states_grad,
        attn_part.T,
        gu_part.T,
        down_part.T,
        small[0:2],
        small[2],
    )


def solution(mesh):
    tokens = P("dp", "ctx", None)
    flags = P("dp", "ctx")
    packs = P(None, ("dp", "ctx"))
    return jax.shard_map(
        on_device,
        mesh=mesh,
        in_specs=(tokens, tokens, flags, flags, packs, packs, packs, P(), P()),
        out_specs=(tokens, P(), tokens, packs, packs, packs, P(), P()),
        check_vma=False,
    )
```

time: 1030 us -> 557 us (0.54)
  matrix products: 347 us -> 11.6 us
  waiting for transfers between devices: 334 us -> 132 us
  Pallas kernels: 0 us -> 158 us
  other arithmetic: 150 us -> 62.9 us
  blocking collectives: 74.3 us -> 0 us
  starting transfers between devices: 31.9 us -> 69.8 us
  local copies, waits for them, and re-layouts: 71.1 us -> 95.9 us
    dot_general x40 -> x4, matrix products: 347 us -> 11.6 us  [dot(): lax.dot_general(left, right, (contract, ((), ())), preferred_element_type...]
    pallas_call x0 -> x7, Pallas kernels: none -> 158 us  [the longest x3 60.6 us: attend_back(): pl.pallas_call(functools.partial(attend_back_kernel, final), grid=(count,...]
    all_gather x7 -> x1, waiting for transfers between devices: 155 us -> 0.01 us  [on_device(): packs = lax.all_gather(feed_rows, ('dp', 'ctx'), axis=0)]
    all_to_all x6 -> x5, waiting for transfers between devices: 176 us -> 40.5 us  [to_sequence(): lax.all_to_all(blocks, 'ctx', split_axis=0, concat_axis=0, tiled=True)]
    ppermute x0 -> x41, waiting for transfers between devices: none -> 91.9 us  [swap(): return lax.ppermute(value, name, pairs)]
    psum x1 -> x0, blocking collectives: 63.9 us -> none  [on_device(): lax.psum((energy, grad_gains, grad_router), ('dp', 'ctx'))]
    reduce_sum x10 -> x3, other arithmetic: 54.5 us -> 1.6 us  [the longest x1 0.75 us: on_device(): valid = jnp.sum(picked * valid_seq.astype(F32)[None, :], axis=1)]
    ppermute x0 -> x41, starting transfers between devices: none -> 50 us  [swap(): return lax.ppermute(value, name, pairs)]
  transfers between devices with their start and end apart: 17 -> 47, of which waited for: 7 -> 16; matrix products, arithmetic and copies ran while one was open for 39% -> 26% of each run, Pallas kernels for 0% -> 23%
where the time goes in v1:
time: 557 us; the launch traced here: 550 us
  Pallas kernels  158 us (28%)
  waiting for transfers between devices  132 us (24%)
  local copies, waits for them, and re-layouts  95.9 us (17%)
  starting transfers between devices  69.8 us (13%)
  other arithmetic  62.9 us (11%)
  between operations  19.9 us (4%)
  matrix products  11.6 us (2%)
    ppermute x41, waiting for transfers between devices, swap(): return lax.ppermute(value, name, pairs)  91.9 us
    pallas_call x3, Pallas kernels, attend_back(): pl.pallas_call(functools.partial(attend_back_kernel, final), grid=(count,...  60.6 us
    ppermute x41, starting transfers between devices, swap(): return lax.ppermute(value, name, pairs)  50 us
    all_to_all x5, waiting for transfers between devices, to_sequence(): lax.all_to_all(blocks, 'ctx', split_axis=0, concat_axis=0, tiled=True)  40.5 us
    pallas_call x1, Pallas kernels, feed_back(): pl.pallas_call(feed_back_kernel, grid=(FF // SLAB,), in_specs=[fixed(ROWS...  34.2 us
    pallas_call x1, Pallas kernels, attend(): pl.pallas_call(attend_kernel, grid=(KV_HEADS,), in_specs=[fixed(ROWS, D),...  30.7 us
    convert_element_type x12, other arithmetic, cut(): return total.astype(BF16).reshape(ahead * behind, D)  24.5 us
    pallas_call x1, Pallas kernels, feed(): pl.pallas_call(feed_kernel, grid=(FF // SLAB,), in_specs=[fixed(ROWS, D),...  24.4 us
  transfers between devices with their start and end apart: 47, of which 16 were waited for; matrix products, arithmetic and copies ran while one was open for 26% of the time, Pallas kernels for 23%

profile of v1, /device:TPU:0, one launch (start us, length us, event | category | flops | bytes accessed | tf_op | source)
XLA Modules:
  0.0 550.5 jit_solution(7607474850466701795)
XLA Ops:
  9.1 4.1 collective-permute-start
  13.3 7.9 %collective-permute-done = bf16[80,960]{1,0:T(8,128)(2,1)S(1)} collective-permute-done((bf16[80,960]{1,0:T(8,128)(2,1)}, bf16[80,960]{1,0:T(8,128)(2,1)S(1)}, u32[]{:S(2)}, u32[]{:S(2)}) %collective-permute-start) | collective-permute-done | bytes 153632 | tf_op jit(solution)/shard_map/ppermute | solution.py:45
  24.9 3.2 all-to-all-start
  29.4 2.4 collective-permute-done.5
  33.9 6.3 %collective-permute-done.1 = bf16[80,960]{1,0:T(8,128)(2,1)S(1)} collective-permute-done((bf16[80,960]{1,0:T(8,128)(2,1)S(1)}, bf16[80,960]{1,0:T(8,128)(2,1)S(1)}, u32[]{:S(2)}, u32[]{:S(2)}) %collective-permute-start.1) | collective-permute-done | bytes 153632 | tf_op jit(solution)/shard_map/ppermute | solution.py:45
  42.8 9.4 %collective-permute-done.2 = bf16[160,960]{1,0:T(8,128)(2,1)S(1)} collective-permute-done((bf16[160,960]{1,0:T(8,128)(2,1)S(1)}, bf16[160,960]{1,0:T(8,128)(2,1)S(1)}, u32[]{:S(2)}, u32[]{:S(2)}) %collective-permute-start.2) | collective-permute-done | bytes 307232 | tf_op jit(solution)/shard_map/ppermute | solution.py:45
  54.5 23.3 %collective-permute-done.7 = bf16[320,960]{1,0:T(8,128)(2,1)S(1)} collective-permute-done((bf16[320,960]{1,0:T(8,128)(2,1)S(1)}, bf16[320,960]{1,0:T(8,128)(2,1)S(1)}, u32[]{:S(2)}, u32[]{:S(2)}) %collective-permute-start.7) | collective-permute-done | bytes 614432 | tf_op jit(solution)/shard_map/ppermute | solution.py:45
  81.9 4.4 all-to-all-start.1
  88.0 2.4 copy.224
  92.2 2.0 copy.225
  98.4 28.2 %all-to-all-done.1 = bf16[4,256,960]{1,2,0:T(8,128)(2,1)} async-done(((bf16[4,256,960]{1,2,0:T(8,128)(2,1)}), bf16[4,256,960]{1,2,0:T(8,128)(2,1)}, u32[]{:S(2)}, u32[]{:S(2)}) %all-to-all-start.1) | async-done | bytes 1966112 | tf_op jit(solution)/shard_map/all_to_all | solution.py:160
  126.6 3.8 all-to-all-start.2
  138.3 2.7 fusion.9.x_ref
  141.0 30.7 %attend.1 = (bf16[656,960]{1,0:T(8,128)(2,1)}, bf16[15,656,64]{2,1,0:T(8,128)(2,1)}, bf16[5,656,64]{2,1,0:T(8,128)(2,1)}, bf16[5,656,64]{2,1,0:T(8,128)(2,1)}, b...) custom-call(bf16[656,960]{1,0:T(8,128)(2,1)} %fusion.9.x_ref, ...), custom_call_target="tpu_custom_call" | custom-call | tf_op jit(solution)/shard_map/attend/pallas_call | solution.py:248
  172.0 2.7 fusion.10.t_ref
  174.7 24.4 %feed.1 = (bf16[656,960]{1,0:T(8,128)(2,1)}, bf16[656,2560]{1,0:T(8,128)(2,1)}, bf16[656,2560]{1,0:T(8,128)(2,1)}, bf16[656,2560]{1,0:T(8,128)(2,1)}, bf16[656,9...) custom-call(f32[656,960]{1,0:T(8,128)} %get-tuple-element.68.h1_ref,, ...), custom_call_target="tpu_custom_call" | custom-call | tf_op jit(solution)/shard_map/feed/pallas_call | solution.py:364
  199.1 8.1 %down_grad.1 = bf16[2560,960]{1,0:T(8,128)(2,1)} custom-call(bf16[656,2560]{1,0:T(8,128)(2,1)} %get-tuple-element.78.hid_ref, bf16[656,960]{1,0:T(8,128)(2,1)} %get-tuple-element.75.d_ffn_ref), custom_call_target="tpu_custom_call" | custom-call | tf_op jit(solution)/shard_map/down_grad/pallas_call | solution.py:408
  207.1 3.1 fusion.31
  212.0 2.4 copy.234
  216.8 2.4 copy.232
  219.2 34.2 %feed_back.1 = (bf16[2,2560,960]{2,1,0:T(8,128)(2,1)}, bf16[656,960]{1,0:T(8,128)(2,1)}, f32[656,960]{1,0:T(8,128)}, f32[8,960]{1,0:T(8,128)}) custom-call(f32[656,960]{1,0:T(8,128)} %get-tuple-element.68.h1_ref, bf16[656,960]{1,0:T(8,128)(2,1)} %get-tuple-element.70.n2_ref, f32[656,960]{1,0:T(8,128)} %get-tuple-element.71.diff_ref, ...), custom_call_target="tpu_custom_call" | custom-call | tf_op jit(solution)/shard_map/feed_back/pallas_call | solution.py:466
  253.4 9.3 %fusion.30 = (bf16[1,2560,960]{2,1,0:T(8,128)(2,1)}, bf16[1,2560,960]{2,1,0:T(8,128)(2,1)}) fusion(bf16[2,2560,960]{2,1,0:T(8,128)(2,1)} %get-tuple-element.93), kind=kLoop, calls=%fused_computation.151 | loop fusion | bytes 19660800 | tf_op jit(solution)/shard_map/slice | solution.py:717
  262.7 4.9 constant_dynamic-slice_fusion.4
  267.5 2.7 copy.240
  270.6 4.9 constant_dynamic-slice_fusion.3
  275.5 2.7 copy.242
  278.2 3.1 fusion.7
  282.7 3.6 all-to-all-start.3
  288.0 2.9 add_convert_fusion.12
  294.0 2.9 add_convert_fusion.13
  296.9 2.0 collective-permute-start.11
  298.8 12.3 %all-to-all-done.3 = bf16[4,256,960]{1,2,0:T(8,128)(2,1)S(1)} async-done(((bf16[4,256,960]{1,2,0:T(8,128)(2,1)}), bf16[4,256,960]{1,2,0:T(8,128)(2,1)S(1)}, u32[]{:S(2)}, u32[]{:S(2)}) %all-to-all-start.3) | async-done | bytes 1966112 | tf_op jit(solution)/shard_map/all_to_all | solution.py:160
  311.1 13.5 %collective-permute-done.11 = bf16[320,960]{1,0:T(8,128)(2,1)S(1)} collective-permute-done((bf16[320,960]{1,0:T(8,128)(2,1)}, bf16[320,960]{1,0:T(8,128)(2,1)S(1)}, u32[]{:S(2)}, u32[]{:S(2)}) %collective-permute-start.11) | collective-permute-done | bytes 614432 | tf_op jit(solution)/shard_map/ppermute | solution.py:45
  325.4 2.3 add_convert_fusion.24
  337.3 22.7 %attend_back.3 = (bf16[960,960]{1,0:T(8,128)(2,1)}, bf16[320,960]{1,0:T(8,128)(2,1)}, bf16[320,960]{1,0:T(8,128)(2,1)}, bf16[960,960]{1,0:T(8,128)(2,1)}, f32[65...) custom-call(bf16[656,960]{1,0:T(8,128)(2,1)} %get-tuple-element.82.d, ...), custom_call_target="tpu_custom_call", output_to_operand_aliasing={{0}: (21, {}), {1}: (22, {}), {2}: (23, {}), {3}: (24, {})} | custom-call | tf_op jit(solution)/shard_map/attend_back/pallas_call | solution.py:590
  360.7 3.1 copy.248
  363.9 4.5 add_convert_fusion
  368.4 2.4 copy.249
  371.3 3.0 copy.245
  374.3 4.5 add_convert_fusion.1
  378.8 2.4 copy.246
  385.2 2.1 collective-permute-start.17
  387.3 22.7 %attend_back.4 = (bf16[960,960]{1,0:T(8,128)(2,1)}, bf16[320,960]{1,0:T(8,128)(2,1)}, bf16[320,960]{1,0:T(8,128)(2,1)}, bf16[960,960]{1,0:T(8,128)(2,1)}, f32[65...) custom-call(bf16[656,960]{1,0:T(8,128)(2,1)} %get-tuple-element.82.d, ...), custom_call_target="tpu_custom_call", output_to_operand_aliasing={{0}: (21, {}), {1}: (22, {}), {2}: (23, {}), {3}: (24, {})} | custom-call | tf_op jit(solution)/shard_map/attend_back/pallas_call | solution.py:590
  410.0 1.9 copy.261
  414.1 2.5 copy.260
  416.6 15.3 %attend_back.5 = (bf16[960,960]{1,0:T(8,128)(2,1)}, bf16[320,960]{1,0:T(8,128)(2,1)}, bf16[320,960]{1,0:T(8,128)(2,1)}, bf16[960,960]{1,0:T(8,128)(2,1)}, f32[65...) custom-call(bf16[656,960]{1,0:T(8,128)(2,1)} %get-tuple-element.82.d, ...), custom_call_target="tpu_custom_call", output_to_operand_aliasing={{0}: (21, {}), {1}: (22, {}), {2}: (23, {}), {3}: (24, {})} | custom-call | tf_op jit(solution)/shard_map/attend_back/pallas_call | solution.py:590
  431.9 2.0 pad_maximum_fusion.3
  437.1 3.1 fusion.8
  441.6 4.7 all-to-all-start.4
  448.5 2.5 copy.254
  457.7 6.8 %collective-permute-start.35 = (bf16[80,960]{1,0:T(8,128)(2,1)S(1)}, bf16[80,960]{1,0:T(8,128)(2,1)S(1)}, u32[]{:S(2)}, u32[]{:S(2)}) collective-permute-start(bf16[80,960]{1,0:T(8,128)(2,1)S(1)} %select_convert_fusion.1), channel_id=1, source_target_pairs={{0,16},{4,20},{8,24},{12,28},{16,0},{20,4},{24,8},{28,12},{1,17},{... | collective-permute-start | bytes 460808 | tf_op jit(solution)/shard_map/ppermute | solution.py:45
  464.5 3.1 broadcast_select_fusion
  468.5 3.6 collective-permute-done.35
  472.1 2.1 fusion.18
  480.5 6.5 %convert_select_fusion = (f32[4,256,960]{1,2,0:T(8,128)}, f32[]{:T(128)}) fusion(bf16[4,256,960]{1,2,0:T(8,128)(2,1)} %all-to-all-done.4, bf16[4,256,960]{1,2,0:T(8,128)(2,1)} %param.10, bf16[4,256,960]{1,2,0:T(8,128)(2,1)} %param.9, f32[4,256]{1,0:T(4,128)S(1)} %copy-done.31, pred[4,256]{1,0:T(4,128)(4,1)S(1)} %broadcast_compare_fusion), kind=kLoop, calls=%fused_computation.2 | loop fusion | flops 8847359 | bytes 9835524 | tf_op jit(solution)/shard_map/jit(_where)/select_n | solution.py:745
  488.4 6.5 %collective-permute-start.21 = (f32[4,960]{1,0:T(4,128)S(1)}, f32[4,960]{1,0:T(4,128)S(1)}, u32[]{:S(2)}, u32[]{:S(2)}) collective-permute-start(f32[4,960]{1,0:T(4,128)S(1)} %pad_maximum_fusion.13), channel_id=1, source_target_pairs={{0,16},{4,20},{8,24},{12,28},{16,0},{20,4},{24,8},{28,12},{1,17},{... | collective-permute-start | bytes 46088 | tf_op jit(solution)/shard_map/ppermute | solution.py:45
  495.5 2.0 collective-permute-start.27
  497.8 2.1 collective-permute-start.38
  504.8 8.4 %collective-permute-done.27 = bf16[320,960]{1,0:T(8,128)(2,1)S(1)} collective-permute-done((bf16[320,960]{1,0:T(8,128)(2,1)S(1)}, bf16[320,960]{1,0:T(8,128)(2,1)S(1)}, u32[]{:S(2)}, u32[]{:S(2)}) %collective-permute-start.27) | collective-permute-done | bytes 614432 | tf_op jit(solution)/shard_map/ppermute | solution.py:45
  515.7 2.0 collective-permute-start.24
  522.7 7.6 %collective-permute-done.33 = bf16[80,960]{1,0:T(8,128)(2,1)S(1)} collective-permute-done((bf16[80,960]{1,0:T(8,128)(2,1)S(1)}, bf16[80,960]{1,0:T(8,128)(2,1)S(1)}, u32[]{:S(2)}, u32[]{:S(2)}) %collective-permute-start.33) | collective-permute-done | bytes 153632 | tf_op jit(solution)/shard_map/ppermute | solution.py:45
  530.3 2.3 collective-permute-done.29
  532.8 2.3 add_bitcast_fusion
  538.3 2.9 collective-permute-done.34
  (242 shorter events, 97.9 us)
Async XLA Ops:
  7.2 15.9 %copy-start.34 = (s32[4,256]{1,0:T(4,128)S(1)}, s32[4,256]{1,0:T(4,128)}, u32[]{:S(2)}) copy-start(s32[4,256]{1,0:T(4,128)} %param.11) | copy-start | bytes 12292
  7.2 15.9 %copy-start.32 = (s32[4,256]{1,0:T(4,128)S(1)}, s32[4,256]{1,0:T(4,128)}, u32[]{:S(2)}) copy-start(s32[4,256]{1,0:T(4,128)} %param.12) | copy-start | bytes 12292
  7.2 167.5 %all-gather.3.cloned.1.call-start = ((), (), s32[]{:S(2)}) async-start(), calls=%async_computation.5 | async-start | bytes 16220160 | tf_op jit(solution)/shard_map/all_gather | solution.py:657
  9.1 12.1 %collective-permute-start = (bf16[80,960]{1,0:T(8,128)(2,1)}, bf16[80,960]{1,0:T(8,128)(2,1)S(1)}, u32[]{:S(2)}, u32[]{:S(2)}) collective-permute-start(bf16[80,960]{1,0:T(8,128)(2,1)} %bitcast.309), channel_id=1, source_target_pairs={{0,16},{4,20},{8,24},{12,28},{16,0},{20,4},{24,8},{28,12},{1,17},{... | collective-permute-start | bytes 460808 | tf_op jit(solution)/shard_map/ppermute | solution.py:45
  22.2 9.7 %collective-permute-start.5 = (bf16[80,960]{1,0:T(8,128)(2,1)S(1)}, bf16[80,960]{1,0:T(8,128)(2,1)S(1)}, u32[]{:S(2)}, u32[]{:S(2)}) collective-permute-start(bf16[80,960]{1,0:T(8,128)(2,1)S(1)} %get-tuple-element.182), channel_id=1, source_target_pairs={{0,8},{4,12},{8,0},{12,4},{16,24},{20,28},{24,16},{28,20},{1,9},{5... | collective-permute-start | bytes 460808 | tf_op jit(solution)/shard_map/ppermute | solution.py:45
  24.9 57.1 %all-to-all-start = ((s32[4,1,256]{2,1,0:T(1,128)}), s32[4,1,256]{2,1,0:T(1,128)S(1)}, u32[]{:S(2)}, u32[]{:S(2)}) async-start(s32[4,1,256]{2,1,0:T(1,128)} %reshape.983), calls=%async_computation | async-start | bytes 8192 | tf_op jit(solution)/shard_map/all_to_all | solution.py:160
  28.1 12.0 %collective-permute-start.1 = (bf16[80,960]{1,0:T(8,128)(2,1)S(1)}, bf16[80,960]{1,0:T(8,128)(2,1)S(1)}, u32[]{:S(2)}, u32[]{:S(2)}) collective-permute-start(bf16[80,960]{1,0:T(8,128)(2,1)S(1)} %get-tuple-element.183), channel_id=1, source_target_pairs={{0,8},{4,12},{8,0},{12,4},{16,24},{20,28},{24,16},{28,20},{1,9},{5... | collective-permute-start | bytes 460808 | tf_op jit(solution)/shard_map/ppermute | solution.py:45
  31.9 10.1 %collective-permute-start.6 = (bf16[160,960]{1,0:T(8,128)(2,1)S(1)}, bf16[160,960]{1,0:T(8,128)(2,1)S(1)}, u32[]{:S(2)}, u32[]{:S(2)}) collective-permute-start(bf16[160,960]{1,0:T(8,128)(2,1)S(1)} %bitcast.305), channel_id=1, source_target_pairs={{0,2},{1,3},{2,0},{3,1},{4,6},{5,7},{6,4},{7,5},{8,10},{9,11},{10,... | collective-permute-start | bytes 921608 | tf_op jit(solution)/shard_map/ppermute | solution.py:45
  40.3 11.9 %collective-permute-start.2 = (bf16[160,960]{1,0:T(8,128)(2,1)S(1)}, bf16[160,960]{1,0:T(8,128)(2,1)S(1)}, u32[]{:S(2)}, u32[]{:S(2)}) collective-permute-start(bf16[160,960]{1,0:T(8,128)(2,1)S(1)} %bitcast.304), channel_id=1, source_target_pairs={{0,4},{4,0},{8,12},{12,8},{16,20},{20,16},{24,28},{28,24},{1,5},{5... | collective-permute-start | bytes 921608 | tf_op jit(solution)/shard_map/ppermute | solution.py:45
  42.2 11.7 %copy-start.33 = (f32[2,960]{1,0:T(2,128)S(1)}, f32[2,960]{1,0:T(2,128)}, u32[]{:S(2)}) copy-start(f32[2,960]{1,0:T(2,128)} %param.16) | copy-start | bytes 23044
  42.3 35.5 %collective-permute-start.7 = (bf16[320,960]{1,0:T(8,128)(2,1)S(1)}, bf16[320,960]{1,0:T(8,128)(2,1)S(1)}, u32[]{:S(2)}, u32[]{:S(2)}) collective-permute-start(bf16[320,960]{1,0:T(8,128)(2,1)S(1)} %bitcast.278), channel_id=1, source_target_pairs={{0,4},{4,0},{8,12},{12,8},{16,20},{20,16},{24,28},{28,24},{1,5},{5... | collective-permute-start | bytes 1843208 | tf_op jit(solution)/shard_map/ppermute | solution.py:45
  52.3 27.3 %collective-permute-start.3 = (bf16[320,960]{1,0:T(8,128)(2,1)S(1)}, bf16[320,960]{1,0:T(8,128)(2,1)S(1)}, u32[]{:S(2)}, u32[]{:S(2)}) collective-permute-start(bf16[320,960]{1,0:T(8,128)(2,1)S(1)} %bitcast.279), channel_id=1, source_target_pairs={{0,2},{1,3},{2,0},{3,1},{4,6},{5,7},{6,4},{7,5},{8,10},{9,11},{10,... | collective-permute-start | bytes 1843208 | tf_op jit(solution)/shard_map/ppermute | solution.py:45
  79.6 8.4 %collective-permute-start.8 = (bf16[640,960]{0,1:T(8,128)(2,1)}, bf16[640,960]{0,1:T(8,128)(2,1)}, u32[]{:S(2)}, u32[]{:S(2)}) collective-permute-start(bf16[640,960]{0,1:T(8,128)(2,1)} %copy.223), channel_id=1, source_target_pairs={{0,1},{1,0},{2,3},{3,2},{4,5},{5,4},{6,7},{7,6},{8,9},{9,8},{10,11... | collective-permute-start | bytes 3686408 | tf_op jit(solution)/shard_map/ppermute | solution.py:45
  81.4 12.8 %collective-permute-start.4 = (bf16[640,960]{0,1:T(8,128)(2,1)}, bf16[640,960]{0,1:T(8,128)(2,1)}, u32[]{:S(2)}, u32[]{:S(2)}) collective-permute-start(bf16[640,960]{0,1:T(8,128)(2,1)} %copy.216), channel_id=1, source_target_pairs={{0,1},{1,0},{2,3},{3,2},{4,5},{5,4},{6,7},{7,6},{8,9},{9,8},{10,11... | collective-permute-start | bytes 3686408 | tf_op jit(solution)/shard_map/ppermute | solution.py:45
  81.9 44.7 %all-to-all-start.1 = ((bf16[4,256,960]{1,2,0:T(8,128)(2,1)}), bf16[4,256,960]{1,2,0:T(8,128)(2,1)}, u32[]{:S(2)}, u32[]{:S(2)}) async-start(bf16[4,256,960]{1,2,0:T(8,128)(2,1)} %param.9), calls=%async_computation.1 | async-start | bytes 3932160 | tf_op jit(solution)/shard_map/all_to_all | solution.py:160
  126.6 45.1 %all-to-all-start.2 = ((bf16[4,256,960]{1,2,0:T(8,128)(2,1)}), bf16[4,256,960]{1,2,0:T(8,128)(2,1)S(1)}, u32[]{:S(2)}, u32[]{:S(2)}) async-start(bf16[4,256,960]{1,2,0:T(8,128)(2,1)} %param.10), calls=%async_computation.2 | async-start | bytes 3932160 | tf_op jit(solution)/shard_map/all_to_all | solution.py:160
  214.4 71.9 %collective-permute-start.10 = (bf16[640,960]{0,1:T(8,128)(2,1)}, bf16[640,960]{0,1:T(8,128)(2,1)}, u32[]{:S(2)}, u32[]{:S(2)}) collective-permute-start(bf16[640,960]{0,1:T(8,128)(2,1)} %copy.234), channel_id=1, source_target_pairs={{0,1},{1,0},{2,3},{3,2},{4,5},{5,4},{6,7},{7,6},{8,9},{9,8},{10,11... | collective-permute-start | bytes 3686408 | tf_op jit(solution)/shard_map/ppermute | solution.py:45
  219.2 67.2 %collective-permute-start.9 = (bf16[640,960]{0,1:T(8,128)(2,1)}, bf16[640,960]{0,1:T(8,128)(2,1)}, u32[]{:S(2)}, u32[]{:S(2)}) collective-permute-start(bf16[640,960]{0,1:T(8,128)(2,1)} %copy.232), channel_id=1, source_target_pairs={{0,1},{1,0},{2,3},{3,2},{4,5},{5,4},{6,7},{7,6},{8,9},{9,8},{10,11... | collective-permute-start | bytes 3686408 | tf_op jit(solution)/shard_map/ppermute | solution.py:45
  270.2 89.9 %collective-permute-start.15 = (bf16[1280,960]{0,1:T(8,128)(2,1)}, bf16[1280,960]{0,1:T(8,128)(2,1)}, u32[]{:S(2)}, u32[]{:S(2)}) collective-permute-start(bf16[1280,960]{0,1:T(8,128)(2,1)} %copy.240), channel_id=1, source_target_pairs={{0,1},{1,0},{2,3},{3,2},{4,5},{5,4},{6,7},{7,6},{8,9},{9,8},{10,11... | collective-permute-start | bytes 7372808 | tf_op jit(solution)/shard_map/ppermute | solution.py:45
  278.2 81.9 %collective-permute-start.16 = (bf16[1280,960]{0,1:T(8,128)(2,1)}, bf16[1280,960]{0,1:T(8,128)(2,1)}, u32[]{:S(2)}, u32[]{:S(2)}) collective-permute-start(bf16[1280,960]{0,1:T(8,128)(2,1)} %copy.242), channel_id=1, source_target_pairs={{0,1},{1,0},{2,3},{3,2},{4,5},{5,4},{6,7},{7,6},{8,9},{9,8},{10,11... | collective-permute-start | bytes 7372808 | tf_op jit(solution)/shard_map/ppermute | solution.py:45
  282.7 28.4 %all-to-all-start.3 = ((bf16[4,256,960]{1,2,0:T(8,128)(2,1)}), bf16[4,256,960]{1,2,0:T(8,128)(2,1)S(1)}, u32[]{:S(2)}, u32[]{:S(2)}) async-start(bf16[4,256,960]{1,2,0:T(8,128)(2,1)} %bitcast.253), calls=%async_computation.3 | async-start | bytes 3932160 | tf_op jit(solution)/shard_map/all_to_all | solution.py:160
  290.9 20.3 %collective-permute-start.12 = (bf16[320,960]{1,0:T(8,128)(2,1)}, bf16[320,960]{1,0:T(8,128)(2,1)}, u32[]{:S(2)}, u32[]{:S(2)}) collective-permute-start(bf16[320,960]{1,0:T(8,128)(2,1)} %bitcast.40), channel_id=1, source_target_pairs={{0,4},{4,0},{8,12},{12,8},{16,20},{20,16},{24,28},{28,24},{1,5},{5... | collective-permute-start | bytes 1843208 | tf_op jit(solution)/shard_map/ppermute | solution.py:45
  296.9 31.3 %copy-start.11 = (bf16[4,1,80,960]{3,2,1,0:T(8,128)(2,1)S(1)}, bf16[4,1,80,960]{3,2,1,0:T(8,128)(2,1)}, u32[]{:S(2)}) copy-start(bf16[4,1,80,960]{3,2,1,0:T(8,128)(2,1)} %get-tuple-element.154) | copy-start | bytes 1843204
  296.9 27.7 %collective-permute-start.11 = (bf16[320,960]{1,0:T(8,128)(2,1)}, bf16[320,960]{1,0:T(8,128)(2,1)S(1)}, u32[]{:S(2)}, u32[]{:S(2)}) collective-permute-start(bf16[320,960]{1,0:T(8,128)(2,1)} %bitcast.37), channel_id=1, source_target_pairs={{0,2},{1,3},{2,0},{3,1},{4,6},{5,7},{6,4},{7,5},{8,10},{9,11},{10,... | collective-permute-start | bytes 1843208 | tf_op jit(solution)/shard_map/ppermute | solution.py:45
  311.1 18.0 %copy-start.2 = (bf16[4,256,960]{1,2,0:T(8,128)(2,1)}, bf16[4,256,960]{1,2,0:T(8,128)(2,1)S(1)}, u32[]{:S(2)}) copy-start(bf16[4,256,960]{1,2,0:T(8,128)(2,1)S(1)} %all-to-all-done.3) | copy-start | bytes 5898244
  327.8 55.8 %copy-start.12 = (bf16[2,1,80,960]{3,2,1,0:T(8,128)(2,1)}, bf16[2,1,80,960]{3,2,1,0:T(8,128)(2,1)S(1)}, u32[]{:S(2)}) copy-start(bf16[2,1,80,960]{3,2,1,0:T(8,128)(2,1)S(1)} %get-tuple-element.168) | copy-start | bytes 921604
  327.8 32.2 %collective-permute-start.14 = (bf16[160,960]{1,0:T(8,128)(2,1)}, bf16[160,960]{1,0:T(8,128)(2,1)}, u32[]{:S(2)}, u32[]{:S(2)}) collective-permute-start(bf16[160,960]{1,0:T(8,128)(2,1)} %bitcast.46), channel_id=1, source_target_pairs={{0,2},{1,3},{2,0},{3,1},{4,6},{5,7},{6,4},{7,5},{8,10},{9,11},{10,... | collective-permute-start | bytes 921608 | tf_op jit(solution)/shard_map/ppermute | solution.py:45
  329.1 56.0 %copy-start.15 = (bf16[2,1,80,960]{3,2,1,0:T(8,128)(2,1)}, bf16[2,1,80,960]{3,2,1,0:T(8,128)(2,1)S(1)}, u32[]{:S(2)}) copy-start(bf16[2,1,80,960]{3,2,1,0:T(8,128)(2,1)S(1)} %get-tuple-element.170) | copy-start | bytes 921604
  329.1 30.9 %collective-permute-start.13 = (bf16[160,960]{1,0:T(8,128)(2,1)}, bf16[160,960]{1,0:T(8,128)(2,1)S(1)}, u32[]{:S(2)}, u32[]{:S(2)}) collective-permute-start(bf16[160,960]{1,0:T(8,128)(2,1)} %bitcast.43), channel_id=1, source_target_pairs={{0,4},{4,0},{8,12},{12,8},{16,20},{20,16},{24,28},{28,24},{1,5},{5... | collective-permute-start | bytes 921608 | tf_op jit(solution)/shard_map/ppermute | solution.py:45
  370.8 39.3 %collective-permute-start.20 = (bf16[640,960]{0,1:T(8,128)(2,1)}, bf16[640,960]{0,1:T(8,128)(2,1)}, u32[]{:S(2)}, u32[]{:S(2)}) collective-permute-start(bf16[640,960]{0,1:T(8,128)(2,1)} %copy.249), channel_id=1, source_target_pairs={{0,4},{4,0},{8,12},{12,8},{16,20},{20,16},{24,28},{28,24},{1,5},{5... | collective-permute-start | bytes 3686408 | tf_op jit(solution)/shard_map/ppermute | solution.py:45
  378.8 6.4 %copy-start.21 = (bf16[160,960]{1,0:T(8,128)(2,1)S(1)}, bf16[160,960]{1,0:T(8,128)(2,1)}, u32[]{:S(2)}) copy-start(bf16[160,960]{1,0:T(8,128)(2,1)} %copy-done.20) | copy-start | bytes 921604
  381.2 28.8 %collective-permute-start.19 = (bf16[640,960]{0,1:T(8,128)(2,1)}, bf16[640,960]{0,1:T(8,128)(2,1)}, u32[]{:S(2)}, u32[]{:S(2)}) collective-permute-start(bf16[640,960]{0,1:T(8,128)(2,1)} %copy.246), channel_id=1, source_target_pairs={{0,2},{1,3},{2,0},{3,1},{4,6},{5,7},{6,4},{7,5},{8,10},{9,11},{10,... | collective-permute-start | bytes 3686408 | tf_op jit(solution)/shard_map/ppermute | solution.py:45
  385.1 24.8 %collective-permute-start.18 = (bf16[80,960]{1,0:T(8,128)(2,1)}, bf16[80,960]{1,0:T(8,128)(2,1)S(1)}, u32[]{:S(2)}, u32[]{:S(2)}) collective-permute-start(bf16[80,960]{1,0:T(8,128)(2,1)} %fusion.20), channel_id=1, source_target_pairs={{0,8},{4,12},{8,0},{12,4},{16,24},{20,28},{24,16},{28,20},{1,9},{5... | collective-permute-start | bytes 460808 | tf_op jit(solution)/shard_map/ppermute | solution.py:45
  385.2 24.8 %collective-permute-start.17 = (bf16[80,960]{1,0:T(8,128)(2,1)S(1)}, bf16[80,960]{1,0:T(8,128)(2,1)S(1)}, u32[]{:S(2)}, u32[]{:S(2)}) collective-permute-start(bf16[80,960]{1,0:T(8,128)(2,1)S(1)} %fusion.19), channel_id=1, source_target_pairs={{0,8},{4,12},{8,0},{12,4},{16,24},{20,28},{24,16},{28,20},{1,9},{5... | collective-permute-start | bytes 460808 | tf_op jit(solution)/shard_map/ppermute | solution.py:45
  413.4 58.7 %collective-permute-start.37 = (bf16[320,960]{1,0:T(8,128)(2,1)}, bf16[320,960]{1,0:T(8,128)(2,1)}, u32[]{:S(2)}, u32[]{:S(2)}) collective-permute-start(bf16[320,960]{1,0:T(8,128)(2,1)} %bitcast.95), channel_id=1, source_target_pairs={{0,2},{1,3},{2,0},{3,1},{4,6},{5,7},{6,4},{7,5},{8,10},{9,11},{10,... | collective-permute-start | bytes 1843208 | tf_op jit(solution)/shard_map/ppermute | solution.py:45
  437.0 37.9 %collective-permute-start.30 = (bf16[640,960]{0,1:T(8,128)(2,1)}, bf16[640,960]{0,1:T(8,128)(2,1)}, u32[]{:S(2)}, u32[]{:S(2)}) collective-permute-start(bf16[640,960]{0,1:T(8,128)(2,1)} %copy.258), channel_id=1, source_target_pairs={{0,1},{1,0},{2,3},{3,2},{4,5},{5,4},{6,7},{7,6},{8,9},{9,8},{10,11... | collective-permute-start | bytes 3686408 | tf_op jit(solution)/shard_map/ppermute | solution.py:45
  441.6 38.9 %all-to-all-start.4 = ((bf16[4,256,960]{1,2,0:T(8,128)(2,1)}), bf16[4,256,960]{1,2,0:T(8,128)(2,1)}, u32[]{:S(2)}, u32[]{:S(2)}) async-start(bf16[4,256,960]{1,2,0:T(8,128)(2,1)} %bitcast.251), calls=%async_computation.4 | async-start | bytes 3932160 | tf_op jit(solution)/shard_map/all_to_all | solution.py:160
  451.0 27.9 %collective-permute-start.26 = (bf16[640,960]{0,1:T(8,128)(2,1)}, bf16[640,960]{0,1:T(8,128)(2,1)}, u32[]{:S(2)}, u32[]{:S(2)}) collective-permute-start(bf16[640,960]{0,1:T(8,128)(2,1)} %copy.254), channel_id=1, source_target_pairs={{0,1},{1,0},{2,3},{3,2},{4,5},{5,4},{6,7},{7,6},{8,9},{9,8},{10,11... | collective-permute-start | bytes 3686408 | tf_op jit(solution)/shard_map/ppermute | solution.py:45
  451.5 13.0 %copy-start.3 = (bf16[4,256,960]{1,2,0:T(8,128)(2,1)S(1)}, bf16[4,256,960]{1,2,0:T(8,128)(2,1)}, u32[]{:S(2)}) copy-start(bf16[4,256,960]{1,2,0:T(8,128)(2,1)} %copy-done.2) | copy-start | bytes 5898244
  452.9 19.2 %collective-permute-start.36 = (bf16[320,960]{1,0:T(8,128)(2,1)S(1)}, bf16[320,960]{1,0:T(8,128)(2,1)S(1)}, u32[]{:S(2)}, u32[]{:S(2)}) collective-permute-start(bf16[320,960]{1,0:T(8,128)(2,1)S(1)} %bitcast.300), channel_id=1, source_target_pairs={{0,4},{4,0},{8,12},{12,8},{16,20},{20,16},{24,28},{28,24},{1,5},{5... | collective-permute-start | bytes 1843208 | tf_op jit(solution)/shard_map/ppermute | solution.py:45
  457.7 14.4 %collective-permute-start.35 = (bf16[80,960]{1,0:T(8,128)(2,1)S(1)}, bf16[80,960]{1,0:T(8,128)(2,1)S(1)}, u32[]{:S(2)}, u32[]{:S(2)}) collective-permute-start(bf16[80,960]{1,0:T(8,128)(2,1)S(1)} %select_convert_fusion.1), channel_id=1, source_target_pairs={{0,16},{4,20},{8,24},{12,28},{16,0},{20,4},{24,8},{28,12},{1,17},{... | collective-permute-start | bytes 460808 | tf_op jit(solution)/shard_map/ppermute | solution.py:45
  467.6 9.0 %copy-start.8 = (bf16[8,1,80,960]{3,2,1,0:T(8,128)(2,1)S(1)}, bf16[8,1,80,960]{3,2,1,0:T(8,128)(2,1)}, u32[]{:S(2)}) copy-start(bf16[8,1,80,960]{3,2,1,0:T(8,128)(2,1)} %get-tuple-element.146) | copy-start | bytes 3686404
  474.2 40.0 %collective-permute-start.39 = (bf16[160,960]{1,0:T(8,128)(2,1)}, bf16[160,960]{1,0:T(8,128)(2,1)}, u32[]{:S(2)}, u32[]{:S(2)}) collective-permute-start(bf16[160,960]{1,0:T(8,128)(2,1)} %fusion.18), channel_id=1, source_target_pairs={{0,8},{4,12},{8,0},{12,4},{16,24},{20,28},{24,16},{28,20},{1,9},{5... | collective-permute-start | bytes 921608 | tf_op jit(solution)/shard_map/ppermute | solution.py:45
  478.2 24.1 %collective-permute-start.31 = (bf16[320,960]{1,0:T(8,128)(2,1)}, bf16[320,960]{1,0:T(8,128)(2,1)}, u32[]{:S(2)}, u32[]{:S(2)}) collective-permute-start(bf16[320,960]{1,0:T(8,128)(2,1)} %bitcast.81), channel_id=1, source_target_pairs={{0,4},{4,0},{8,12},{12,8},{16,20},{20,16},{24,28},{28,24},{1,5},{5... | collective-permute-start | bytes 1843208 | tf_op jit(solution)/shard_map/ppermute | solution.py:45
  480.5 14.5 %copy-start.6 = (bf16[8,1,80,960]{3,2,1,0:T(8,128)(2,1)S(1)}, bf16[8,1,80,960]{3,2,1,0:T(8,128)(2,1)}, u32[]{:S(2)}) copy-start(bf16[8,1,80,960]{3,2,1,0:T(8,128)(2,1)} %get-tuple-element.150) | copy-start | bytes 3686404
  488.4 9.1 %collective-permute-start.21 = (f32[4,960]{1,0:T(4,128)S(1)}, f32[4,960]{1,0:T(4,128)S(1)}, u32[]{:S(2)}, u32[]{:S(2)}) collective-permute-start(f32[4,960]{1,0:T(4,128)S(1)} %pad_maximum_fusion.13), channel_id=1, source_target_pairs={{0,16},{4,20},{8,24},{12,28},{16,0},{20,4},{24,8},{28,12},{1,17},{... | collective-permute-start | bytes 46088 | tf_op jit(solution)/shard_map/ppermute | solution.py:45
  494.9 7.3 %copy-start.10 = (bf16[2,1,160,960]{3,2,1,0:T(8,128)(2,1)S(1)}, bf16[2,1,160,960]{3,2,1,0:T(8,128)(2,1)}, u32[]{:S(2)}) copy-start(bf16[2,1,160,960]{3,2,1,0:T(8,128)(2,1)} %get-tuple-element.144) | copy-start | bytes 1843204
  495.5 17.7 %collective-permute-start.27 = (bf16[320,960]{1,0:T(8,128)(2,1)S(1)}, bf16[320,960]{1,0:T(8,128)(2,1)S(1)}, u32[]{:S(2)}, u32[]{:S(2)}) collective-permute-start(bf16[320,960]{1,0:T(8,128)(2,1)S(1)} %bitcast.299), channel_id=1, source_target_pairs={{0,2},{1,3},{2,0},{3,1},{4,6},{5,7},{6,4},{7,5},{8,10},{9,11},{10,... | collective-permute-start | bytes 1843208 | tf_op jit(solution)/shard_map/ppermute | solution.py:45
  497.6 4.0 collective-permute-start.22
  497.8 16.4 %collective-permute-start.38 = (bf16[160,960]{1,0:T(8,128)(2,1)S(1)}, bf16[160,960]{1,0:T(8,128)(2,1)S(1)}, u32[]{:S(2)}, u32[]{:S(2)}) collective-permute-start(bf16[160,960]{1,0:T(8,128)(2,1)S(1)} %fusion.16), channel_id=1, source_target_pairs={{0,8},{4,12},{8,0},{12,4},{16,24},{20,28},{24,16},{28,20},{1,9},{5... | collective-permute-start | bytes 921608 | tf_op jit(solution)/shard_map/ppermute | solution.py:45
  501.6 14.1 %collective-permute-start.23 = (f32[4,960]{1,0:T(4,128)S(1)}, f32[4,960]{1,0:T(4,128)S(1)}, u32[]{:S(2)}, u32[]{:S(2)}) collective-permute-start(f32[4,960]{1,0:T(4,128)S(1)} %fusion.40), channel_id=1, source_target_pairs={{0,4},{4,0},{8,12},{12,8},{16,20},{20,16},{24,28},{28,24},{1,5},{5... | collective-permute-start | bytes 46088 | tf_op jit(solution)/shard_map/ppermute | solution.py:45
  503.6 14.8 %collective-permute-start.32 = (bf16[160,960]{1,0:T(8,128)(2,1)S(1)}, bf16[160,960]{1,0:T(8,128)(2,1)S(1)}, u32[]{:S(2)}, u32[]{:S(2)}) collective-permute-start(bf16[160,960]{1,0:T(8,128)(2,1)S(1)} %bitcast.302), channel_id=1, source_target_pairs={{0,2},{1,3},{2,0},{3,1},{4,6},{5,7},{6,4},{7,5},{8,10},{9,11},{10,... | collective-permute-start | bytes 921608 | tf_op jit(solution)/shard_map/ppermute | solution.py:45
  513.4 7.3 %copy-start.14 = (bf16[2,1,80,960]{3,2,1,0:T(8,128)(2,1)S(1)}, bf16[2,1,80,960]{3,2,1,0:T(8,128)(2,1)}, u32[]{:S(2)}) copy-start(bf16[2,1,80,960]{3,2,1,0:T(8,128)(2,1)} %copy-done.12) | copy-start | bytes 921604
  513.4 7.3 %copy-start.17 = (bf16[2,1,80,960]{3,2,1,0:T(8,128)(2,1)S(1)}, bf16[2,1,80,960]{3,2,1,0:T(8,128)(2,1)}, u32[]{:S(2)}) copy-start(bf16[2,1,80,960]{3,2,1,0:T(8,128)(2,1)} %copy-done.15) | copy-start | bytes 921604
  513.4 7.3 %copy-start.23 = (bf16[160,960]{1,0:T(8,128)(2,1)S(1)}, bf16[160,960]{1,0:T(8,128)(2,1)}, u32[]{:S(2)}) copy-start(bf16[160,960]{1,0:T(8,128)(2,1)} %copy-done.20) | copy-start | bytes 921604
  513.4 7.3 %copy-start.28 = (bf16[80,960]{1,0:T(8,128)(2,1)S(1)}, bf16[80,960]{1,0:T(8,128)(2,1)}, u32[]{:S(2)}) copy-start(bf16[80,960]{1,0:T(8,128)(2,1)} %copy-done.26) | copy-start | bytes 460804
  513.5 7.3 %copy-start.30 = (bf16[80,960]{1,0:T(8,128)(2,1)S(1)}, bf16[80,960]{1,0:T(8,128)(2,1)}, u32[]{:S(2)}) copy-start(bf16[80,960]{1,0:T(8,128)(2,1)} %copy-done.29) | copy-start | bytes 460804
  513.5 7.1 %collective-permute-start.28 = (bf16[160,960]{1,0:T(8,128)(2,1)S(1)}, bf16[160,960]{1,0:T(8,128)(2,1)S(1)}, u32[]{:S(2)}, u32[]{:S(2)}) collective-permute-start(bf16[160,960]{1,0:T(8,128)(2,1)S(1)} %bitcast.303), channel_id=1, source_target_pairs={{0,4},{4,0},{8,12},{12,8},{16,20},{20,16},{24,28},{28,24},{1,5},{5... | collective-permute-start | bytes 921608 | tf_op jit(solution)/shard_map/ppermute | solution.py:45
  515.6 17.2 %collective-permute-start.40 = (bf16[160,960]{1,0:T(8,128)(2,1)S(1)}, bf16[160,960]{1,0:T(8,128)(2,1)S(1)}, u32[]{:S(2)}, u32[]{:S(2)}) collective-permute-start(bf16[160,960]{1,0:T(8,128)(2,1)S(1)} %select_convert_fusion), channel_id=1, source_target_pairs={{0,16},{4,20},{8,24},{12,28},{16,0},{20,4},{24,8},{28,12},{1,17},{... | collective-permute-start | bytes 921608 | tf_op jit(solution)/shard_map/ppermute | solution.py:45
  515.7 6.9 %collective-permute-start.24 = (f32[4,960]{1,0:T(4,128)S(1)}, f32[4,960]{1,0:T(4,128)S(1)}, u32[]{:S(2)}, u32[]{:S(2)}) collective-permute-start(f32[4,960]{1,0:T(4,128)S(1)} %add.360), channel_id=1, source_target_pairs={{0,2},{1,3},{2,0},{3,1},{4,6},{5,7},{6,4},{7,5},{8,10},{9,11},{10,... | collective-permute-start | bytes 46088 | tf_op jit(solution)/shard_map/ppermute | solution.py:45
  518.4 11.9 %collective-permute-start.33 = (bf16[80,960]{1,0:T(8,128)(2,1)S(1)}, bf16[80,960]{1,0:T(8,128)(2,1)S(1)}, u32[]{:S(2)}, u32[]{:S(2)}) collective-permute-start(bf16[80,960]{1,0:T(8,128)(2,1)S(1)} %fusion.24), channel_id=1, source_target_pairs={{0,8},{4,12},{8,0},{12,4},{16,24},{20,28},{24,16},{28,20},{1,9},{5... | collective-permute-start | bytes 460808 | tf_op jit(solution)/shard_map/ppermute | solution.py:45
  520.7 11.9 %collective-permute-start.29 = (bf16[80,960]{1,0:T(8,128)(2,1)S(1)}, bf16[80,960]{1,0:T(8,128)(2,1)S(1)}, u32[]{:S(2)}, u32[]{:S(2)}) collective-permute-start(bf16[80,960]{1,0:T(8,128)(2,1)S(1)} %fusion.22), channel_id=1, source_target_pairs={{0,8},{4,12},{8,0},{12,4},{16,24},{20,28},{24,16},{28,20},{1,9},{5... | collective-permute-start | bytes 460808 | tf_op jit(solution)/shard_map/ppermute | solution.py:45
  522.6 12.5 %collective-permute-start.25 = (f32[4,960]{1,0:T(4,128)S(1)}, f32[4,960]{1,0:T(4,128)S(1)}, u32[]{:S(2)}, u32[]{:S(2)}) collective-permute-start(f32[4,960]{1,0:T(4,128)S(1)} %add.361), channel_id=1, source_target_pairs={{0,1},{1,0},{2,3},{3,2},{4,5},{5,4},{6,7},{7,6},{8,9},{9,8},{10,11... | collective-permute-start | bytes 46088 | tf_op jit(solution)/shard_map/ppermute | solution.py:45
  532.7 8.4 %collective-permute-start.34 = (bf16[80,960]{1,0:T(8,128)(2,1)S(1)}, bf16[80,960]{1,0:T(8,128)(2,1)S(1)}, u32[]{:S(2)}, u32[]{:S(2)}) collective-permute-start(bf16[80,960]{1,0:T(8,128)(2,1)S(1)} %select_convert_fusion.2), channel_id=1, source_target_pairs={{0,16},{4,20},{8,24},{12,28},{16,0},{20,4},{24,8},{28,12},{1,17},{... | collective-permute-start | bytes 460808 | tf_op jit(solution)/shard_map/ppermute | solution.py:45
  (18 other events, 59.0 us)
Sparse Core Ops, SparseCore 0:
  11.5 152.2 all-gather.2

commit v2 on v1

--- a/solution.py
+++ b/solution.py
@@ -20,6 +20,7 @@
 TILE = 256
 WIDE = 768
 SLAB = 1280
+SPLIT = ((0, 2), (2, 2), (4, 1))
 CHUNK = 640
 TILES = ((0, 256, 512), (256, 512, 768), (512, ROWS, 768))
 NEG = -1e30
@@ -50,106 +51,224 @@
     return (lax.axis_index(name) >> bit) & 1
 
 
-def merge(whole, other, place, ahead):
-    low_side = own_bit(place) == 0
-    size = whole.shape[0]
-    whole, other = [v.reshape(ahead, size // ahead, D) for v in (whole, other)]
-    both = [jnp.where(low_side, whole, other), jnp.where(low_side, other, whole)]
-    return jnp.stack(both, axis=1).reshape(2 * size, D)
-
-
-def gather_halves(shard, bits):
-    other = swap(shard, bits[0])
-    low_side = own_bit(bits[0]) == 0
-    halves = [jnp.where(low_side, shard, other), jnp.where(low_side, other, shard)]
-    last = len(bits) - 1
-    for step in range(1, last + 1):
-        moved = []
-        for half, spots in zip(halves, routes(bits)):
-            spot = spots[step - 1]
-            ahead = 1 << sum(1 for s in spots[: step - 1] if s < spot)
-            moved.append((half, swap(half, bits[spot]), bits[spot], ahead))
-        halves = [merge(*m) for m in moved]
-    return halves
-
-
 def routes(bits):
     count = len(bits)
     far = list(range(1, count - 3))
     return [far + [count - 3, count - 2, count - 1], far + [count - 2, count - 3, count - 1]]
 
 
+def late_routes(bits):
+    count = len(bits)
+    far = list(range(count - 4, 0, -1))
+    return [[count - 3] + far + [count - 2], far + [count - 3, count - 2]]
+
+
+def join(*values):
+    return lax.optimization_barrier(values)
+
+
+def own_bits(bits):
+    return jnp.stack([own_bit(place) for place in bits]).astype(jnp.int32)
+
+
+def order_kernel(spots, own, mine0, other0, mine1, other1, out, sems):
+    last = len(spots[0])
+
+    def copies(place):
+        found = []
+        for half, (mine, other) in enumerate(((mine0, other0), (mine1, other1))):
+            slot = 0
+            for level, spot in enumerate(spots[half]):
+                slot = slot + ((((place >> level) & 1) ^ own[spot]) << (last - spot))
+            core = own[last + 1]
+            for k, (source, side) in enumerate(((mine, core), (other, 1 - core))):
+                found.append(
+                    pltpu.make_async_copy(
+                        source.at[place], out.at[half, slot, side], sems.at[2 * half + k, place]
+                    )
+                )
+        return found
+
+    def begin(place, carry):
+        for copy in copies(place):
+            copy.start()
+        return carry
+
+    def end(place, carry):
+        for copy in copies(place):
+            copy.wait()
+        return carry
+
+    count = mine0.shape[0]
+    lax.fori_loop(0, count, begin, 0)
+    lax.fori_loop(0, count, end, 0)
+
+
+class Gather:
+    def __init__(self, shard, bits):
+        self.bits = bits
+        self.halves, self.routes = [shard[None]], routes(bits)
+        self.step, self.part = 0, None
+        self.got = []
+
+    def send(self):
+        if self.step == 0:
+            self.got = [swap(self.halves[0], self.bits[0])]
+        else:
+            spots = [route[self.step - 1] for route in self.routes]
+            self.got = [swap(h, self.bits[s]) for h, s in zip(self.halves, spots)]
+        self.step += 1
+
+    def take(self):
+        if self.step == 1:
+            low_side = own_bit(self.bits[0]) == 0
+            shard, other = self.halves[0], self.got[0]
+            self.halves = [jnp.where(low_side, shard, other), jnp.where(low_side, other, shard)]
+        elif self.step < len(self.bits):
+            self.halves = [jnp.concatenate(p, axis=0) for p in zip(self.halves, self.got)]
+        else:
+            self.part = self.ordered()
+
+    def ordered(self):
+        count, rows, width = self.halves[0].shape
+        anywhere = pl.BlockSpec(memory_space=pl.ANY)
+        out = pl.pallas_call(
+            functools.partial(order_kernel, [r[:-1] for r in self.routes]),
+            in_specs=[pl.BlockSpec(memory_space=pltpu.SMEM)] + [anywhere] * 4,
+            out_specs=pl.BlockSpec(memory_space=pltpu.VMEM),
+            out_shape=jax.ShapeDtypeStruct((2, count, 2, rows, width), BF16),
+            scratch_shapes=[pltpu.SemaphoreType.DMA((4, count))],
+            compiler_params=pltpu.CompilerParams(vmem_limit_bytes=VMEM_LIMIT),
+            name="order",
+        )(own_bits(self.bits), self.halves[0], self.got[0], self.halves[1], self.got[1])
+        return out.reshape(-1, width)
+
+
 class Scatter:
-    def __init__(self, grads, bits):
+    def __init__(self, keep, send, bits, late=False):
         self.bits = bits
-        self.rows = [g.shape[0] >> (len(bits) - 1) for g in grads]
-        self.routes = [r[::-1] for r in routes(bits)]
-        self.parts = [[g] for g in grads]
-        self.held = [sorted(r) for r in self.routes]
-        self.step = 0
-        self.part = None
-        self.got = []
-
-    def cut(self, parts, held, spot, side, rows):
-        ahead = 1 << held.index(spot)
-        behind = (1 << (len(held) - held.index(spot) - 1)) * rows
+        self.keep, self.out = keep, send
+        self.routes = late_routes(bits) if late else [route[-2::-1] for route in routes(bits)]
+        self.step, self.part = 0, None
+        self.got, self.outs = [], []
+
+    def choose(self, half, choice):
         total = 0.0
-        for part in parts:
-            cube = part.reshape(ahead, 2, behind, D)
-            total = total + lax.dynamic_index_in_dim(cube, side, 1, keepdims=False).astype(F32)
-        return total.astype(BF16).reshape(ahead * behind, D)
-
-    def send(self):
-        arrive = []
-        if self.step < len(self.bits) - 1:
-            for i in range(2):
-                spot = self.routes[i][self.step]
-                mine = own_bit(self.bits[spot])
-                parts, held, rows = self.parts[i], self.held[i], self.rows[i]
-                out = self.cut(parts, held, spot, 1 - mine, rows)
-                self.parts[i] = [self.cut(parts, held, spot, mine, rows)]
-                self.held[i] = [h for h in held if h != spot]
-                arrive.append(swap(out, self.bits[spot]))
+        for array, held in self.parts[half]:
+            rows, width = array.shape[-2:]
+            run = [h for h in held if h in choice]
+            if run:
+                at, index = held.index(run[0]), 0
+                for spot in run:
+                    index = 2 * index + choice[spot]
+                cube = array.reshape(1 << at, 1 << len(run), -1, width)
+                array = lax.dynamic_index_in_dim(cube, index, 1, keepdims=False)
+            total = total + array.reshape(-1, rows, width).astype(F32)
+        return total
+
+    def cut(self):
+        last = len(self.bits) - 1
+        if self.step == 0:
+            self.outs, self.spots = [self.out], [last]
+        elif self.step < last:
+            self.outs, self.spots = [], []
+            for half, route in enumerate(self.routes):
+                choice = {s: own_bit(self.bits[s]) for s in route[: self.step]}
+                spot = route[self.step - 1]
+                choice[spot] = 1 - choice[spot]
+                self.outs.append(self.choose(half, choice).astype(BF16))
+                self.spots.append(spot)
         else:
             low_side = own_bit(self.bits[0]) == 0
             sums = []
-            for parts in self.parts:
-                sums.append(sum(p.astype(F32) for p in parts))
-            out = jnp.where(low_side, sums[1], sums[0]).astype(BF16)
-            self.keep = jnp.where(low_side, sums[0], sums[1])
-            arrive.append(swap(out, self.bits[0]))
+            for half, route in enumerate(self.routes):
+                sums.append(self.choose(half, {s: own_bit(self.bits[s]) for s in route})[0])
+            self.mine = jnp.where(low_side, sums[0], sums[1])
+            self.outs = [jnp.where(low_side, sums[1], sums[0]).astype(BF16)]
+            self.spots = [0]
+
+    def send(self):
+        if not self.outs:
+            self.cut()
+        self.got = [swap(out, self.bits[spot]) for out, spot in zip(self.outs, self.spots)]
+        self.outs = []
         self.step += 1
-        return arrive
-
-    def take(self, arrive):
+
+    def take(self):
+        if self.step == 1:
+            held = sorted(self.routes[0])
+            self.parts = [
+                [(self.keep[half], held), (self.got[0][half], held)] for half in range(2)
+            ]
+        elif self.step <= len(self.bits) - 1:
+            for parts, got, route in zip(self.parts, self.got, self.routes):
+                parts.append((got, sorted(route[self.step - 1 :])))
+        else:
+            self.part = self.mine + self.got[0].astype(F32)
+
+
+def split_cores(whole, bits):
+    count = 1 << (len(bits) - 2)
+    cube = whole.reshape(2 * count, 2, -1, whole.shape[-1])
+    mine = own_bit(bits[-1])
+    both = [lax.dynamic_index_in_dim(cube, side, 1, keepdims=False) for side in (mine, 1 - mine)]
+    return [b.reshape(2, count, -1, whole.shape[-1]) for b in both]
+
+
+def start(*moves):
+    for m in moves:
+        if m.part is None and not m.got:
+            m.send()
+
+
+def start_ahead(moves, *values):
+    moves = [m for m in moves if m.part is None and not m.got]
+    for m in moves:
+        m.cut()
+    flat = list(join(*values, *[o for m in moves for o in m.outs]))
+    values, flat = flat[: len(values)], flat[len(values) :]
+    for m in moves:
+        m.outs, flat = flat[: len(m.outs)], flat[len(m.outs) :]
+        m.send()
+    return values if len(values) != 1 else values[0]
+
+
+def take(*moves):
+    for m in moves:
+        if m.got:
+            m.take()
+            m.got = []
+
+
+def wait(moves, *values):
+    moves = [m for m in moves if m.got]
+    flat = list(join(*values, *[g for m in moves for g in m.got]))
+    values, flat = flat[: len(values)], flat[len(values) :]
+    for m in moves:
+        m.got, flat = flat[: len(m.got)], flat[len(m.got) :]
+    take(*moves)
+    return values if len(values) != 1 else values[0]
+
+
+def finish(*moves):
+    while any(m.part is None for m in moves):
+        start(*moves)
+        take(*moves)
+
+
+class Total:
+    def __init__(self, value, bits):
+        self.value, self.bits = value, bits
+        self.step, self.part, self.got = 0, None, []
+
+    def send(self):
+        self.got = [swap(self.value, self.bits[self.step])]
+        self.step += 1
+
+    def take(self):
+        self.value = self.value + self.got[0]
         if self.step == len(self.bits):
-            return self.keep + arrive[0].astype(F32)
-        for parts, got in zip(self.parts, arrive):
-            parts.append(got)
-
-
-def advance(scatters, value):
-    active = [s for s in scatters if s.part is None]
-    if value is not None:
-        flat = join(value, *[g for s in active for g in s.got])
-        value, flat = flat[0], list(flat[1:])
-        for s in active:
-            s.got, flat = flat[: len(s.got)], flat[len(s.got) :]
-    for s in active:
-        s.part = s.take(s.got)
-        if s.part is None:
-            s.got = s.send()
-    return value
-
-
-def join(*values):
-    return lax.optimization_barrier(values)
-
-
-def all_sum(value, bits):
-    for place in bits:
-        value = value + swap(value, place)
-    return value
+            self.part = self.value
 
 
 def dot(left, right, contract):
@@ -183,13 +302,11 @@
 
 
 def weight_specs(first):
-    return [
-        pl.BlockSpec((D // KV_HEADS, D), lambda g: (first + g, 0)),
-        pl.BlockSpec((HEAD, D), lambda g: (HEADS + first + g, 0)),
-        pl.BlockSpec((HEAD, D), lambda g: (first + g, 0)),
-    ] + [
-        pl.BlockSpec((HEAD, D), lambda g, r=r: (KV_HEADS + PER_KV * (first + g) + r, 0))
-        for r in range(PER_KV)
+    places = [HEADS, HEADS + KV_HEADS] + [QKV_COLS // HEAD + r for r in range(PER_KV)]
+    steps = [1, 1] + [PER_KV] * PER_KV
+    return [pl.BlockSpec((D // KV_HEADS, D), lambda g: (first + g, 0))] + [
+        pl.BlockSpec((HEAD, D), lambda g, p=p, s=s: (p + s * (first + g), 0))
+        for p, s in zip(places, steps)
     ]
 
 
@@ -239,7 +356,7 @@
     h1_ref[...] += nn(o_ref[0], jnp.concatenate([wo0_ref[...], wo1_ref[...], wo2_ref[...]], axis=0))
 
 
-def attend(x, gain, cosine, sine, aux, row, w_low, w_high):
+def attend(x, gain, cosine, sine, aux, row, w_attn):
     whole = lambda *shape: pl.BlockSpec(shape, lambda g: (0,) * len(shape))
     fixed = lambda *shape: pl.BlockSpec(
         shape, lambda g: (0,) * len(shape), pipeline_mode=pl.Buffered(1)
@@ -283,7 +400,7 @@
         ],
         compiler_params=pltpu.CompilerParams(vmem_limit_bytes=VMEM_LIMIT),
         name="attend",
-    )(x, gain, cosine, sine, aux, row, w_low, w_low, w_high, w_high, w_high, w_high)
+    )(x, gain, cosine, sine, aux, row, *[w_attn] * 6)
 
 
 def feed_specs(packs):
@@ -400,31 +517,54 @@
     )(h1, x, t, aux, gain, router, *packs)
 
 
-def down_grad_kernel(hid_ref, d_ffn_ref, out_ref):
-    out_ref[...] = tn(hid_ref[...], d_ffn_ref[...]).astype(BF16)
-
-
-def down_grad(hid, d_ffn):
-    return pl.pallas_call(
+def shared_out(core_ref, total, refs, rows):
+    low = core_ref[0] == 0
+    for pair in range(total.shape[0] // (2 * rows)):
+        even = total[2 * pair * rows : (2 * pair + 1) * rows]
+        odd = total[(2 * pair + 1) * rows : (2 * pair + 2) * rows]
+        refs[0][pair] = jnp.where(low, even, odd).astype(BF16)
+        refs[1][pair] = jnp.where(low, odd, even).astype(BF16)
+
+
+def down_grad_kernel(hid_ref, d_ffn_ref, core_ref, *outs):
+    total = tn(hid_ref[...], d_ffn_ref[...])
+    if len(outs) == 1:
+        outs[0][...] = total.astype(BF16)
+    else:
+        shared_out(core_ref, total, outs, outs[0].shape[1])
+
+
+def down_grad(hid, d_ffn, core, bits):
+    rows = FF >> len(bits)
+    shape, spec = (FF, D), pl.BlockSpec((CHUNK, D), lambda j: (j, 0))
+    outs = 1
+    if rows % 16 == 0:
+        outs, shape = 2, (FF // (2 * rows), rows, D)
+        spec = pl.BlockSpec((CHUNK // (2 * rows), rows, D), lambda j: (j, 0, 0))
+    got = pl.pallas_call(
         down_grad_kernel,
         grid=(FF // CHUNK,),
         in_specs=[
             pl.BlockSpec((ROWS, CHUNK), lambda j: (0, j)),
             pl.BlockSpec((ROWS, D), lambda j: (0, 0)),
-        ],
-        out_specs=pl.BlockSpec((CHUNK, D), lambda j: (j, 0)),
-        out_shape=jax.ShapeDtypeStruct((FF, D), BF16),
+            pl.BlockSpec(memory_space=pltpu.SMEM),
+        ],
+        out_specs=[spec] * outs,
+        out_shape=[jax.ShapeDtypeStruct(shape, BF16)] * outs,
         compiler_params=pltpu.CompilerParams(vmem_limit_bytes=VMEM_LIMIT),
         name="down_grad",
-    )(hid, d_ffn)
+    )(hid, d_ffn, core)
+    if outs == 1:
+        return split_cores(got[0], bits)
+    return [a.reshape(2, -1, rows, D) for a in got]
 
 
 def feed_back_kernel(
     h1_ref, n2_ref, diff_ref, cols_ref, gain_ref, router_ref, g_ref, u_ref, d_ffn_ref,
-    wg_ref, wu_ref, wd_ref,
-    ggu_ref, da_ref, part_ref, sums_ref,
-    d_gate, d_up,
+    wg_ref, wu_ref, wd_ref, core_ref,
+    *rest,
 ):
+    *grads, da_ref, part_ref, sums_ref, d_gate, d_up = rest
     step = pl.program_id(0)
 
     @pl.when(step == 0)
@@ -439,8 +579,14 @@
         sig = jax.nn.sigmoid(gate)
         d_gate[:, span] = (d_hidden * up * sig * (1.0 + gate * (1.0 - sig))).astype(BF16)
         d_up[:, span] = (d_hidden * gate * sig).astype(BF16)
-        ggu_ref[0, span] = tn(d_gate[:, span], n2_ref[...]).astype(BF16)
-        ggu_ref[1, span] = tn(d_up[:, span], n2_ref[...]).astype(BF16)
+        for half, source in enumerate((d_gate, d_up)):
+            total = tn(source[:, span], n2_ref[...])
+            if len(grads) == 1:
+                grads[0][half, span] = total.astype(BF16)
+            else:
+                rows = grads[0].shape[2]
+                spots = slice(start // (2 * rows), (start + CHUNK) // (2 * rows))
+                shared_out(core_ref, total, [a.at[half, spots] for a in grads], rows)
     part_ref[...] += nn(d_gate[...], rows_of(wg_ref)) + nn(d_up[...], rows_of(wu_ref))
 
     @pl.when(step == pl.num_programs(0) - 1)
@@ -458,12 +604,17 @@
         part_ref[...] = diff + cols_ref[:, 1:2] * router_ref[...] + d_inner
 
 
-def feed_back(h1, n2, diff, cols, gain, router, g, u, d_ffn, packs):
+def feed_back(h1, n2, diff, cols, gain, router, g, u, d_ffn, packs, core, bits):
+    rows = 2 * FF >> len(bits)
+    spec, outs, shape = pl.BlockSpec((2, SLAB, D), lambda j: (0, j, 0)), 1, (2, FF, D)
+    if rows % 16 == 0:
+        outs, shape = 2, (2, FF // (2 * rows), rows, D)
+        spec = pl.BlockSpec((2, SLAB // (2 * rows), rows, D), lambda j: (0, j, 0, 0))
     whole = lambda *shape: pl.BlockSpec(shape, lambda j: (0,) * len(shape))
     fixed = lambda *shape: pl.BlockSpec(
         shape, lambda j: (0,) * len(shape), pipeline_mode=pl.Buffered(1)
     )
-    return pl.pallas_call(
+    *grads, da, part, sums = pl.pallas_call(
         feed_back_kernel,
         grid=(FF // SLAB,),
         in_specs=[
@@ -477,15 +628,16 @@
             pl.BlockSpec((ROWS, SLAB), lambda j: (0, j)),
             fixed(ROWS, D),
             *feed_specs(packs),
+            pl.BlockSpec(memory_space=pltpu.SMEM),
         ],
         out_specs=[
-            pl.BlockSpec((2, SLAB, D), lambda j: (0, j, 0)),
+            *[spec] * outs,
             whole(ROWS, D),
             whole(ROWS, D),
             whole(8, D),
         ],
         out_shape=[
-            jax.ShapeDtypeStruct((2, FF, D), BF16),
+            *[jax.ShapeDtypeStruct(shape, BF16)] * outs,
             jax.ShapeDtypeStruct((ROWS, D), BF16),
             jax.ShapeDtypeStruct((ROWS, D), F32),
             jax.ShapeDtypeStruct((8, D), F32),
@@ -496,16 +648,18 @@
         ],
         compiler_params=pltpu.CompilerParams(vmem_limit_bytes=VMEM_LIMIT),
         name="feed_back",
-    )(h1, n2, diff, cols, gain, router, g, u, d_ffn, *packs)
+    )(h1, n2, diff, cols, gain, router, g, u, d_ffn, *packs, core)
+    if outs == 1:
+        grads = split_cores(grads[0].reshape(2 * FF, D), bits)
+    return [*grads, da, part, sums]
 
 
 def attend_back_kernel(
-    final, da_ref, part_ref, x_ref, n1_ref, gain_ref, cos_ref, sin_ref, aux_ref, row_ref,
+    first, final, da_ref, part_ref, x_ref, n1_ref, gain_ref, cos_ref, sin_ref, aux_ref, row_ref,
     q_ref, k_ref, v_ref, o_ref, l_ref, wq_ref, wk_ref, wv_ref, wo0_ref, wo1_ref, wo2_ref,
-    sofar_ref, _gq, _gk, _gv, _go,
-    gq_ref, gk_ref, gv_ref, go_ref, dn1, grad_ref, sums_ref,
-    bias, wide_q, wide_do, dq,
+    *rest,
 ):
+    pack_ref, dn1, grad_ref, sums_ref, bias, wide_q, wide_do, dq, stage, sems = rest[-10:]
     group = pl.program_id(0)
     per = D // KV_HEADS
 
@@ -514,12 +668,22 @@
         bias[...] = jnp.where(aux_ref[:, 3:4] <= row_ref[0:1, :], 0.0, NEG)
         wide_q[...] = jnp.zeros_like(wide_q)
         wide_do[...] = jnp.zeros_like(wide_do)
-        dn1[...] = sofar_ref[...]
+        dn1[...] = rest[0][...] if len(rest) > 10 else jnp.zeros_like(dn1)
 
     w_out = jnp.concatenate([wo0_ref[...], wo1_ref[...], wo2_ref[...]], axis=0)
     d_heads = nt(da_ref[...], w_out)
     d_low = d_heads.astype(BF16)
-    go_ref[...] = tn(o_ref[0], da_ref[...]).astype(BF16)
+    stage[per + 2 * HEAD :] = tn(o_ref[0], da_ref[...]).astype(BF16)
+    copies, top = [], 0
+    for rows, base in ((per, 0), (HEAD, D), (HEAD, D + KV_WIDTH), (per, QKV_COLS)):
+        place = pl.multiple_of(base + (first + group) * rows, HEAD)
+        copies.append(
+            pltpu.make_async_copy(
+                stage.at[top : top + rows], pack_ref.at[pl.ds(place, rows)], sems.at[len(copies)]
+            )
+        )
+        top += rows
+    copies[3].start()
     both = d_low.astype(F32) * o_ref[0].astype(F32)
     key, value = k_ref[0], v_ref[0]
     d_key = jnp.zeros((ROWS, HEAD), F32)
@@ -556,12 +720,13 @@
         jnp.concatenate(d_queries + [d_key * 0.125], axis=1), cos_ref[...], -sin_ref[...]
     )
     d_mixed = jnp.concatenate(turned_back + [d_value], axis=1).astype(BF16)
-    grads = tn(d_mixed, n1_ref[...]).astype(BF16)
-    gq_ref[...] = grads[:per]
-    gk_ref[...] = grads[per : per + HEAD]
-    gv_ref[...] = grads[per + HEAD :]
+    stage[: per + 2 * HEAD] = tn(d_mixed, n1_ref[...]).astype(BF16)
+    for copy in copies[:3]:
+        copy.start()
     packed = jnp.concatenate([wq_ref[...], wk_ref[...], wv_ref[...]], axis=0)
     dn1[...] += nn(d_mixed, packed)
+    for copy in copies:
+        copy.wait()
 
     if not final:
         return
@@ -588,7 +753,7 @@
     final = first + count == KV_HEADS
     kept = pl.BlockSpec(memory_space=pl.ANY)
     return pl.pallas_call(
-        functools.partial(attend_back_kernel, final),
+        functools.partial(attend_back_kernel, first, final),
         grid=(count,),
         in_specs=[
             fixed(ROWS, D),
@@ -606,26 +771,16 @@
             pl.BlockSpec((1, ROWS, per), lambda g: (first + g, 0, 0)),
             pl.BlockSpec((1, 8, WIDE), lambda g: (first + g, 0, 0)),
             *weight_specs(first),
-            fixed(ROWS, D),
+            *([fixed(ROWS, D), kept] if so_far else []),
+        ],
+        out_specs=[
             kept,
-            kept,
-            kept,
-            kept,
-        ],
-        out_specs=[
-            pl.BlockSpec((per, D), lambda g: (first + g, 0)),
-            pl.BlockSpec((HEAD, D), lambda g: (first + g, 0)),
-            pl.BlockSpec((HEAD, D), lambda g: (first + g, 0)),
-            pl.BlockSpec((per, D), lambda g: (first + g, 0)),
             whole(ROWS, D),
             whole(ROWS, D),
             whole(8, D),
         ],
         out_shape=[
-            jax.ShapeDtypeStruct((D, D), BF16),
-            jax.ShapeDtypeStruct((KV_WIDTH, D), BF16),
-            jax.ShapeDtypeStruct((KV_WIDTH, D), BF16),
-            jax.ShapeDtypeStruct((D, D), BF16),
+            jax.ShapeDtypeStruct((QKV_COLS + D, D), BF16),
             jax.ShapeDtypeStruct((ROWS, D), F32),
             jax.ShapeDtypeStruct((ROWS, D), BF16),
             jax.ShapeDtypeStruct((8, D), F32),
@@ -635,8 +790,10 @@
             pltpu.VMEM((WIDE, HEAD), BF16),
             pltpu.VMEM((WIDE, HEAD), BF16),
             pltpu.VMEM((WIDE, HEAD), F32),
-        ],
-        input_output_aliases={21: 0, 22: 1, 23: 2, 24: 3},
+            pltpu.VMEM((2 * (per + HEAD), D), BF16),
+            pltpu.SemaphoreType.DMA((4,)),
+        ],
+        input_output_aliases={21: 0} if so_far else {},
         compiler_params=pltpu.CompilerParams(vmem_limit_bytes=VMEM_LIMIT),
         name="attend_back",
     )(*given, *so_far)
@@ -650,20 +807,24 @@
     seq_length = block_rows * ctx_count
     bits = device_bits()
     gain_one, gain_two = norm_gains[0:1], norm_gains[1:2]
-
+    core = own_bit(bits[-1]).astype(jnp.int32).reshape(1)
+
+    feed_rows = jnp.concatenate([gate_up.T, down_proj.T], axis=0)
+    packs = lax.all_gather(feed_rows, ("dp", "ctx"), axis=0)
+    thin = down_proj.shape[1]
+    if thin % 16:
+        broad = packs[:, : 2 * thin].reshape(2 * FF, width)
+        packs = (broad, broad, packs[:, 2 * thin :].reshape(FF, width))
+    else:
+        packs = (packs,) * 3
     flags = to_sequence((validity + 2 * chosen).reshape(seq_count, 1, block_rows))
     x_seq = to_sequence(states).reshape(seq_length, width)
-    feed_rows = jnp.concatenate([gate_up.T, down_proj.T], axis=0)
-    packs = lax.all_gather(feed_rows, ("dp", "ctx"), axis=0)
-    w_low, w_high = gather_halves(attn_pack.T, bits)
-    teacher_late, w_low, w_high = join(teacher, w_low, w_high)
-    t_seq = to_sequence(teacher_late).reshape(seq_length, width)
-    thin = down_proj.shape[1]
-    if thin % 16:
-        wide = packs[:, : 2 * thin].reshape(2 * FF, width)
-        packs = (wide, wide, packs[:, 2 * thin :].reshape(FF, width))
-    else:
-        packs = (packs, packs, packs)
+    attn_in = Gather(attn_pack.T, bits)
+    start(attn_in)
+    flags = wait([attn_in], flags)
+    start(attn_in)
+    wait([attn_in])
+    start(attn_in)
 
     flags = flags.reshape(seq_length)
     chosen_seq, valid_seq = flags >> 1, flags & 1
@@ -675,10 +836,6 @@
     pos = jnp.sum(picked * place.astype(F32)[None, :], axis=1)
     valid = jnp.sum(picked * valid_seq.astype(F32)[None, :], axis=1)
     live = (jnp.arange(ROWS) < jnp.sum(chosen_seq)).astype(F32)
-
-    x_low = dot(pick, x_seq, ((1,), (0,))).astype(BF16)
-    t_low = dot(pick, t_seq, ((1,), (0,))).astype(BF16)
-
     half = HEAD // 2
     freqs = THETA ** (-(jnp.arange(half).astype(F32) * 2.0 / HEAD))
     angles = pos[:, None] * freqs[None, :]
@@ -692,63 +849,87 @@
     row = jnp.pad(row, ((0, 0), (0, WIDE - ROWS)), constant_values=1e6)
     router_row = router[None, :]
 
-    n1, q, k, v, o, lse, h1 = attend(x_low, gain_one, cosine, sine, aux, row, w_low, w_high)
+    x_seq, pick, cosine, sine, aux, row = wait(
+        [attn_in], x_seq, pick, cosine, sine, aux, row
+    )
+    start(attn_in)
+    x_low = dot(pick, x_seq, ((1,), (0,))).astype(BF16)
+    x_low = wait([attn_in], x_low)
+    start(attn_in)
+    wait([attn_in])
+    finish(attn_in)
+    w_attn = attn_in.part
+    (late,) = join(teacher, w_attn)[:1]
+    t_seq = to_sequence(late).reshape(seq_length, width)
+
+    n1, q, k, v, o, lse, h1 = attend(x_low, gain_one, cosine, sine, aux, row, w_attn)
+    t_low = dot(pick, t_seq, ((1,), (0,))).astype(BF16)
     n2, g, u, hid, y, diff, cols, sums, d_ffn = feed(
         h1, x_low, t_low, aux, gain_two, router_row, packs
     )
     energy = jnp.sum(sums[1])
 
-    def to_home(compact):
-        whole = dot(pick, compact, ((0,), (0,))).astype(BF16)
-        return to_sequence(whole.reshape(ctx_count, block_rows, width))
-
-    out_home = to_home(y)
-    down_half = down_grad(hid, d_ffn).reshape(2, FF // 2, width)
-    down = Scatter([down_half[0], down_half[1]], bits)
-    got = down.send()
-    got = join(*got)
-    down.take(got)
-    got = down.send()
-    grad_gu, da, part, two = feed_back(
-        h1, n2, diff, cols, gain_two, router_row, g, u, d_ffn, packs
-    )
-    da, out_home, *got = join(da, out_home, *got)
-    down.take(got)
-    wide = Scatter([grad_gu[0], grad_gu[1]], bits)
-    got, got_wide = down.send(), wide.send()
+    def spread(compact):
+        whole = dot(compact, pick, ((0,), (0,))).astype(BF16)
+        return whole.reshape(width, ctx_count, block_rows).transpose(1, 0, 2)
+
+    def to_home(columns):
+        return to_sequence(columns.transpose(0, 2, 1))
+
+    down = Scatter(*down_grad(hid, d_ffn, core, bits), bits)
+    start(down)
+    d_ffn, out_columns = wait([down], d_ffn, spread(y))
+    out_home = to_home(out_columns)
+    d_ffn = start_ahead([down], d_ffn)
+    *grad_gu, da, part, two = feed_back(
+        h1, n2, diff, cols, gain_two, router_row, g, u, d_ffn, packs, core, bits
+    )
+    da, out_home, *grad_gu = wait([down], da, out_home, *grad_gu)
+    wide = Scatter(*grad_gu, bits)
+    start(wide, down)
+    da = wait([wide], da)
+    da = start_ahead([wide], da)
 
     given = (da, part, x_low, n1, gain_one, cosine, sine, aux, row, q, k, v, o, lse)
-    given += (w_low, w_low, w_high, w_high, w_high, w_high)
-    room = [jnp.zeros((D, width), BF16), jnp.zeros((KV_WIDTH, width), BF16)]
-    so_far = [jnp.zeros((ROWS, width), F32), room[0], room[1], room[1], room[0]]
-    down.got, wide.got = got, got_wide
-    for first, count in ((0, 2), (2, 2), (4, 1)):
-        gq, gk, gv, go, dn1, d_states, one = attend_back(first, count, given, so_far)
-        dn1 = advance([down, wide], dn1)
-        so_far = [dn1, gq, gk, gv, go]
-    attn = Scatter(
-        [jnp.concatenate([gq, gk], axis=0), jnp.concatenate([gv, go], axis=0)], bits
-    )
-    grad_home = to_home(d_states)
-    attn.got = attn.send()
-    while attn.part is None or wide.part is None or down.part is None:
-        advance([attn, wide, down], None)
-    attn_part, gu_part, down_part = attn.part, wide.part, down.part
-    grad_gain_one, grad_gain_two, grad_router = one[0], two[0], sums[0]
+    given += (w_attn,) * 6
+    so_far = []
+    for first, count in SPLIT:
+        grad_attn, dn1, d_states, one = attend_back(first, count, given, so_far)
+        if first + count < KV_HEADS:
+            dn1 = wait([wide, down], dn1)
+            dn1 = start_ahead([wide, down], dn1)
+        so_far = [dn1, grad_attn]
+    grad_attn, d_states = wait([wide, down], grad_attn, d_states)
+    attn = Scatter(*split_cores(grad_attn, bits), bits, late=True)
 
     x_home = states.astype(F32)
     still = (chosen == 0)[..., None]
     valid_home = validity.astype(F32)[..., None]
     apart = valid_home * (x_home - teacher.astype(F32))
     energy = energy + 0.5 * jnp.sum(jnp.where(still, apart * apart, 0.0))
+    scalars = jnp.concatenate(
+        [energy[None], jnp.sum(validity).astype(F32)[None], jnp.zeros((D - 2,), F32)]
+    )
+    total = Total(jnp.stack([one[0], two[0], sums[0], scalars], axis=0), bits)
+
+    start(attn, wide, down, total)
+    columns = wait([attn, total], spread(d_states))
+    grad_home = to_home(columns)
+    take(wide, down)
+    while attn.step < len(bits):
+        start(attn, wide, down, total)
+        if attn.step < len(bits):
+            wait([attn, total])
+            take(wide, down)
+    grad_home, attn.mine = join(grad_home, attn.mine)
+    take(attn, wide, down, total)
+    finish(attn, wide, down, total)
+    attn_part, gu_part, down_part = attn.part, wide.part, down.part
+
     states_out = jnp.where(still, states, out_home)
     states_grad = jnp.where(still, apart, grad_home.astype(F32))
 
-    scalars = jnp.concatenate(
-        [energy[None], jnp.sum(validity).astype(F32)[None], jnp.zeros((D - 2,), F32)]
-    )
-    small = jnp.stack([grad_gain_one, grad_gain_two, grad_router, scalars], axis=0)
-    small = all_sum(small, bits)
+    small = total.part
     mse_loss = 2.0 * small[3, 0] / (small[3, 1] * D)
     return (
         states_out,

time: 557 us -> 456 us (0.82)
  local copies, waits for them, and re-layouts: 95.9 us -> 29 us
  waiting for transfers between devices: 132 us -> 94.9 us
  starting transfers between devices: 69.8 us -> 61.5 us
  Pallas kernels: 158 us -> 165 us
    all_to_all x5, waiting for transfers between devices: 40.5 us -> 7.34 us  [to_sequence(): lax.all_to_all(blocks, 'ctx', split_axis=0, concat_axis=0, tiled=True)]
    reshape x11 -> x3, local copies, waits for them, and re-layouts: 20.2 us -> 3.18 us  [the longest x2 2.92 us: spread(): return whole.reshape(width, ctx_count, block_rows).transpose(1, 0, 2)]
    dynamic_slice x6 -> x1, local copies, waits for them, and re-layouts: 16.6 us -> 3.7 us  [split_cores(): lax.dynamic_index_in_dim(cube, side, 1, keepdims=False)]
    optimization_barrier x6 -> x1, local copies, waits for them, and re-layouts: 13.7 us -> 0.91 us  [join(): return lax.optimization_barrier(values)]
    ppermute x41 -> x38, waiting for transfers between devices: 91.9 us -> 79.6 us  [swap(): return lax.ppermute(value, name, pairs)]
    convert_element_type x15 -> x21, other arithmetic: 27.1 us -> 37.9 us  [the longest x17 30.4 us: cut(): self.outs.append(self.choose(half, choice).astype(BF16))]
    ppermute x41 -> x38, starting transfers between devices: 50 us -> 41.3 us  [swap(): return lax.ppermute(value, name, pairs)]
    all_gather x1, waiting for transfers between devices: 0.01 us -> 7.89 us  [on_device(): packs = lax.all_gather(feed_rows, ('dp', 'ctx'), axis=0)]
  transfers between devices with their start and end apart: 47 -> 44, of which waited for: 16 -> 19; matrix products, arithmetic and copies ran while one was open for 26% -> 16% of each run, Pallas kernels for 23% -> 30%
where the time goes in v2:
time: 456 us; the launch traced here: 449 us
  Pallas kernels  165 us (36%)
  waiting for transfers between devices  94.9 us (21%)
  other arithmetic  66.9 us (15%)
  starting transfers between devices  61.5 us (13%)
  local copies, waits for them, and re-layouts  29 us (6%)
  between operations  19.5 us (4%)
  matrix products  12.7 us (3%)
    ppermute x38, waiting for transfers between devices, swap(): return lax.ppermute(value, name, pairs)  79.6 us
    pallas_call x3, Pallas kernels, attend_back(): pl.pallas_call(functools.partial(attend_back_kernel, first, final), grid=...  62 us
    ppermute x38, starting transfers between devices, swap(): return lax.ppermute(value, name, pairs)  41.3 us
    pallas_call x1, Pallas kernels, feed_back(): pl.pallas_call(feed_back_kernel, grid=(FF // SLAB,), in_specs=[fixed(ROWS...  34.1 us
    pallas_call x1, Pallas kernels, attend(): pl.pallas_call(attend_kernel, grid=(KV_HEADS,), in_specs=[fixed(ROWS, D),...  30.7 us
    convert_element_type x17, other arithmetic, cut(): self.outs.append(self.choose(half, choice).astype(BF16))  30.4 us
    pallas_call x1, Pallas kernels, feed(): pl.pallas_call(feed_kernel, grid=(FF // SLAB,), in_specs=[fixed(ROWS, D),...  24.2 us
    all_to_all x5, starting transfers between devices, to_sequence(): lax.all_to_all(blocks, 'ctx', split_axis=0, concat_axis=0, tiled=True)  20.2 us
  transfers between devices with their start and end apart: 44, of which 19 were waited for; matrix products, arithmetic and copies ran while one was open for 16% of the time, Pallas kernels for 30%

profile of v2, /device:TPU:0, one launch (start us, length us, event | category | flops | bytes accessed | tf_op | source)
XLA Modules:
  0.0 449.5 jit_solution(7422494583180889976)
XLA Ops:
  7.2 1.9 pad_maximum_fusion.4
  10.4 4.3 all-to-all-start.1
  14.7 3.1 collective-permute-start
  18.5 3.6 all-to-all-start
  22.1 4.0 collective-permute-done
  27.8 3.9 collective-permute-start.2
  35.5 6.4 %collective-permute-done.2 = bf16[1,80,960]{2,1,0:T(8,128)(2,1)S(1)} collective-permute-done((bf16[1,80,960]{2,1,0:T(8,128)(2,1)S(1)}, bf16[1,80,960]{2,1,0:T(8,128)(2,1)S(1)}, u32[]{:S(2)}, u32[]{:S(2)}) %collective-permute-start.2) | collective-permute-done | bytes 153632 | tf_op jit(solution)/shard_map/ppermute | solution.py:46
  41.9 3.6 collective-permute-done.1
  52.6 10.0 %collective-permute-done.4 = bf16[2,80,960]{2,1,0:T(8,128)(2,1)S(1)} collective-permute-done((bf16[2,80,960]{2,1,0:T(8,128)(2,1)}, bf16[2,80,960]{2,1,0:T(8,128)(2,1)S(1)}, u32[]{:S(2)}, u32[]{:S(2)}) %collective-permute-start.4) | collective-permute-done | bytes 307232 | tf_op jit(solution)/shard_map/ppermute | solution.py:46
  64.2 2.4 collective-permute-start.6
  66.6 2.7 convolution_convert_fusion.3.x_ref
  69.3 15.8 %collective-permute-done.6 = bf16[4,80,960]{2,1,0:T(8,128)(2,1)S(1)} collective-permute-done((bf16[4,80,960]{2,1,0:T(8,128)(2,1)S(1)}, bf16[4,80,960]{2,1,0:T(8,128)(2,1)S(1)}, u32[]{:S(2)}, u32[]{:S(2)}) %collective-permute-start.6) | collective-permute-done | bytes 614432 | tf_op jit(solution)/shard_map/ppermute | solution.py:46
  88.7 2.1 collective-permute-done.8.other1
  90.8 2.8 collective-permute-done.7.other0
  93.6 5.9 %order.1 = bf16[2,8,2,80,960]{4,3,2,1,0:T(8,128)(2,1)} custom-call(s32[5]{0:T(128)} %stack.58.own, bf16[8,80,960]{2,1,0:T(8,128)(2,1)} %copy-done.16, bf16[8,80,960]{2,1,0:T(8,128)(2,1)} %collective-permute-done.7.other0, bf16[8,80,960]{2,1,0:T(8,128)(2,1)} %copy-done.17, bf16[8,80,960]{2,1,0:T(8,128)(2,1)} %collective-permute-done.8.other1), custom_call_target="tpu_custom_call" | custom-call | tf_op jit(solution)/shard_map/order/pallas_call | solution.py:135
  99.5 4.2 all-to-all-start.2
  105.2 30.7 %attend.1 = (bf16[656,960]{1,0:T(8,128)(2,1)}, bf16[15,656,64]{2,1,0:T(8,128)(2,1)}, bf16[5,656,64]{2,1,0:T(8,128)(2,1)}, bf16[5,656,64]{2,1,0:T(8,128)(2,1)}, b...) custom-call(bf16[656,960]{1,0:T(8,128)(2,1)} %convolution_convert_fusion.3.x_ref, ...), custom_call_target="tpu_custom_call" | custom-call | tf_op jit(solution)/shard_map/attend/pallas_call | solution.py:365
  135.9 6.8 %all-to-all-done.2 = bf16[4,256,960]{1,2,0:T(8,128)(2,1)S(1)} async-done(((bf16[4,256,960]{1,2,0:T(8,128)(2,1)}), bf16[4,256,960]{1,2,0:T(8,128)(2,1)S(1)}, u32[]{:S(2)}, u32[]{:S(2)}) %all-to-all-start.2) | async-done | bytes 1966112 | tf_op jit(solution)/shard_map/all_to_all | solution.py:279
  144.0 2.7 convolution_convert_fusion.2.t_ref
  146.7 7.9 %all-gather.3.cloned.1.call-done = bf16[7680,960]{1,0:T(8,128)(2,1)} async-done(((bf16[240,960]{1,0:T(8,128)(2,1)}), bf16[7680,960]{1,0:T(8,128)(2,1)}) %all-gather.3.cloned.1.call-update) | async-done | bytes 14745616 | tf_op jit(solution)/shard_map/all_gather | solution.py:813
  154.6 24.2 %feed.1 = (bf16[656,960]{1,0:T(8,128)(2,1)}, bf16[656,2560]{1,0:T(8,128)(2,1)}, bf16[656,2560]{1,0:T(8,128)(2,1)}, bf16[656,2560]{1,0:T(8,128)(2,1)}, bf16[656,9...) custom-call(f32[656,960]{1,0:T(8,128)} %get-tuple-element.128.h1_ref, ...), custom_call_target="tpu_custom_call" | custom-call | tf_op jit(solution)/shard_map/feed/pallas_call | solution.py:481
  178.8 8.1 %down_grad.1 = (bf16[16,80,960]{2,1,0:T(8,128)(2,1)}, bf16[16,80,960]{2,1,0:T(8,128)(2,1)}) custom-call(bf16[656,2560]{1,0:T(8,128)(2,1)} %get-tuple-element.137.hid_ref, bf16[656,960]{1,0:T(8,128)(2,1)} %get-tuple-element.142.d_ffn_ref, s32[1]{0:T(128)} %bitcast.9.core_ref), custom_call_target="tpu_custom_call" | custom-call | tf_op jit(solution)/shard_map/down_grad/pallas_call | solution.py:544
  187.1 3.5 convolution_convert_fusion.1
  193.5 3.6 all-to-all-start.3
  197.1 2.2 fusion.48
  203.2 2.0 collective-permute-start.10
  205.2 1.9 collective-permute-start.11
  207.1 34.1 %feed_back.1 = (bf16[2,8,160,960]{3,2,1,0:T(8,128)(2,1)}, bf16[2,8,160,960]{3,2,1,0:T(8,128)(2,1)}, bf16[656,960]{1,0:T(8,128)(2,1)}, f32[656,960]{1,0:T(8,128)}, f32[8,960]{1,0:T(8,128)}) custom-call(f32[656,960]{1,0:T(8,128)} %get-tuple-element.128.h1_ref, bf16[656,960]{1,0:T(8,128)(2,1)} %get-tuple-element.130.n2_ref, ...), custom_call_target="tpu_custom_call" | custom-call | tf_op jit(solution)/shard_map/feed_back/pallas_call | solution.py:617
  241.3 3.8 fusion.45
  245.1 5.0 %collective-permute-done.12 = bf16[2,8,160,960]{3,2,1,0:T(8,128)(2,1)S(1)} collective-permute-done((bf16[2,8,160,960]{3,2,1,0:T(8,128)(2,1)}, bf16[2,8,160,960]{3,2,1,0:T(8,128)(2,1)S(1)}, u32[]{:S(2)}, u32[]{:S(2)}) %collective-permute-start.12) | collective-permute-done | bytes 4915232 | tf_op jit(solution)/shard_map/ppermute | solution.py:46
  251.0 2.0 fusion.3
  254.9 2.2 fusion.16
  257.1 1.7 collective-permute-start.15
  258.9 2.0 fusion.17
  260.8 2.0 collective-permute-start.16
  262.8 22.7 %attend_back.3 = (bf16[2560,960]{1,0:T(8,128)(2,1)}, f32[656,960]{1,0:T(8,128)}, bf16[656,960]{1,0:T(8,128)(2,1)}, f32[8,960]{1,0:T(8,128)}) custom-call(bf16[656,960]{1,0:T(8,128)(2,1)} %get-tuple-element.155.da_ref, f32[656,960]{1,0:T(8,128)} %get-tuple-element.156.part_ref, bf16[656,960]{1,0:T(8,128)(2,1)} %convolution_convert_fusion.3.x_ref, ...), custom_call_target="tpu_custom_call" | custom-call | tf_op jit(solution)/shard_map/attend_back/pallas_call | solution.py:755
  285.5 7.3 %collective-permute-done.15 = bf16[2,80,960]{2,1,0:T(8,128)(2,1)S(1)} collective-permute-done((bf16[2,80,960]{2,1,0:T(8,128)(2,1)}, bf16[2,80,960]{2,1,0:T(8,128)(2,1)S(1)}, u32[]{:S(2)}, u32[]{:S(2)}) %collective-permute-start.15) | collective-permute-done | bytes 307232 | tf_op jit(solution)/shard_map/ppermute | solution.py:46
  292.8 2.1 fusion.30
  294.9 1.7 fusion.27
  296.6 2.7 fusion.5
  299.3 2.7 fusion.6
  306.0 24.0 %attend_back.4 = (bf16[2560,960]{1,0:T(8,128)(2,1)}, f32[656,960]{1,0:T(8,128)}, bf16[656,960]{1,0:T(8,128)(2,1)}, f32[8,960]{1,0:T(8,128)}) custom-call(bf16[656,960]{1,0:T(8,128)(2,1)} %get-tuple-element.155.da_ref, f32[656,960]{1,0:T(8,128)} %get-tuple-element.156.part_ref, ...), custom_call_target="tpu_custom_call", output_to_operand_aliasing={{0}: (21, {})} | custom-call | tf_op jit(solution)/shard_map/attend_back/pallas_call | solution.py:755
  330.0 2.5 fusion.13
  332.5 2.1 fusion.15
  334.6 2.3 fusion.40
  338.9 2.1 collective-permute-start.23
  341.0 15.3 %attend_back.5 = (bf16[2560,960]{1,0:T(8,128)(2,1)}, f32[656,960]{1,0:T(8,128)}, bf16[656,960]{1,0:T(8,128)(2,1)}, f32[8,960]{1,0:T(8,128)}) custom-call(bf16[656,960]{1,0:T(8,128)(2,1)} %get-tuple-element.155.da_ref, f32[656,960]{1,0:T(8,128)} %get-tuple-element.156.part_ref, ...), custom_call_target="tpu_custom_call", output_to_operand_aliasing={{0}: (21, {})} | custom-call | tf_op jit(solution)/shard_map/attend_back/pallas_call | solution.py:755
  357.1 3.7 constant_dynamic-slice_fusion.2
  361.5 3.3 select_reduce_fusion.1
  370.2 3.9 convolution_convert_fusion
  376.0 2.0 fusion.47
  384.9 4.6 %all-to-all-start.4 = ((bf16[4,256,960]{1,2,0:T(8,128)(2,1)}), bf16[4,256,960]{1,2,0:T(8,128)(2,1)}, u32[]{:S(2)}, u32[]{:S(2)}) async-start(bf16[4,256,960]{1,2,0:T(8,128)(2,1)} %bitcast.295), calls=%async_computation.4 | async-start | bytes 3932160 | tf_op jit(solution)/shard_map/all_to_all | solution.py:279
  390.2 2.2 fusion.18
  392.4 1.8 collective-permute-start.37
  394.2 4.7 %collective-permute-done.28 = f32[4,960]{1,0:T(4,128)S(1)} collective-permute-done((f32[4,960]{1,0:T(4,128)S(1)}, f32[4,960]{1,0:T(4,128)S(1)}, u32[]{:S(2)}, u32[]{:S(2)}) %collective-permute-start.28) | collective-permute-done | bytes 15392 | tf_op jit(solution)/shard_map/ppermute | solution.py:46
  400.3 2.3 collective-permute-start.30
  404.4 2.4 fusion.31
  406.8 3.7 collective-permute-done.31
  410.5 6.7 %collective-permute-done.29 = bf16[2,80,960]{2,1,0:T(8,128)(2,1)S(1)} collective-permute-done((bf16[2,80,960]{2,1,0:T(8,128)(2,1)S(1)}, bf16[2,80,960]{2,1,0:T(8,128)(2,1)S(1)}, u32[]{:S(2)}, u32[]{:S(2)}) %collective-permute-start.29) | collective-permute-done | bytes 307232 | tf_op jit(solution)/shard_map/ppermute | solution.py:46
  421.8 3.1 fusion.7
  424.9 1.9 collective-permute-done.33
  426.8 1.8 collective-permute-done.32
  433.3 4.8 %convert_select_fusion = f32[4,256,960]{1,2,0:T(8,128)} fusion(bf16[4,256,960]{1,2,0:T(8,128)(2,1)} %all-to-all-done.4, bf16[4,256,960]{1,2,0:T(8,128)(2,1)} %param.10, bf16[4,256,960]{1,2,0:T(8,128)(2,1)S(1)} %copy-done, f32[4,256]{1,0:T(4,128)S(1)} %get-tuple-element.243, pred[4,256]{1,0:T(4,128)(4,1)S(1)} %broadcast_compare_fusion), kind=kLoop, calls=%fused_computation.2 | loop fusion | flops 5898240 | bytes 9835520 | tf_op jit(solution)/shard_map/jit(_where)/select_n | solution.py:930
  438.2 2.3 collective-permute-done.36
  (213 shorter events, 64.5 us)
Async XLA Ops:
  7.2 7.5 %copy-start.37 = (bf16[960,80]{0,1:T(8,128)(2,1)S(1)}, bf16[960,80]{0,1:T(8,128)(2,1)}, u32[]{:S(2)}) copy-start(bf16[960,80]{0,1:T(8,128)(2,1)} %param.13) | copy-start | bytes 460804
  7.2 147.4 %all-gather.3.cloned.1.call-start = ((), (), s32[]{:S(2)}) async-start(), calls=%async_computation.5 | async-start | bytes 16220160 | tf_op jit(solution)/shard_map/all_gather | solution.py:813
  10.4 8.1 %all-to-all-start.1 = ((s32[4,1,256]{2,1,0:T(1,128)}), s32[4,1,256]{2,1,0:T(1,128)S(1)}, u32[]{:S(2)}, u32[]{:S(2)}) async-start(s32[4,1,256]{2,1,0:T(1,128)} %reshape.787), calls=%async_computation.1 | async-start | bytes 8192 | tf_op jit(solution)/shard_map/all_to_all | solution.py:279
  14.7 11.4 %collective-permute-start = (bf16[1,80,960]{2,1,0:T(8,128)(2,1)S(1)}, bf16[1,80,960]{2,1,0:T(8,128)(2,1)S(1)}, u32[]{:S(2)}, u32[]{:S(2)}) collective-permute-start(bf16[1,80,960]{2,1,0:T(8,128)(2,1)S(1)} %bitcast.322), channel_id=1, source_target_pairs={{0,16},{4,20},{8,24},{12,28},{16,0},{20,4},{24,8},{28,12},{1,17},{... | collective-permute-start | bytes 460808 | tf_op jit(solution)/shard_map/ppermute | solution.py:46
  18.5 33.9 %all-to-all-start = ((bf16[4,256,960]{1,2,0:T(8,128)(2,1)}), bf16[4,256,960]{1,2,0:T(8,128)(2,1)S(1)}, u32[]{:S(2)}, u32[]{:S(2)}) async-start(bf16[4,256,960]{1,2,0:T(8,128)(2,1)} %param.9), calls=%async_computation | async-start | bytes 3932160 | tf_op jit(solution)/shard_map/all_to_all | solution.py:279
  27.8 14.1 %collective-permute-start.2 = (bf16[1,80,960]{2,1,0:T(8,128)(2,1)S(1)}, bf16[1,80,960]{2,1,0:T(8,128)(2,1)S(1)}, u32[]{:S(2)}, u32[]{:S(2)}) collective-permute-start(bf16[1,80,960]{2,1,0:T(8,128)(2,1)S(1)} %get-tuple-element.232), channel_id=1, source_target_pairs={{0,8},{4,12},{8,0},{12,4},{16,24},{20,28},{24,16},{28,20},{1,9},{5... | collective-permute-start | bytes 460808 | tf_op jit(solution)/shard_map/ppermute | solution.py:46
  31.7 13.8 %collective-permute-start.1 = (bf16[1,80,960]{2,1,0:T(8,128)(2,1)S(1)}, bf16[1,80,960]{2,1,0:T(8,128)(2,1)S(1)}, u32[]{:S(2)}, u32[]{:S(2)}) collective-permute-start(bf16[1,80,960]{2,1,0:T(8,128)(2,1)S(1)} %get-tuple-element.233), channel_id=1, source_target_pairs={{0,8},{4,12},{8,0},{12,4},{16,24},{20,28},{24,16},{28,20},{1,9},{5... | collective-permute-start | bytes 460808 | tf_op jit(solution)/shard_map/ppermute | solution.py:46
  46.3 16.3 %collective-permute-start.4 = (bf16[2,80,960]{2,1,0:T(8,128)(2,1)}, bf16[2,80,960]{2,1,0:T(8,128)(2,1)S(1)}, u32[]{:S(2)}, u32[]{:S(2)}) collective-permute-start(bf16[2,80,960]{2,1,0:T(8,128)(2,1)} %pad_maximum_fusion.8), channel_id=1, source_target_pairs={{0,2},{1,3},{2,0},{3,1},{4,6},{5,7},{6,4},{7,5},{8,10},{9,11},{10,... | collective-permute-start | bytes 921608 | tf_op jit(solution)/shard_map/ppermute | solution.py:46
  48.0 16.0 %collective-permute-start.3 = (bf16[2,80,960]{2,1,0:T(8,128)(2,1)}, bf16[2,80,960]{2,1,0:T(8,128)(2,1)S(1)}, u32[]{:S(2)}, u32[]{:S(2)}) collective-permute-start(bf16[2,80,960]{2,1,0:T(8,128)(2,1)} %pad_maximum_fusion.7), channel_id=1, source_target_pairs={{0,4},{4,0},{8,12},{12,8},{16,20},{20,16},{24,28},{28,24},{1,5},{5... | collective-permute-start | bytes 921608 | tf_op jit(solution)/shard_map/ppermute | solution.py:46
  52.6 14.0 %copy-start.24 = (bf16[656,1024]{1,0:T(8,128)(2,1)S(1)}, bf16[656,1024]{1,0:T(8,128)(2,1)}, u32[]{:S(2)}) copy-start(bf16[656,1024]{1,0:T(8,128)(2,1)} %fusion.2) | copy-start | bytes 4030468
  62.6 6.6 %copy-start.28 = (bf16[2,80,960]{2,1,0:T(8,128)(2,1)}, bf16[2,80,960]{2,1,0:T(8,128)(2,1)S(1)}, u32[]{:S(2)}) copy-start(bf16[2,80,960]{2,1,0:T(8,128)(2,1)S(1)} %collective-permute-done.4) | copy-start | bytes 921604
  64.0 5.3 %copy-start.30 = (bf16[2,80,960]{2,1,0:T(8,128)(2,1)}, bf16[2,80,960]{2,1,0:T(8,128)(2,1)S(1)}, u32[]{:S(2)}) copy-start(bf16[2,80,960]{2,1,0:T(8,128)(2,1)S(1)} %collective-permute-done.3) | copy-start | bytes 921604
  64.2 20.9 %collective-permute-start.6 = (bf16[4,80,960]{2,1,0:T(8,128)(2,1)S(1)}, bf16[4,80,960]{2,1,0:T(8,128)(2,1)S(1)}, u32[]{:S(2)}, u32[]{:S(2)}) collective-permute-start(bf16[4,80,960]{2,1,0:T(8,128)(2,1)S(1)} %pad_maximum_fusion.3), channel_id=1, source_target_pairs={{0,4},{4,0},{8,12},{12,8},{16,20},{20,16},{24,28},{28,24},{1,5},{5... | collective-permute-start | bytes 1843208 | tf_op jit(solution)/shard_map/ppermute | solution.py:46
  66.6 18.5 %collective-permute-start.5 = (bf16[4,80,960]{2,1,0:T(8,128)(2,1)S(1)}, bf16[4,80,960]{2,1,0:T(8,128)(2,1)S(1)}, u32[]{:S(2)}, u32[]{:S(2)}) collective-permute-start(bf16[4,80,960]{2,1,0:T(8,128)(2,1)S(1)} %pad_maximum_fusion.2), channel_id=1, source_target_pairs={{0,2},{1,3},{2,0},{3,1},{4,6},{5,7},{6,4},{7,5},{8,10},{9,11},{10,... | collective-permute-start | bytes 1843208 | tf_op jit(solution)/shard_map/ppermute | solution.py:46
  86.3 7.3 %copy-start.16 = (bf16[8,80,960]{2,1,0:T(8,128)(2,1)}, bf16[8,80,960]{2,1,0:T(8,128)(2,1)S(1)}, u32[]{:S(2)}) copy-start(bf16[8,80,960]{2,1,0:T(8,128)(2,1)S(1)} %pad_maximum_fusion.mine0) | copy-start | bytes 3686404
  87.6 3.2 collective-permute-start.8
  87.6 5.9 %collective-permute-start.7 = (bf16[8,80,960]{2,1,0:T(8,128)(2,1)S(1)}, bf16[8,80,960]{2,1,0:T(8,128)(2,1)}, u32[]{:S(2)}, u32[]{:S(2)}) collective-permute-start(bf16[8,80,960]{2,1,0:T(8,128)(2,1)S(1)} %pad_maximum_fusion.mine0), channel_id=1, source_target_pairs={{0,1},{1,0},{2,3},{3,2},{4,5},{5,4},{6,7},{7,6},{8,9},{9,8},{10,11... | collective-permute-start | bytes 3686408 | tf_op jit(solution)/shard_map/ppermute | solution.py:46
  99.5 43.2 %all-to-all-start.2 = ((bf16[4,256,960]{1,2,0:T(8,128)(2,1)}), bf16[4,256,960]{1,2,0:T(8,128)(2,1)S(1)}, u32[]{:S(2)}, u32[]{:S(2)}) async-start(bf16[4,256,960]{1,2,0:T(8,128)(2,1)} %param.10), calls=%async_computation.2 | async-start | bytes 3932160 | tf_op jit(solution)/shard_map/all_to_all | solution.py:279
  186.8 5.1 %collective-permute-start.9 = (bf16[2,8,80,960]{3,2,1,0:T(8,128)(2,1)}, bf16[2,8,80,960]{3,2,1,0:T(8,128)(2,1)S(1)}, u32[]{:S(2)}, u32[]{:S(2)}) collective-permute-start(bf16[2,8,80,960]{3,2,1,0:T(8,128)(2,1)} %bitcast.333), channel_id=1, source_target_pairs={{0,1},{1,0},{2,3},{3,2},{4,5},{5,4},{6,7},{7,6},{8,9},{9,8},{10,11... | collective-permute-start | bytes 7372808 | tf_op jit(solution)/shard_map/ppermute | solution.py:46
  193.5 47.7 %all-to-all-start.3 = ((bf16[4,256,960]{1,2,0:T(8,128)(2,1)}), bf16[4,256,960]{1,2,0:T(8,128)(2,1)S(1)}, u32[]{:S(2)}, u32[]{:S(2)}) async-start(bf16[4,256,960]{1,2,0:T(8,128)(2,1)} %bitcast.297), calls=%async_computation.3 | async-start | bytes 3932160 | tf_op jit(solution)/shard_map/all_to_all | solution.py:279
  203.2 38.0 %collective-permute-start.10 = (bf16[4,80,960]{2,1,0:T(8,128)(2,1)}, bf16[4,80,960]{2,1,0:T(8,128)(2,1)}, u32[]{:S(2)}, u32[]{:S(2)}) collective-permute-start(bf16[4,80,960]{2,1,0:T(8,128)(2,1)} %fusion.4), channel_id=1, source_target_pairs={{0,2},{1,3},{2,0},{3,1},{4,6},{5,7},{6,4},{7,5},{8,10},{9,11},{10,... | collective-permute-start | bytes 1843208 | tf_op jit(solution)/shard_map/ppermute | solution.py:46
  205.2 36.0 %collective-permute-start.11 = (bf16[4,80,960]{2,1,0:T(8,128)(2,1)}, bf16[4,80,960]{2,1,0:T(8,128)(2,1)}, u32[]{:S(2)}, u32[]{:S(2)}) collective-permute-start(bf16[4,80,960]{2,1,0:T(8,128)(2,1)} %bitcast.22), channel_id=1, source_target_pairs={{0,4},{4,0},{8,12},{12,8},{16,20},{20,16},{24,28},{28,24},{1,5},{5... | collective-permute-start | bytes 1843208 | tf_op jit(solution)/shard_map/ppermute | solution.py:46
  241.2 8.9 %collective-permute-start.12 = (bf16[2,8,160,960]{3,2,1,0:T(8,128)(2,1)}, bf16[2,8,160,960]{3,2,1,0:T(8,128)(2,1)S(1)}, u32[]{:S(2)}, u32[]{:S(2)}) collective-permute-start(bf16[2,8,160,960]{3,2,1,0:T(8,128)(2,1)} %get-tuple-element.151), channel_id=1, source_target_pairs={{0,1},{1,0},{2,3},{3,2},{4,5},{5,4},{6,7},{7,6},{8,9},{9,8},{10,11... | collective-permute-start | bytes 14745608 | tf_op jit(solution)/shard_map/ppermute | solution.py:46
  245.1 5.9 %copy-start.2 = (bf16[1,8,160,960]{3,2,1,0:T(8,128)(2,1)}, bf16[1,8,160,960]{3,2,1,0:T(8,128)(2,1)S(1)}, u32[]{:S(2)}) copy-start(bf16[1,8,160,960]{3,2,1,0:T(8,128)(2,1)S(1)} %get-tuple-element.223) | copy-start | bytes 7372804
  245.1 7.9 %copy-start.1 = (bf16[1,8,160,960]{3,2,1,0:T(8,128)(2,1)}, bf16[1,8,160,960]{3,2,1,0:T(8,128)(2,1)S(1)}, u32[]{:S(2)}) copy-start(bf16[1,8,160,960]{3,2,1,0:T(8,128)(2,1)S(1)} %get-tuple-element.222) | copy-start | bytes 7372804
  254.7 38.1 %collective-permute-start.13 = (bf16[4,160,960]{2,1,0:T(8,128)(2,1)}, bf16[4,160,960]{2,1,0:T(8,128)(2,1)}, u32[]{:S(2)}, u32[]{:S(2)}) collective-permute-start(bf16[4,160,960]{2,1,0:T(8,128)(2,1)} %fusion.3), channel_id=1, source_target_pairs={{0,2},{1,3},{2,0},{3,1},{4,6},{5,7},{6,4},{7,5},{8,10},{9,11},{10,... | collective-permute-start | bytes 3686408 | tf_op jit(solution)/shard_map/ppermute | solution.py:46
  254.8 38.1 %collective-permute-start.14 = (bf16[4,160,960]{2,1,0:T(8,128)(2,1)}, bf16[4,160,960]{2,1,0:T(8,128)(2,1)}, u32[]{:S(2)}, u32[]{:S(2)}) collective-permute-start(bf16[4,160,960]{2,1,0:T(8,128)(2,1)} %bitcast.29), channel_id=1, source_target_pairs={{0,4},{4,0},{8,12},{12,8},{16,20},{20,16},{24,28},{28,24},{1,5},{5... | collective-permute-start | bytes 3686408 | tf_op jit(solution)/shard_map/ppermute | solution.py:46
  257.1 35.7 %collective-permute-start.15 = (bf16[2,80,960]{2,1,0:T(8,128)(2,1)}, bf16[2,80,960]{2,1,0:T(8,128)(2,1)S(1)}, u32[]{:S(2)}, u32[]{:S(2)}) collective-permute-start(bf16[2,80,960]{2,1,0:T(8,128)(2,1)} %fusion.16), channel_id=1, source_target_pairs={{0,4},{4,0},{8,12},{12,8},{16,20},{20,16},{24,28},{28,24},{1,5},{5... | collective-permute-start | bytes 921608 | tf_op jit(solution)/shard_map/ppermute | solution.py:46
  260.8 32.0 %collective-permute-start.16 = (bf16[2,80,960]{2,1,0:T(8,128)(2,1)}, bf16[2,80,960]{2,1,0:T(8,128)(2,1)S(1)}, u32[]{:S(2)}, u32[]{:S(2)}) collective-permute-start(bf16[2,80,960]{2,1,0:T(8,128)(2,1)} %fusion.17), channel_id=1, source_target_pairs={{0,2},{1,3},{2,0},{3,1},{4,6},{5,7},{6,4},{7,5},{8,10},{9,11},{10,... | collective-permute-start | bytes 921608 | tf_op jit(solution)/shard_map/ppermute | solution.py:46
  292.8 6.5 %copy-start.31 = (bf16[2,80,960]{2,1,0:T(8,128)(2,1)}, bf16[2,80,960]{2,1,0:T(8,128)(2,1)S(1)}, u32[]{:S(2)}) copy-start(bf16[2,80,960]{2,1,0:T(8,128)(2,1)S(1)} %collective-permute-done.15) | copy-start | bytes 921604
  292.8 6.5 %copy-start.34 = (bf16[2,80,960]{2,1,0:T(8,128)(2,1)}, bf16[2,80,960]{2,1,0:T(8,128)(2,1)S(1)}, u32[]{:S(2)}) copy-start(bf16[2,80,960]{2,1,0:T(8,128)(2,1)S(1)} %collective-permute-done.16) | copy-start | bytes 921604
  302.0 28.0 %collective-permute-start.17 = (bf16[2,160,960]{2,1,0:T(8,128)(2,1)}, bf16[2,160,960]{2,1,0:T(8,128)(2,1)S(1)}, u32[]{:S(2)}, u32[]{:S(2)}) collective-permute-start(bf16[2,160,960]{2,1,0:T(8,128)(2,1)} %fusion.5), channel_id=1, source_target_pairs={{0,4},{4,0},{8,12},{12,8},{16,20},{20,16},{24,28},{28,24},{1,5},{5... | collective-permute-start | bytes 1843208 | tf_op jit(solution)/shard_map/ppermute | solution.py:46
  302.3 27.7 %collective-permute-start.18 = (bf16[2,160,960]{2,1,0:T(8,128)(2,1)}, bf16[2,160,960]{2,1,0:T(8,128)(2,1)}, u32[]{:S(2)}, u32[]{:S(2)}) collective-permute-start(bf16[2,160,960]{2,1,0:T(8,128)(2,1)} %fusion.6), channel_id=1, source_target_pairs={{0,2},{1,3},{2,0},{3,1},{4,6},{5,7},{6,4},{7,5},{8,10},{9,11},{10,... | collective-permute-start | bytes 1843208 | tf_op jit(solution)/shard_map/ppermute | solution.py:46
  303.9 26.0 %collective-permute-start.19 = (bf16[1,80,960]{2,1,0:T(8,128)(2,1)}, bf16[1,80,960]{2,1,0:T(8,128)(2,1)}, u32[]{:S(2)}, u32[]{:S(2)}) collective-permute-start(bf16[1,80,960]{2,1,0:T(8,128)(2,1)} %fusion.30), channel_id=1, source_target_pairs={{0,8},{4,12},{8,0},{12,4},{16,24},{20,28},{24,16},{28,20},{1,9},{5... | collective-permute-start | bytes 460808 | tf_op jit(solution)/shard_map/ppermute | solution.py:46
  305.3 24.7 %collective-permute-start.20 = (bf16[1,80,960]{2,1,0:T(8,128)(2,1)}, bf16[1,80,960]{2,1,0:T(8,128)(2,1)}, u32[]{:S(2)}, u32[]{:S(2)}) collective-permute-start(bf16[1,80,960]{2,1,0:T(8,128)(2,1)} %fusion.27), channel_id=1, source_target_pairs={{0,8},{4,12},{8,0},{12,4},{16,24},{20,28},{24,16},{28,20},{1,9},{5... | collective-permute-start | bytes 460808 | tf_op jit(solution)/shard_map/ppermute | solution.py:46
  330.0 4.6 %copy-start.22 = (bf16[2,160,960]{2,1,0:T(8,128)(2,1)}, bf16[2,160,960]{2,1,0:T(8,128)(2,1)S(1)}, u32[]{:S(2)}) copy-start(bf16[2,160,960]{2,1,0:T(8,128)(2,1)S(1)} %collective-permute-done.17) | copy-start | bytes 1843204
  330.0 4.6 %copy-start.32 = (bf16[2,80,960]{2,1,0:T(8,128)(2,1)S(1)}, bf16[2,80,960]{2,1,0:T(8,128)(2,1)}, u32[]{:S(2)}) copy-start(bf16[2,80,960]{2,1,0:T(8,128)(2,1)} %copy-done.31) | copy-start | bytes 921604
  336.9 19.4 %collective-permute-start.21 = (bf16[1,160,960]{2,1,0:T(8,128)(2,1)}, bf16[1,160,960]{2,1,0:T(8,128)(2,1)S(1)}, u32[]{:S(2)}, u32[]{:S(2)}) collective-permute-start(bf16[1,160,960]{2,1,0:T(8,128)(2,1)} %fusion.15), channel_id=1, source_target_pairs={{0,8},{4,12},{8,0},{12,4},{16,24},{20,28},{24,16},{28,20},{1,9},{5... | collective-permute-start | bytes 921608 | tf_op jit(solution)/shard_map/ppermute | solution.py:46
  338.2 18.1 %collective-permute-start.22 = (bf16[1,160,960]{2,1,0:T(8,128)(2,1)}, bf16[1,160,960]{2,1,0:T(8,128)(2,1)S(1)}, u32[]{:S(2)}, u32[]{:S(2)}) collective-permute-start(bf16[1,160,960]{2,1,0:T(8,128)(2,1)} %fusion.13), channel_id=1, source_target_pairs={{0,8},{4,12},{8,0},{12,4},{16,24},{20,28},{24,16},{28,20},{1,9},{5... | collective-permute-start | bytes 921608 | tf_op jit(solution)/shard_map/ppermute | solution.py:46
  338.9 17.4 %collective-permute-start.23 = (bf16[80,960]{1,0:T(8,128)(2,1)}, bf16[80,960]{1,0:T(8,128)(2,1)S(1)}, u32[]{:S(2)}, u32[]{:S(2)}) collective-permute-start(bf16[80,960]{1,0:T(8,128)(2,1)} %fusion.40), channel_id=1, source_target_pairs={{0,16},{4,20},{8,24},{12,28},{16,0},{20,4},{24,8},{28,12},{1,17},{... | collective-permute-start | bytes 460808 | tf_op jit(solution)/shard_map/ppermute | solution.py:46
  360.8 15.2 %collective-permute-start.24 = (bf16[2,8,80,960]{3,2,1,0:T(8,128)(2,1)}, bf16[2,8,80,960]{3,2,1,0:T(8,128)(2,1)}, u32[]{:S(2)}, u32[]{:S(2)}) collective-permute-start(bf16[2,8,80,960]{3,2,1,0:T(8,128)(2,1)} %bitcast.58), channel_id=1, source_target_pairs={{0,1},{1,0},{2,3},{3,2},{4,5},{5,4},{6,7},{7,6},{8,9},{9,8},{10,11... | collective-permute-start | bytes 7372808 | tf_op jit(solution)/shard_map/ppermute | solution.py:46
  361.5 12.7 %slice-start = ((s8[5242880]{0:T(1024)(128)(4,1)}), s8[1048576]{0:T(1024)(128)(4,1)S(1)}, s32[]{:S(2)}) async-start(s8[5242880]{0:T(1024)(128)(4,1)} %bitcast.284), calls=%async_computation.6 | async-start | bytes 2097152
  369.1 5.0 %slice-start.1 = ((s8[5242880]{0:T(1024)(128)(4,1)}), s8[4194304]{0:T(1024)(128)(4,1)S(1)}, s32[]{:S(2)}) async-start(s8[5242880]{0:T(1024)(128)(4,1)} %bitcast.284), calls=%async_computation.7 | async-start | bytes 8388608
  369.2 6.9 %collective-permute-start.25 = (f32[4,960]{1,0:T(4,128)S(1)}, f32[4,960]{1,0:T(4,128)S(1)}, u32[]{:S(2)}, u32[]{:S(2)}) collective-permute-start(f32[4,960]{1,0:T(4,128)S(1)} %pad_maximum_fusion.9), channel_id=1, source_target_pairs={{0,16},{4,20},{8,24},{12,28},{16,0},{20,4},{24,8},{28,12},{1,17},{... | collective-permute-start | bytes 46088 | tf_op jit(solution)/shard_map/ppermute | solution.py:46
  374.5 6.5 %copy-start.18 = (bf16[8,1,80,960]{3,2,1,0:T(8,128)(2,1)}, bf16[8,1,80,960]{3,2,1,0:T(8,128)(2,1)S(1)}, u32[]{:S(2)}) copy-start(bf16[8,1,80,960]{3,2,1,0:T(8,128)(2,1)S(1)} %get-tuple-element.221) | copy-start | bytes 3686404
  379.4 19.5 %collective-permute-start.27 = (bf16[4,80,960]{2,1,0:T(8,128)(2,1)}, bf16[4,80,960]{2,1,0:T(8,128)(2,1)}, u32[]{:S(2)}, u32[]{:S(2)}) collective-permute-start(bf16[4,80,960]{2,1,0:T(8,128)(2,1)} %bitcast.64), channel_id=1, source_target_pairs={{0,8},{4,12},{8,0},{12,4},{16,24},{20,28},{24,16},{28,20},{1,9},{5... | collective-permute-start | bytes 1843208 | tf_op jit(solution)/shard_map/ppermute | solution.py:46
  382.0 16.9 %collective-permute-start.26 = (bf16[4,80,960]{2,1,0:T(8,128)(2,1)}, bf16[4,80,960]{2,1,0:T(8,128)(2,1)}, u32[]{:S(2)}, u32[]{:S(2)}) collective-permute-start(bf16[4,80,960]{2,1,0:T(8,128)(2,1)} %bitcast.61), channel_id=1, source_target_pairs={{0,4},{4,0},{8,12},{12,8},{16,20},{20,16},{24,28},{28,24},{1,5},{5... | collective-permute-start | bytes 1843208 | tf_op jit(solution)/shard_map/ppermute | solution.py:46
  384.9 5.3 %copy-start.23 = (bf16[2,160,960]{2,1,0:T(8,128)(2,1)S(1)}, bf16[2,160,960]{2,1,0:T(8,128)(2,1)}, u32[]{:S(2)}) copy-start(bf16[2,160,960]{2,1,0:T(8,128)(2,1)} %copy-done.22) | copy-start | bytes 1843204
  384.9 5.3 %copy-start.27 = (bf16[1,160,960]{2,1,0:T(8,128)(2,1)S(1)}, bf16[1,160,960]{2,1,0:T(8,128)(2,1)}, u32[]{:S(2)}) copy-start(bf16[1,160,960]{2,1,0:T(8,128)(2,1)} %copy-done.26) | copy-start | bytes 921604
  384.9 48.4 %all-to-all-start.4 = ((bf16[4,256,960]{1,2,0:T(8,128)(2,1)}), bf16[4,256,960]{1,2,0:T(8,128)(2,1)}, u32[]{:S(2)}, u32[]{:S(2)}) async-start(bf16[4,256,960]{1,2,0:T(8,128)(2,1)} %bitcast.295), calls=%async_computation.4 | async-start | bytes 3932160 | tf_op jit(solution)/shard_map/all_to_all | solution.py:279
  389.5 9.4 %copy-start.13 = (bf16[1,8,80,960]{3,2,1,0:T(8,128)(2,1)S(1)}, bf16[1,8,80,960]{3,2,1,0:T(8,128)(2,1)}, u32[]{:S(2)}) copy-start(bf16[1,8,80,960]{3,2,1,0:T(8,128)(2,1)} %copy-done.12) | copy-start | bytes 3686404
  389.5 9.4 %collective-permute-start.28 = (f32[4,960]{1,0:T(4,128)S(1)}, f32[4,960]{1,0:T(4,128)S(1)}, u32[]{:S(2)}, u32[]{:S(2)}) collective-permute-start(f32[4,960]{1,0:T(4,128)S(1)} %fusion.44), channel_id=1, source_target_pairs={{0,8},{4,12},{8,0},{12,4},{16,24},{20,28},{24,16},{28,20},{1,9},{5... | collective-permute-start | bytes 46088 | tf_op jit(solution)/shard_map/ppermute | solution.py:46
  392.4 10.2 %copy-start.15 = (bf16[1,8,80,960]{3,2,1,0:T(8,128)(2,1)S(1)}, bf16[1,8,80,960]{3,2,1,0:T(8,128)(2,1)}, u32[]{:S(2)}) copy-start(bf16[1,8,80,960]{3,2,1,0:T(8,128)(2,1)} %copy-done.14) | copy-start | bytes 3686404
  392.4 29.4 %collective-permute-start.37 = (bf16[160,960]{1,0:T(8,128)(2,1)S(1)}, bf16[160,960]{1,0:T(8,128)(2,1)S(1)}, u32[]{:S(2)}, u32[]{:S(2)}) collective-permute-start(bf16[160,960]{1,0:T(8,128)(2,1)S(1)} %fusion.18), channel_id=1, source_target_pairs={{0,16},{4,20},{8,24},{12,28},{16,0},{20,4},{24,8},{28,12},{1,17},{... | collective-permute-start | bytes 921608 | tf_op jit(solution)/shard_map/ppermute | solution.py:46
  399.0 5.5 %copy-start.33 = (bf16[2,80,960]{2,1,0:T(8,128)(2,1)S(1)}, bf16[2,80,960]{2,1,0:T(8,128)(2,1)}, u32[]{:S(2)}) copy-start(bf16[2,80,960]{2,1,0:T(8,128)(2,1)} %copy-done.31) | copy-start | bytes 921604
  399.0 5.5 %copy-start.36 = (bf16[2,80,960]{2,1,0:T(8,128)(2,1)S(1)}, bf16[2,80,960]{2,1,0:T(8,128)(2,1)}, u32[]{:S(2)}) copy-start(bf16[2,80,960]{2,1,0:T(8,128)(2,1)} %copy-done.34) | copy-start | bytes 921604
  400.3 10.3 %collective-permute-start.30 = (bf16[2,80,960]{2,1,0:T(8,128)(2,1)S(1)}, bf16[2,80,960]{2,1,0:T(8,128)(2,1)S(1)}, u32[]{:S(2)}, u32[]{:S(2)}) collective-permute-start(bf16[2,80,960]{2,1,0:T(8,128)(2,1)S(1)} %bitcast.320), channel_id=1, source_target_pairs={{0,4},{4,0},{8,12},{12,8},{16,20},{20,16},{24,28},{28,24},{1,5},{5... | collective-permute-start | bytes 921608 | tf_op jit(solution)/shard_map/ppermute | solution.py:46
  403.8 13.5 %collective-permute-start.29 = (bf16[2,80,960]{2,1,0:T(8,128)(2,1)S(1)}, bf16[2,80,960]{2,1,0:T(8,128)(2,1)S(1)}, u32[]{:S(2)}, u32[]{:S(2)}) collective-permute-start(bf16[2,80,960]{2,1,0:T(8,128)(2,1)S(1)} %bitcast.321), channel_id=1, source_target_pairs={{0,8},{4,12},{8,0},{12,4},{16,24},{20,28},{24,16},{28,20},{1,9},{5... | collective-permute-start | bytes 921608 | tf_op jit(solution)/shard_map/ppermute | solution.py:46
  403.9 6.6 %collective-permute-start.31 = (f32[4,960]{1,0:T(4,128)S(1)}, f32[4,960]{1,0:T(4,128)S(1)}, u32[]{:S(2)}, u32[]{:S(2)}) collective-permute-start(f32[4,960]{1,0:T(4,128)S(1)} %fusion.62), channel_id=1, source_target_pairs={{0,4},{4,0},{8,12},{12,8},{16,20},{20,16},{24,28},{28,24},{1,5},{5... | collective-permute-start | bytes 46088 | tf_op jit(solution)/shard_map/ppermute | solution.py:46
  417.3 7.6 %collective-permute-start.34 = (f32[4,960]{1,0:T(4,128)S(1)}, f32[4,960]{1,0:T(4,128)S(1)}, u32[]{:S(2)}, u32[]{:S(2)}) collective-permute-start(f32[4,960]{1,0:T(4,128)S(1)} %add.675), channel_id=1, source_target_pairs={{0,2},{1,3},{2,0},{3,1},{4,6},{5,7},{6,4},{7,5},{8,10},{9,11},{10,... | collective-permute-start | bytes 46088 | tf_op jit(solution)/shard_map/ppermute | solution.py:46
  419.7 7.1 %collective-permute-start.33 = (bf16[1,80,960]{2,1,0:T(8,128)(2,1)S(1)}, bf16[1,80,960]{2,1,0:T(8,128)(2,1)S(1)}, u32[]{:S(2)}, u32[]{:S(2)}) collective-permute-start(bf16[1,80,960]{2,1,0:T(8,128)(2,1)S(1)} %get-tuple-element.218), channel_id=1, source_target_pairs={{0,2},{1,3},{2,0},{3,1},{4,6},{5,7},{6,4},{7,5},{8,10},{9,11},{10,... | collective-permute-start | bytes 460808 | tf_op jit(solution)/shard_map/ppermute | solution.py:46
  420.7 7.9 %collective-permute-start.32 = (bf16[1,80,960]{2,1,0:T(8,128)(2,1)S(1)}, bf16[1,80,960]{2,1,0:T(8,128)(2,1)S(1)}, u32[]{:S(2)}, u32[]{:S(2)}) collective-permute-start(bf16[1,80,960]{2,1,0:T(8,128)(2,1)S(1)} %get-tuple-element.219), channel_id=1, source_target_pairs={{0,2},{1,3},{2,0},{3,1},{4,6},{5,7},{6,4},{7,5},{8,10},{9,11},{10,... | collective-permute-start | bytes 460808 | tf_op jit(solution)/shard_map/ppermute | solution.py:46
  428.6 1.6 collective-permute-start.35
  430.1 10.4 %collective-permute-start.36 = (bf16[80,960]{1,0:T(8,128)(2,1)S(1)}, bf16[80,960]{1,0:T(8,128)(2,1)S(1)}, u32[]{:S(2)}, u32[]{:S(2)}) collective-permute-start(bf16[80,960]{1,0:T(8,128)(2,1)S(1)} %get-tuple-element.216), channel_id=1, source_target_pairs={{0,16},{4,20},{8,24},{12,28},{16,0},{20,4},{24,8},{28,12},{1,17},{... | collective-permute-start | bytes 460808 | tf_op jit(solution)/shard_map/ppermute | solution.py:46
  (23 other events, 66.8 us)
Sparse Core Ops, SparseCore 0:
  11.5 143.0 all-gather.2

commit v3 on v2

--- a/solution.py
+++ b/solution.py
@@ -20,7 +20,7 @@
 TILE = 256
 WIDE = 768
 SLAB = 1280
-SPLIT = ((0, 2), (2, 2), (4, 1))
+SPLIT = ((0, 3), (3, 2))
 CHUNK = 640
 TILES = ((0, 256, 512), (256, 512, 768), (512, ROWS, 768))
 NEG = -1e30
@@ -426,9 +426,16 @@
     return ref[start // each : (start + size) // each].reshape(size, D)
 
 
+def spread(compact, pick_ref, out_ref):
+    size = out_ref.shape[2]
+    for block in range(out_ref.shape[0]):
+        places = pick_ref[:, block * size : (block + 1) * size]
+        out_ref[block] = tn(compact, places).astype(BF16)
+
+
 def feed_kernel(
-    h1_ref, x_ref, t_ref, aux_ref, gain_ref, router_ref, wg_ref, wu_ref, wd_ref,
-    n2_ref, g_ref, u_ref, hid_ref, y_ref, diff_ref, cols_ref, sums_ref, d_ffn_ref,
+    h1_ref, x_ref, t_ref, aux_ref, gain_ref, router_ref, pick_ref, wg_ref, wu_ref, wd_ref,
+    n2_ref, g_ref, u_ref, hid_ref, out_ref, diff_ref, cols_ref, sums_ref, d_ffn_ref,
 ):
     step = pl.program_id(0)
 
@@ -456,7 +463,7 @@
         prob = jax.nn.sigmoid(jnp.sum(x * router_ref[...], axis=-1, keepdims=True))
         mix = live * prob
         result = x + mix * branch
-        y_ref[...] = result.astype(BF16)
+        spread(result.astype(BF16), pick_ref, out_ref)
         diff = valid * (result - t_ref[...].astype(F32))
         d_logit = live * jnp.sum(diff * branch, axis=-1, keepdims=True) * prob * (1.0 - prob)
         diff_ref[...] = diff
@@ -473,7 +480,7 @@
         )
 
 
-def feed(h1, x, t, aux, gain, router, packs):
+def feed(h1, x, t, aux, gain, router, pick, packs, blocks):
     whole = lambda *shape: pl.BlockSpec(shape, lambda j: (0,) * len(shape))
     fixed = lambda *shape: pl.BlockSpec(
         shape, lambda j: (0,) * len(shape), pipeline_mode=pl.Buffered(1)
@@ -488,6 +495,7 @@
             fixed(ROWS, 8),
             fixed(1, D),
             fixed(1, D),
+            fixed(*pick.shape),
             *feed_specs(packs),
         ],
         out_specs=[
@@ -495,7 +503,7 @@
             pl.BlockSpec((ROWS, SLAB), lambda j: (0, j)),
             pl.BlockSpec((ROWS, SLAB), lambda j: (0, j)),
             pl.BlockSpec((ROWS, SLAB), lambda j: (0, j)),
-            whole(ROWS, D),
+            whole(*blocks),
             whole(ROWS, D),
             whole(ROWS, 128),
             whole(8, D),
@@ -506,7 +514,7 @@
             jax.ShapeDtypeStruct((ROWS, FF), BF16),
             jax.ShapeDtypeStruct((ROWS, FF), BF16),
             jax.ShapeDtypeStruct((ROWS, FF), BF16),
-            jax.ShapeDtypeStruct((ROWS, D), BF16),
+            jax.ShapeDtypeStruct(blocks, BF16),
             jax.ShapeDtypeStruct((ROWS, D), F32),
             jax.ShapeDtypeStruct((ROWS, 128), F32),
             jax.ShapeDtypeStruct((8, D), F32),
@@ -514,7 +522,7 @@
         ],
         compiler_params=pltpu.CompilerParams(vmem_limit_bytes=VMEM_LIMIT),
         name="feed",
-    )(h1, x, t, aux, gain, router, *packs)
+    )(h1, x, t, aux, gain, router, pick, *packs)
 
 
 def shared_out(core_ref, total, refs, rows):
@@ -655,11 +663,15 @@
 
 
 def attend_back_kernel(
-    first, final, da_ref, part_ref, x_ref, n1_ref, gain_ref, cos_ref, sin_ref, aux_ref, row_ref,
+    first, final, da_ref, n1_ref, cos_ref, sin_ref, aux_ref, row_ref,
     q_ref, k_ref, v_ref, o_ref, l_ref, wq_ref, wk_ref, wv_ref, wo0_ref, wo1_ref, wo2_ref,
     *rest,
 ):
-    pack_ref, dn1, grad_ref, sums_ref, bias, wide_q, wide_do, dq, stage, sems = rest[-10:]
+    *rest, bias, wide_q, wide_do, dq, stage, sems = rest
+    if final:
+        *rest, part_ref, x_ref, gain_ref, pick_ref, pack_ref, dn1, grad_ref, sums_ref = rest
+    else:
+        *rest, pack_ref, dn1 = rest
     group = pl.program_id(0)
     per = D // KV_HEADS
 
@@ -668,7 +680,7 @@
         bias[...] = jnp.where(aux_ref[:, 3:4] <= row_ref[0:1, :], 0.0, NEG)
         wide_q[...] = jnp.zeros_like(wide_q)
         wide_do[...] = jnp.zeros_like(wide_do)
-        dn1[...] = rest[0][...] if len(rest) > 10 else jnp.zeros_like(dn1)
+        dn1[...] = rest[0][...] if rest else jnp.zeros_like(dn1)
 
     w_out = jnp.concatenate([wo0_ref[...], wo1_ref[...], wo2_ref[...]], axis=0)
     d_heads = nt(da_ref[...], w_out)
@@ -741,10 +753,10 @@
         )
         scaled = d_norm * gain_ref[...]
         d_x = inv * scaled - x * inv**3 * jnp.mean(scaled * x, axis=-1, keepdims=True)
-        grad_ref[...] = (part_ref[...] + d_x).astype(BF16)
-
-
-def attend_back(first, count, given, so_far):
+        spread((part_ref[...] + d_x).astype(BF16), pick_ref, grad_ref)
+
+
+def attend_back(first, count, given, so_far, closing, blocks):
     whole = lambda *shape: pl.BlockSpec(shape, lambda g: (0,) * len(shape))
     fixed = lambda *shape: pl.BlockSpec(
         shape, lambda g: (0,) * len(shape), pipeline_mode=pl.Buffered(1)
@@ -758,9 +770,6 @@
         in_specs=[
             fixed(ROWS, D),
             fixed(ROWS, D),
-            fixed(ROWS, D),
-            fixed(ROWS, D),
-            fixed(1, D),
             fixed(ROWS, HEAD),
             fixed(ROWS, HEAD),
             fixed(ROWS, 8),
@@ -772,18 +781,21 @@
             pl.BlockSpec((1, 8, WIDE), lambda g: (first + g, 0, 0)),
             *weight_specs(first),
             *([fixed(ROWS, D), kept] if so_far else []),
+            *([fixed(*c.shape) for c in closing] if final else []),
         ],
         out_specs=[
             kept,
             whole(ROWS, D),
-            whole(ROWS, D),
-            whole(8, D),
+            *([whole(*blocks), whole(8, D)] if final else []),
         ],
         out_shape=[
             jax.ShapeDtypeStruct((QKV_COLS + D, D), BF16),
             jax.ShapeDtypeStruct((ROWS, D), F32),
-            jax.ShapeDtypeStruct((ROWS, D), BF16),
-            jax.ShapeDtypeStruct((8, D), F32),
+            *(
+                [jax.ShapeDtypeStruct(blocks, BF16), jax.ShapeDtypeStruct((8, D), F32)]
+                if final
+                else []
+            ),
         ],
         scratch_shapes=[
             pltpu.VMEM((ROWS, WIDE), F32),
@@ -793,10 +805,10 @@
             pltpu.VMEM((2 * (per + HEAD), D), BF16),
             pltpu.SemaphoreType.DMA((4,)),
         ],
-        input_output_aliases={21: 0} if so_far else {},
+        input_output_aliases={18: 0} if so_far else {},
         compiler_params=pltpu.CompilerParams(vmem_limit_bytes=VMEM_LIMIT),
         name="attend_back",
-    )(*given, *so_far)
+    )(*given, *so_far, *(closing if final else ()))
 
 
 def on_device(states, teacher, validity, chosen, attn_pack, gate_up, down_proj, norm_gains, router):
@@ -849,8 +861,18 @@
     row = jnp.pad(row, ((0, 0), (0, WIDE - ROWS)), constant_values=1e6)
     router_row = router[None, :]
 
-    x_seq, pick, cosine, sine, aux, row = wait(
-        [attn_in], x_seq, pick, cosine, sine, aux, row
+
+    x_home = states.astype(F32)
+    still = (chosen == 0)[..., None]
+    valid_home = validity.astype(F32)[..., None]
+    apart = valid_home * (x_home - teacher.astype(F32))
+    energy = 0.5 * jnp.sum(jnp.where(still, apart * apart, 0.0))
+    scalars = jnp.concatenate(
+        [energy[None], jnp.sum(validity).astype(F32)[None], jnp.zeros((D - 2,), F32)]
+    )
+
+    x_seq, pick, cosine, sine, aux, row, scalars = wait(
+        [attn_in], x_seq, pick, cosine, sine, aux, row, scalars
     )
     start(attn_in)
     x_low = dot(pick, x_seq, ((1,), (0,))).astype(BF16)
@@ -864,21 +886,17 @@
 
     n1, q, k, v, o, lse, h1 = attend(x_low, gain_one, cosine, sine, aux, row, w_attn)
     t_low = dot(pick, t_seq, ((1,), (0,))).astype(BF16)
-    n2, g, u, hid, y, diff, cols, sums, d_ffn = feed(
-        h1, x_low, t_low, aux, gain_two, router_row, packs
-    )
-    energy = jnp.sum(sums[1])
-
-    def spread(compact):
-        whole = dot(compact, pick, ((0,), (0,))).astype(BF16)
-        return whole.reshape(width, ctx_count, block_rows).transpose(1, 0, 2)
+    blocks = (ctx_count, width, block_rows)
+    n2, g, u, hid, out_columns, diff, cols, sums, d_ffn = feed(
+        h1, x_low, t_low, aux, gain_two, router_row, pick, packs, blocks
+    )
 
     def to_home(columns):
         return to_sequence(columns.transpose(0, 2, 1))
 
     down = Scatter(*down_grad(hid, d_ffn, core, bits), bits)
     start(down)
-    d_ffn, out_columns = wait([down], d_ffn, spread(y))
+    d_ffn = wait([down], d_ffn)
     out_home = to_home(out_columns)
     d_ffn = start_ahead([down], d_ffn)
     *grad_gu, da, part, two = feed_back(
@@ -890,30 +908,24 @@
     da = wait([wide], da)
     da = start_ahead([wide], da)
 
-    given = (da, part, x_low, n1, gain_one, cosine, sine, aux, row, q, k, v, o, lse)
+    given = (da, n1, cosine, sine, aux, row, q, k, v, o, lse)
     given += (w_attn,) * 6
     so_far = []
     for first, count in SPLIT:
-        grad_attn, dn1, d_states, one = attend_back(first, count, given, so_far)
+        closing = (part, x_low, gain_one, pick)
+        grad_attn, dn1, *ends = attend_back(first, count, given, so_far, closing, blocks)
         if first + count < KV_HEADS:
             dn1 = wait([wide, down], dn1)
             dn1 = start_ahead([wide, down], dn1)
         so_far = [dn1, grad_attn]
-    grad_attn, d_states = wait([wide, down], grad_attn, d_states)
+    columns, one = ends
+    grad_attn = wait([wide, down], grad_attn)
     attn = Scatter(*split_cores(grad_attn, bits), bits, late=True)
-
-    x_home = states.astype(F32)
-    still = (chosen == 0)[..., None]
-    valid_home = validity.astype(F32)[..., None]
-    apart = valid_home * (x_home - teacher.astype(F32))
-    energy = energy + 0.5 * jnp.sum(jnp.where(still, apart * apart, 0.0))
-    scalars = jnp.concatenate(
-        [energy[None], jnp.sum(validity).astype(F32)[None], jnp.zeros((D - 2,), F32)]
-    )
+    scalars = scalars.at[0].add(jnp.sum(sums[1]))
     total = Total(jnp.stack([one[0], two[0], sums[0], scalars], axis=0), bits)
 
     start(attn, wide, down, total)
-    columns = wait([attn, total], spread(d_states))
+    wait([attn, total])
     grad_home = to_home(columns)
     take(wide, down)
     while attn.step < len(bits):

time: 456 us -> 428 us (0.939)
  waiting for transfers between devices: 94.9 us -> 79.6 us
  matrix products: 12.7 us -> 5.39 us
    ppermute x38, waiting for transfers between devices: 79.6 us -> 70 us  [swap(): return lax.ppermute(value, name, pairs)]
    all_gather x1, waiting for transfers between devices: 7.89 us -> 0.01 us  [on_device(): packs = lax.all_gather(feed_rows, ('dp', 'ctx'), axis=0)]
    dot_general x4 -> x2, matrix products: 12.7 us -> 5.39 us  [dot(): lax.dot_general(left, right, (contract, ((), ())), preferred_element_type...]
    convert_element_type x17, other arithmetic: 30.4 us -> 24.4 us  [cut(): self.outs.append(self.choose(half, choice).astype(BF16))]
    unnamed x86 -> x30, local copies, waits for them, and re-layouts: 5.69 us -> 0.22 us
    pallas_call x3 -> x2, Pallas kernels: 62 us -> 56.7 us  [attend_back(): pl.pallas_call(functools.partial(attend_back_kernel, first, final), grid=...]
  transfers between devices with their start and end apart: 44 -> 44, of which waited for: 19 -> 17; matrix products, arithmetic and copies ran while one was open for 16% -> 18% of each run, Pallas kernels for 30% -> 30%
where the time goes in v3:
time: 428 us; the launch traced here: 420 us
  Pallas kernels  162 us (38%)
  waiting for transfers between devices  79.6 us (19%)
  starting transfers between devices  62.8 us (15%)
  other arithmetic  62.6 us (15%)
  local copies, waits for them, and re-layouts  27.7 us (6%)
  between operations  20.2 us (5%)
  matrix products  5.39 us (1%)
    ppermute x38, waiting for transfers between devices, swap(): return lax.ppermute(value, name, pairs)  70 us
    pallas_call x2, Pallas kernels, attend_back(): pl.pallas_call(functools.partial(attend_back_kernel, first, final), grid=...  56.7 us
    ppermute x38, starting transfers between devices, swap(): return lax.ppermute(value, name, pairs)  41.8 us
    pallas_call x1, Pallas kernels, feed_back(): pl.pallas_call(feed_back_kernel, grid=(FF // SLAB,), in_specs=[fixed(ROWS...  34.1 us
    pallas_call x1, Pallas kernels, attend(): pl.pallas_call(attend_kernel, grid=(KV_HEADS,), in_specs=[fixed(ROWS, D),...  30.7 us
    pallas_call x1, Pallas kernels, feed(): pl.pallas_call(feed_kernel, grid=(FF // SLAB,), in_specs=[fixed(ROWS, D),...  26.2 us
    convert_element_type x17, other arithmetic, cut(): self.outs.append(self.choose(half, choice).astype(BF16))  24.4 us
    all_to_all x5, starting transfers between devices, to_sequence(): lax.all_to_all(blocks, 'ctx', split_axis=0, concat_axis=0, tiled=True)  20.9 us
  transfers between devices with their start and end apart: 44, of which 17 were waited for; matrix products, arithmetic and copies ran while one was open for 18% of the time, Pallas kernels for 30%

profile of v3, /device:TPU:0, one launch (start us, length us, event | category | flops | bytes accessed | tf_op | source)
XLA Modules:
  0.0 420.1 jit_solution(4659602862764866242)
XLA Ops:
  7.2 1.9 pad_maximum_fusion.4
  11.1 4.3 %all-to-all-start.1 = ((s32[4,1,256]{2,1,0:T(1,128)}), s32[4,1,256]{2,1,0:T(1,128)S(1)}, u32[]{:S(2)}, u32[]{:S(2)}) async-start(s32[4,1,256]{2,1,0:T(1,128)} %reshape.808), calls=%async_computation.1 | async-start | bytes 8192 | tf_op jit(solution)/shard_map/all_to_all | solution.py:279
  15.4 3.1 collective-permute-start
  19.9 3.8 select_reduce_fusion.1
  24.6 4.6 %all-to-all-start = ((bf16[4,256,960]{1,2,0:T(8,128)(2,1)}), bf16[4,256,960]{1,2,0:T(8,128)(2,1)}, u32[]{:S(2)}, u32[]{:S(2)}) async-start(bf16[4,256,960]{1,2,0:T(8,128)(2,1)} %param.11), calls=%async_computation | async-start | bytes 3932160 | tf_op jit(solution)/shard_map/all_to_all | solution.py:279
  30.8 3.9 collective-permute-start.2
  38.6 2.8 collective-permute-done.2
  41.4 3.2 collective-permute-done.1
  44.6 1.7 collective-permute-start.4
  46.3 1.6 collective-permute-start.3
  49.7 9.6 %all-to-all-done = bf16[4,256,960]{1,2,0:T(8,128)(2,1)} async-done(((bf16[4,256,960]{1,2,0:T(8,128)(2,1)}), bf16[4,256,960]{1,2,0:T(8,128)(2,1)}, u32[]{:S(2)}, u32[]{:S(2)}) %all-to-all-start) | async-done | bytes 1966112 | tf_op jit(solution)/shard_map/all_to_all | solution.py:279
  59.3 1.8 copy.170
  61.1 6.3 %collective-permute-done.4 = bf16[2,80,960]{2,1,0:T(8,128)(2,1)S(1)} collective-permute-done((bf16[2,80,960]{2,1,0:T(8,128)(2,1)S(1)}, bf16[2,80,960]{2,1,0:T(8,128)(2,1)S(1)}, u32[]{:S(2)}, u32[]{:S(2)}) %collective-permute-start.4) | collective-permute-done | bytes 307232 | tf_op jit(solution)/shard_map/ppermute | solution.py:46
  69.5 2.7 convolution_convert_fusion.1.x_ref.rest_3_
  72.2 11.7 %collective-permute-done.6 = bf16[4,80,960]{2,1,0:T(8,128)(2,1)S(1)} collective-permute-done((bf16[4,80,960]{2,1,0:T(8,128)(2,1)S(1)}, bf16[4,80,960]{2,1,0:T(8,128)(2,1)S(1)}, u32[]{:S(2)}, u32[]{:S(2)}) %collective-permute-start.6) | collective-permute-done | bytes 614432 | tf_op jit(solution)/shard_map/ppermute | solution.py:46
  88.8 3.7 collective-permute-done.8.other1
  92.4 2.0 collective-permute-done.7.other0
  94.4 5.9 %order.1 = bf16[2,8,2,80,960]{4,3,2,1,0:T(8,128)(2,1)} custom-call(s32[5]{0:T(128)} %stack.60.own, bf16[8,80,960]{2,1,0:T(8,128)(2,1)} %copy-done.9, bf16[8,80,960]{2,1,0:T(8,128)(2,1)} %collective-permute-done.7.other0, bf16[8,80,960]{2,1,0:T(8,128)(2,1)} %pad_maximum_fusion.1.mine1, bf16[8,80,960]{2,1,0:T(8,128)(2,1)} %collective-permute-done.8.other1), custom_call_target="tpu_custom_call" | custom-call | tf_op jit(solution)/shard_map/order/pallas_call | solution.py:135
  100.4 4.7 %all-to-all-start.2 = ((bf16[4,256,960]{1,2,0:T(8,128)(2,1)}), bf16[4,256,960]{1,2,0:T(8,128)(2,1)}, u32[]{:S(2)}, u32[]{:S(2)}) async-start(bf16[4,256,960]{1,2,0:T(8,128)(2,1)} %param.12), calls=%async_computation.2 | async-start | bytes 3932160 | tf_op jit(solution)/shard_map/all_to_all | solution.py:279
  106.6 30.7 %attend.1 = (bf16[656,960]{1,0:T(8,128)(2,1)}, bf16[15,656,64]{2,1,0:T(8,128)(2,1)}, bf16[5,656,64]{2,1,0:T(8,128)(2,1)}, bf16[5,656,64]{2,1,0:T(8,128)(2,1)}, b...) custom-call(bf16[656,960]{1,0:T(8,128)(2,1)} %convolution_convert_fusion.1.x_ref.rest_3_, ...), custom_call_target="tpu_custom_call" | custom-call | tf_op jit(solution)/shard_map/attend/pallas_call | solution.py:365
  137.3 1.8 copy.171
  139.1 2.7 convolution_convert_fusion.t_ref
  141.8 26.2 %feed.1 = (bf16[656,960]{1,0:T(8,128)(2,1)}, bf16[656,2560]{1,0:T(8,128)(2,1)}, bf16[656,2560]{1,0:T(8,128)(2,1)}, bf16[656,2560]{1,0:T(8,128)(2,1)}, bf16[4,960...) custom-call(f32[656,960]{1,0:T(8,128)} %get-tuple-element.128.h1_ref, ...), custom_call_target="tpu_custom_call" | custom-call | tf_op jit(solution)/shard_map/feed/pallas_call | solution.py:488
  168.0 8.1 %down_grad.1 = (bf16[16,80,960]{2,1,0:T(8,128)(2,1)}, bf16[16,80,960]{2,1,0:T(8,128)(2,1)}) custom-call(bf16[656,2560]{1,0:T(8,128)(2,1)} %get-tuple-element.136.hid_ref, bf16[656,960]{1,0:T(8,128)(2,1)} %get-tuple-element.141.d_ffn_ref, s32[1]{0:T(128)} %bitcast.11.core_ref), custom_call_target="tpu_custom_call" | custom-call | tf_op jit(solution)/shard_map/down_grad/pallas_call | solution.py:552
  176.7 3.6 all-to-all-start.3
  180.3 2.0 fusion.48
  182.3 2.9 fusion.49
  187.8 2.0 collective-permute-start.10
  191.3 34.1 %feed_back.1 = (bf16[2,8,160,960]{3,2,1,0:T(8,128)(2,1)}, bf16[2,8,160,960]{3,2,1,0:T(8,128)(2,1)}, bf16[656,960]{1,0:T(8,128)(2,1)}, f32[656,960]{1,0:T(8,128)}, f32[8,960]{1,0:T(8,128)}) custom-call(f32[656,960]{1,0:T(8,128)} %get-tuple-element.128.h1_ref, bf16[656,960]{1,0:T(8,128)(2,1)} %get-tuple-element.130.n2_ref, ...), custom_call_target="tpu_custom_call" | custom-call | tf_op jit(solution)/shard_map/feed_back/pallas_call | solution.py:625
  225.5 3.1 fusion.45
  228.7 5.7 %collective-permute-done.12 = bf16[2,8,160,960]{3,2,1,0:T(8,128)(2,1)S(1)} collective-permute-done((bf16[2,8,160,960]{3,2,1,0:T(8,128)(2,1)}, bf16[2,8,160,960]{3,2,1,0:T(8,128)(2,1)S(1)}, u32[]{:S(2)}, u32[]{:S(2)}) %collective-permute-start.12) | collective-permute-done | bytes 4915232 | tf_op jit(solution)/shard_map/ppermute | solution.py:46
  235.2 2.1 fusion.3
  237.3 1.6 add_convert_fusion
  239.4 2.1 fusion.16
  243.1 2.1 fusion.17
  245.1 2.0 collective-permute-start.16
  247.1 29.4 %attend_back.2 = (bf16[2560,960]{1,0:T(8,128)(2,1)}, f32[656,960]{1,0:T(8,128)}) custom-call(bf16[656,960]{1,0:T(8,128)(2,1)} %get-tuple-element.154.da_ref, bf16[656,960]{1,0:T(8,128)(2,1)} %get-tuple-element.155.n1_ref, f32[656,64]{1,0:T(8,128)} %get-tuple-element.120.cos_ref, f32[656,64]{1,0:T(8,128)} %get-tuple-element.121.sin_ref, ...), custom_call_target="tpu_custom_call" | custom-call | tf_op jit(solution)/shard_map/attend_back/pallas_call | solution.py:767
  277.1 1.9 fusion.30
  279.0 1.9 fusion.27
  280.9 2.7 fusion.5
  283.6 2.7 fusion.6
  286.7 1.7 collective-permute-start.18
  288.4 1.6 collective-permute-start.19
  290.5 27.3 %attend_back.3 = (bf16[2560,960]{1,0:T(8,128)(2,1)}, f32[656,960]{1,0:T(8,128)}, bf16[4,960,256]{2,1,0:T(8,128)(2,1)}, f32[8,960]{1,0:T(8,128)}) custom-call(bf16[656,960]{1,0:T(8,128)(2,1)} %get-tuple-element.154.da_ref, bf16[656,960]{1,0:T(8,128)(2,1)} %get-tuple-element.155.n1_ref, ...), custom_call_target="tpu_custom_call", output_to_operand_aliasing={{0}: (18, {})} | custom-call | tf_op jit(solution)/shard_map/attend_back/pallas_call | solution.py:767
  317.8 3.6 constant_dynamic-slice_fusion.2
  325.5 3.0 broadcast_select_fusion
  329.2 3.8 all-to-all-start.4
  333.1 2.6 collective-permute-start.22
  337.2 1.6 collective-permute-start.34
  340.8 2.0 constant_dynamic-slice_fusion.1
  342.9 2.0 fusion.47
  348.3 1.8 fusion.41
  351.5 6.9 %collective-permute-done.35 = bf16[1,160,960]{2,1,0:T(8,128)(2,1)S(1)} collective-permute-done((bf16[1,160,960]{2,1,0:T(8,128)(2,1)S(1)}, bf16[1,160,960]{2,1,0:T(8,128)(2,1)S(1)}, u32[]{:S(2)}, u32[]{:S(2)}) %collective-permute-start.35) | collective-permute-done | bytes 307232 | tf_op jit(solution)/shard_map/ppermute | solution.py:46
  358.4 2.3 fusion.18
  360.7 16.8 %collective-permute-done.25 = f32[4,960]{1,0:T(4,128)S(1)} collective-permute-done((f32[4,960]{1,0:T(4,128)S(1)}, f32[4,960]{1,0:T(4,128)S(1)}, u32[]{:S(2)}, u32[]{:S(2)}) %collective-permute-start.25) | collective-permute-done | bytes 15392 | tf_op jit(solution)/shard_map/ppermute | solution.py:46
  377.7 1.6 collective-permute-start.27
  380.2 2.5 fusion.31
  382.7 4.5 %collective-permute-done.28 = f32[4,960]{1,0:T(4,128)S(1)} collective-permute-done((f32[4,960]{1,0:T(4,128)S(1)}, f32[4,960]{1,0:T(4,128)S(1)}, u32[]{:S(2)}, u32[]{:S(2)}) %collective-permute-start.28) | collective-permute-done | bytes 15392 | tf_op jit(solution)/shard_map/ppermute | solution.py:46
  388.3 1.6 collective-permute-start.31
  391.6 1.6 collective-permute-start.29
  393.2 3.2 fusion.7
  396.8 1.8 collective-permute-done.29
  399.9 1.6 collective-permute-start.33
  401.5 4.8 %convert_select_fusion = f32[4,256,960]{1,2,0:T(8,128)} fusion(bf16[4,256,960]{1,2,0:T(8,128)(2,1)S(1)} %all-to-all-done.4, bf16[4,256,960]{1,2,0:T(8,128)(2,1)} %param.12, bf16[4,256,960]{1,2,0:T(8,128)(2,1)} %param.11, f32[4,256]{1,0:T(4,128)S(1)} %get-tuple-element.231, pred[4,256]{1,0:T(4,128)(4,1)S(1)} %broadcast_compare_fusion), kind=kLoop, calls=%fused_computation.2 | loop fusion | flops 5898240 | bytes 9835520 | tf_op jit(solution)/shard_map/jit(_where)/select_n | solution.py:942
  (153 shorter events, 49.2 us)
Async XLA Ops:
  7.2 134.6 %all-gather.3.cloned.1.call-start = ((), (), s32[]{:S(2)}) async-start(), calls=%async_computation.5 | async-start | bytes 16220160 | tf_op jit(solution)/shard_map/all_gather | solution.py:825
  11.1 13.5 %all-to-all-start.1 = ((s32[4,1,256]{2,1,0:T(1,128)}), s32[4,1,256]{2,1,0:T(1,128)S(1)}, u32[]{:S(2)}, u32[]{:S(2)}) async-start(s32[4,1,256]{2,1,0:T(1,128)} %reshape.808), calls=%async_computation.1 | async-start | bytes 8192 | tf_op jit(solution)/shard_map/all_to_all | solution.py:279
  15.4 13.8 %collective-permute-start = (bf16[1,80,960]{2,1,0:T(8,128)(2,1)}, bf16[1,80,960]{2,1,0:T(8,128)(2,1)S(1)}, u32[]{:S(2)}, u32[]{:S(2)}) collective-permute-start(bf16[1,80,960]{2,1,0:T(8,128)(2,1)} %bitcast.298), channel_id=1, source_target_pairs={{0,16},{4,20},{8,24},{12,28},{16,0},{20,4},{24,8},{28,12},{1,17},{... | collective-permute-start | bytes 460808 | tf_op jit(solution)/shard_map/ppermute | solution.py:46
  24.6 6.2 %copy-start.13 = (bf16[960,80]{0,1:T(8,128)(2,1)S(1)}, bf16[960,80]{0,1:T(8,128)(2,1)}, u32[]{:S(2)}) copy-start(bf16[960,80]{0,1:T(8,128)(2,1)} %param.15) | copy-start | bytes 460804
  24.6 34.7 %all-to-all-start = ((bf16[4,256,960]{1,2,0:T(8,128)(2,1)}), bf16[4,256,960]{1,2,0:T(8,128)(2,1)}, u32[]{:S(2)}, u32[]{:S(2)}) async-start(bf16[4,256,960]{1,2,0:T(8,128)(2,1)} %param.11), calls=%async_computation | async-start | bytes 3932160 | tf_op jit(solution)/shard_map/all_to_all | solution.py:279
  30.8 10.5 %collective-permute-start.2 = (bf16[1,80,960]{2,1,0:T(8,128)(2,1)S(1)}, bf16[1,80,960]{2,1,0:T(8,128)(2,1)S(1)}, u32[]{:S(2)}, u32[]{:S(2)}) collective-permute-start(bf16[1,80,960]{2,1,0:T(8,128)(2,1)S(1)} %get-tuple-element.220), channel_id=1, source_target_pairs={{0,8},{4,12},{8,0},{12,4},{16,24},{20,28},{24,16},{28,20},{1,9},{5... | collective-permute-start | bytes 460808 | tf_op jit(solution)/shard_map/ppermute | solution.py:46
  34.7 9.8 %collective-permute-start.1 = (bf16[1,80,960]{2,1,0:T(8,128)(2,1)S(1)}, bf16[1,80,960]{2,1,0:T(8,128)(2,1)S(1)}, u32[]{:S(2)}, u32[]{:S(2)}) collective-permute-start(bf16[1,80,960]{2,1,0:T(8,128)(2,1)S(1)} %get-tuple-element.221), channel_id=1, source_target_pairs={{0,8},{4,12},{8,0},{12,4},{16,24},{20,28},{24,16},{28,20},{1,9},{5... | collective-permute-start | bytes 460808 | tf_op jit(solution)/shard_map/ppermute | solution.py:46
  44.6 22.8 %collective-permute-start.4 = (bf16[2,80,960]{2,1,0:T(8,128)(2,1)S(1)}, bf16[2,80,960]{2,1,0:T(8,128)(2,1)S(1)}, u32[]{:S(2)}, u32[]{:S(2)}) collective-permute-start(bf16[2,80,960]{2,1,0:T(8,128)(2,1)S(1)} %pad_maximum_fusion.8), channel_id=1, source_target_pairs={{0,2},{1,3},{2,0},{3,1},{4,6},{5,7},{6,4},{7,5},{8,10},{9,11},{10,... | collective-permute-start | bytes 921608 | tf_op jit(solution)/shard_map/ppermute | solution.py:46
  46.3 21.1 %collective-permute-start.3 = (bf16[2,80,960]{2,1,0:T(8,128)(2,1)S(1)}, bf16[2,80,960]{2,1,0:T(8,128)(2,1)S(1)}, u32[]{:S(2)}, u32[]{:S(2)}) collective-permute-start(bf16[2,80,960]{2,1,0:T(8,128)(2,1)S(1)} %pad_maximum_fusion.7), channel_id=1, source_target_pairs={{0,4},{4,0},{8,12},{12,8},{16,20},{20,16},{24,28},{28,24},{1,5},{5... | collective-permute-start | bytes 921608 | tf_op jit(solution)/shard_map/ppermute | solution.py:46
  49.7 89.4 %copy-start = (bf16[656,1024]{1,0:T(8,128)(2,1)}, bf16[656,1024]{1,0:T(8,128)(2,1)S(1)}, u32[]{:S(2)}) copy-start(bf16[656,1024]{1,0:T(8,128)(2,1)S(1)} %fusion.2.pick_ref.rest_5_) | copy-start | bytes 4030468
  67.4 4.8 %copy-start.10 = (bf16[2,80,960]{2,1,0:T(8,128)(2,1)}, bf16[2,80,960]{2,1,0:T(8,128)(2,1)S(1)}, u32[]{:S(2)}) copy-start(bf16[2,80,960]{2,1,0:T(8,128)(2,1)S(1)} %collective-permute-done.4) | copy-start | bytes 921604
  67.4 4.8 %copy-start.12 = (bf16[2,80,960]{2,1,0:T(8,128)(2,1)}, bf16[2,80,960]{2,1,0:T(8,128)(2,1)S(1)}, u32[]{:S(2)}) copy-start(bf16[2,80,960]{2,1,0:T(8,128)(2,1)S(1)} %collective-permute-done.3) | copy-start | bytes 921604
  67.6 16.3 %collective-permute-start.6 = (bf16[4,80,960]{2,1,0:T(8,128)(2,1)S(1)}, bf16[4,80,960]{2,1,0:T(8,128)(2,1)S(1)}, u32[]{:S(2)}, u32[]{:S(2)}) collective-permute-start(bf16[4,80,960]{2,1,0:T(8,128)(2,1)S(1)} %pad_maximum_fusion.3), channel_id=1, source_target_pairs={{0,4},{4,0},{8,12},{12,8},{16,20},{20,16},{24,28},{28,24},{1,5},{5... | collective-permute-start | bytes 1843208 | tf_op jit(solution)/shard_map/ppermute | solution.py:46
  69.1 16.0 %collective-permute-start.5 = (bf16[4,80,960]{2,1,0:T(8,128)(2,1)S(1)}, bf16[4,80,960]{2,1,0:T(8,128)(2,1)S(1)}, u32[]{:S(2)}, u32[]{:S(2)}) collective-permute-start(bf16[4,80,960]{2,1,0:T(8,128)(2,1)S(1)} %pad_maximum_fusion.2), channel_id=1, source_target_pairs={{0,2},{1,3},{2,0},{3,1},{4,6},{5,7},{6,4},{7,5},{8,10},{9,11},{10,... | collective-permute-start | bytes 1843208 | tf_op jit(solution)/shard_map/ppermute | solution.py:46
  83.9 2.4 copy-start.11
  86.3 1.5 copy-start.9
  87.6 4.8 %collective-permute-start.8 = (bf16[8,80,960]{2,1,0:T(8,128)(2,1)}, bf16[8,80,960]{2,1,0:T(8,128)(2,1)}, u32[]{:S(2)}, u32[]{:S(2)}) collective-permute-start(bf16[8,80,960]{2,1,0:T(8,128)(2,1)} %pad_maximum_fusion.1.mine1), channel_id=1, source_target_pairs={{0,1},{1,0},{2,3},{3,2},{4,5},{5,4},{6,7},{7,6},{8,9},{9,8},{10,11... | collective-permute-start | bytes 3686408 | tf_op jit(solution)/shard_map/ppermute | solution.py:46
  87.8 6.6 %collective-permute-start.7 = (bf16[8,80,960]{2,1,0:T(8,128)(2,1)S(1)}, bf16[8,80,960]{2,1,0:T(8,128)(2,1)}, u32[]{:S(2)}, u32[]{:S(2)}) collective-permute-start(bf16[8,80,960]{2,1,0:T(8,128)(2,1)S(1)} %pad_maximum_fusion.mine0), channel_id=1, source_target_pairs={{0,1},{1,0},{2,3},{3,2},{4,5},{5,4},{6,7},{7,6},{8,9},{9,8},{10,11... | collective-permute-start | bytes 3686408 | tf_op jit(solution)/shard_map/ppermute | solution.py:46
  100.4 4.7 %copy-start.14 = (f32[2,960]{1,0:T(2,128)S(1)}, f32[2,960]{1,0:T(2,128)}, u32[]{:S(2)}) copy-start(f32[2,960]{1,0:T(2,128)} %param.18) | copy-start | bytes 23044
  100.4 36.9 %all-to-all-start.2 = ((bf16[4,256,960]{1,2,0:T(8,128)(2,1)}), bf16[4,256,960]{1,2,0:T(8,128)(2,1)}, u32[]{:S(2)}, u32[]{:S(2)}) async-start(bf16[4,256,960]{1,2,0:T(8,128)(2,1)} %param.12), calls=%async_computation.2 | async-start | bytes 3932160 | tf_op jit(solution)/shard_map/all_to_all | solution.py:279
  176.1 6.2 %collective-permute-start.9 = (bf16[2,8,80,960]{3,2,1,0:T(8,128)(2,1)}, bf16[2,8,80,960]{3,2,1,0:T(8,128)(2,1)}, u32[]{:S(2)}, u32[]{:S(2)}) collective-permute-start(bf16[2,8,80,960]{3,2,1,0:T(8,128)(2,1)} %bitcast.307), channel_id=1, source_target_pairs={{0,1},{1,0},{2,3},{3,2},{4,5},{5,4},{6,7},{7,6},{8,9},{9,8},{10,11... | collective-permute-start | bytes 7372808 | tf_op jit(solution)/shard_map/ppermute | solution.py:46
  176.7 48.7 %all-to-all-start.3 = ((bf16[4,256,960]{1,2,0:T(8,128)(2,1)}), bf16[4,256,960]{1,2,0:T(8,128)(2,1)S(1)}, u32[]{:S(2)}, u32[]{:S(2)}) async-start(bf16[4,256,960]{1,2,0:T(8,128)(2,1)} %bitcast.288), calls=%async_computation.3 | async-start | bytes 3932160 | tf_op jit(solution)/shard_map/all_to_all | solution.py:279
  182.3 3.0 copy-start.6
  182.3 4.3 %copy-start.5 = (bf16[8,80,960]{2,1,0:T(8,128)(2,1)}, bf16[8,80,960]{2,1,0:T(8,128)(2,1)S(1)}, u32[]{:S(2)}) copy-start(bf16[8,80,960]{2,1,0:T(8,128)(2,1)S(1)} %get-tuple-element.216) | copy-start | bytes 3686404
  185.3 2.5 copy-start.7
  185.3 2.5 copy-start.8
  187.8 37.7 %collective-permute-start.10 = (bf16[4,80,960]{2,1,0:T(8,128)(2,1)}, bf16[4,80,960]{2,1,0:T(8,128)(2,1)}, u32[]{:S(2)}, u32[]{:S(2)}) collective-permute-start(bf16[4,80,960]{2,1,0:T(8,128)(2,1)} %fusion.4), channel_id=1, source_target_pairs={{0,2},{1,3},{2,0},{3,1},{4,6},{5,7},{6,4},{7,5},{8,10},{9,11},{10,... | collective-permute-start | bytes 1843208 | tf_op jit(solution)/shard_map/ppermute | solution.py:46
  189.7 35.7 %collective-permute-start.11 = (bf16[4,80,960]{2,1,0:T(8,128)(2,1)}, bf16[4,80,960]{2,1,0:T(8,128)(2,1)}, u32[]{:S(2)}, u32[]{:S(2)}) collective-permute-start(bf16[4,80,960]{2,1,0:T(8,128)(2,1)} %bitcast.23), channel_id=1, source_target_pairs={{0,4},{4,0},{8,12},{12,8},{16,20},{20,16},{24,28},{28,24},{1,5},{5... | collective-permute-start | bytes 1843208 | tf_op jit(solution)/shard_map/ppermute | solution.py:46
  225.4 8.9 %collective-permute-start.12 = (bf16[2,8,160,960]{3,2,1,0:T(8,128)(2,1)}, bf16[2,8,160,960]{3,2,1,0:T(8,128)(2,1)S(1)}, u32[]{:S(2)}, u32[]{:S(2)}) collective-permute-start(bf16[2,8,160,960]{3,2,1,0:T(8,128)(2,1)} %get-tuple-element.150), channel_id=1, source_target_pairs={{0,1},{1,0},{2,3},{3,2},{4,5},{5,4},{6,7},{7,6},{8,9},{9,8},{10,11... | collective-permute-start | bytes 14745608 | tf_op jit(solution)/shard_map/ppermute | solution.py:46
  228.7 6.5 %copy-start.2 = (bf16[1,8,160,960]{3,2,1,0:T(8,128)(2,1)}, bf16[1,8,160,960]{3,2,1,0:T(8,128)(2,1)S(1)}, u32[]{:S(2)}) copy-start(bf16[1,8,160,960]{3,2,1,0:T(8,128)(2,1)S(1)} %get-tuple-element.211) | copy-start | bytes 7372804
  228.7 8.6 %copy-start.1 = (bf16[1,8,160,960]{3,2,1,0:T(8,128)(2,1)}, bf16[1,8,160,960]{3,2,1,0:T(8,128)(2,1)S(1)}, u32[]{:S(2)}) copy-start(bf16[1,8,160,960]{3,2,1,0:T(8,128)(2,1)S(1)} %get-tuple-element.210) | copy-start | bytes 7372804
  235.2 2.1 copy-start.3
  235.2 3.7 copy-start.4
  238.9 38.2 %collective-permute-start.13 = (bf16[4,160,960]{2,1,0:T(8,128)(2,1)}, bf16[4,160,960]{2,1,0:T(8,128)(2,1)}, u32[]{:S(2)}, u32[]{:S(2)}) collective-permute-start(bf16[4,160,960]{2,1,0:T(8,128)(2,1)} %fusion.3), channel_id=1, source_target_pairs={{0,2},{1,3},{2,0},{3,1},{4,6},{5,7},{6,4},{7,5},{8,10},{9,11},{10,... | collective-permute-start | bytes 3686408 | tf_op jit(solution)/shard_map/ppermute | solution.py:46
  239.0 38.1 %collective-permute-start.14 = (bf16[4,160,960]{2,1,0:T(8,128)(2,1)}, bf16[4,160,960]{2,1,0:T(8,128)(2,1)}, u32[]{:S(2)}, u32[]{:S(2)}) collective-permute-start(bf16[4,160,960]{2,1,0:T(8,128)(2,1)} %bitcast.30), channel_id=1, source_target_pairs={{0,4},{4,0},{8,12},{12,8},{16,20},{20,16},{24,28},{28,24},{1,5},{5... | collective-permute-start | bytes 3686408 | tf_op jit(solution)/shard_map/ppermute | solution.py:46
  241.5 35.6 %collective-permute-start.15 = (bf16[2,80,960]{2,1,0:T(8,128)(2,1)}, bf16[2,80,960]{2,1,0:T(8,128)(2,1)}, u32[]{:S(2)}, u32[]{:S(2)}) collective-permute-start(bf16[2,80,960]{2,1,0:T(8,128)(2,1)} %fusion.16), channel_id=1, source_target_pairs={{0,4},{4,0},{8,12},{12,8},{16,20},{20,16},{24,28},{28,24},{1,5},{5... | collective-permute-start | bytes 921608 | tf_op jit(solution)/shard_map/ppermute | solution.py:46
  245.1 31.9 %collective-permute-start.16 = (bf16[2,80,960]{2,1,0:T(8,128)(2,1)}, bf16[2,80,960]{2,1,0:T(8,128)(2,1)}, u32[]{:S(2)}, u32[]{:S(2)}) collective-permute-start(bf16[2,80,960]{2,1,0:T(8,128)(2,1)} %fusion.17), channel_id=1, source_target_pairs={{0,2},{1,3},{2,0},{3,1},{4,6},{5,7},{6,4},{7,5},{8,10},{9,11},{10,... | collective-permute-start | bytes 921608 | tf_op jit(solution)/shard_map/ppermute | solution.py:46
  286.2 31.6 %collective-permute-start.17 = (bf16[2,160,960]{2,1,0:T(8,128)(2,1)}, bf16[2,160,960]{2,1,0:T(8,128)(2,1)}, u32[]{:S(2)}, u32[]{:S(2)}) collective-permute-start(bf16[2,160,960]{2,1,0:T(8,128)(2,1)} %fusion.5), channel_id=1, source_target_pairs={{0,4},{4,0},{8,12},{12,8},{16,20},{20,16},{24,28},{28,24},{1,5},{5... | collective-permute-start | bytes 1843208 | tf_op jit(solution)/shard_map/ppermute | solution.py:46
  286.7 31.1 %collective-permute-start.18 = (bf16[2,160,960]{2,1,0:T(8,128)(2,1)}, bf16[2,160,960]{2,1,0:T(8,128)(2,1)}, u32[]{:S(2)}, u32[]{:S(2)}) collective-permute-start(bf16[2,160,960]{2,1,0:T(8,128)(2,1)} %fusion.6), channel_id=1, source_target_pairs={{0,2},{1,3},{2,0},{3,1},{4,6},{5,7},{6,4},{7,5},{8,10},{9,11},{10,... | collective-permute-start | bytes 1843208 | tf_op jit(solution)/shard_map/ppermute | solution.py:46
  288.4 29.3 %collective-permute-start.19 = (bf16[1,80,960]{2,1,0:T(8,128)(2,1)}, bf16[1,80,960]{2,1,0:T(8,128)(2,1)}, u32[]{:S(2)}, u32[]{:S(2)}) collective-permute-start(bf16[1,80,960]{2,1,0:T(8,128)(2,1)} %fusion.30), channel_id=1, source_target_pairs={{0,8},{4,12},{8,0},{12,4},{16,24},{20,28},{24,16},{28,20},{1,9},{5... | collective-permute-start | bytes 460808 | tf_op jit(solution)/shard_map/ppermute | solution.py:46
  290.0 27.8 %collective-permute-start.20 = (bf16[1,80,960]{2,1,0:T(8,128)(2,1)}, bf16[1,80,960]{2,1,0:T(8,128)(2,1)}, u32[]{:S(2)}, u32[]{:S(2)}) collective-permute-start(bf16[1,80,960]{2,1,0:T(8,128)(2,1)} %fusion.27), channel_id=1, source_target_pairs={{0,8},{4,12},{8,0},{12,4},{16,24},{20,28},{24,16},{28,20},{1,9},{5... | collective-permute-start | bytes 460808 | tf_op jit(solution)/shard_map/ppermute | solution.py:46
  321.4 21.5 %collective-permute-start.21 = (bf16[2,8,80,960]{3,2,1,0:T(8,128)(2,1)}, bf16[2,8,80,960]{3,2,1,0:T(8,128)(2,1)}, u32[]{:S(2)}, u32[]{:S(2)}) collective-permute-start(bf16[2,8,80,960]{3,2,1,0:T(8,128)(2,1)} %bitcast.53), channel_id=1, source_target_pairs={{0,1},{1,0},{2,3},{3,2},{4,5},{5,4},{6,7},{7,6},{8,9},{9,8},{10,11... | collective-permute-start | bytes 7372808 | tf_op jit(solution)/shard_map/ppermute | solution.py:46
  329.2 70.6 %all-to-all-start.4 = ((bf16[4,256,960]{1,2,0:T(8,128)(2,1)}), bf16[4,256,960]{1,2,0:T(8,128)(2,1)S(1)}, u32[]{:S(2)}, u32[]{:S(2)}) async-start(bf16[4,256,960]{1,2,0:T(8,128)(2,1)} %bitcast.287), calls=%async_computation.4 | async-start | bytes 3932160 | tf_op jit(solution)/shard_map/all_to_all | solution.py:279
  333.1 9.7 %collective-permute-start.22 = (f32[4,960]{1,0:T(4,128)S(1)}, f32[4,960]{1,0:T(4,128)S(1)}, u32[]{:S(2)}, u32[]{:S(2)}) collective-permute-start(f32[4,960]{1,0:T(4,128)S(1)} %pad_maximum_fusion.9), channel_id=1, source_target_pairs={{0,16},{4,20},{8,24},{12,28},{16,0},{20,4},{24,8},{28,12},{1,17},{... | collective-permute-start | bytes 46088 | tf_op jit(solution)/shard_map/ppermute | solution.py:46
  337.2 13.7 %collective-permute-start.34 = (bf16[1,160,960]{2,1,0:T(8,128)(2,1)S(1)}, bf16[1,160,960]{2,1,0:T(8,128)(2,1)S(1)}, u32[]{:S(2)}, u32[]{:S(2)}) collective-permute-start(bf16[1,160,960]{2,1,0:T(8,128)(2,1)S(1)} %fusion.13), channel_id=1, source_target_pairs={{0,8},{4,12},{8,0},{12,4},{16,24},{20,28},{24,16},{28,20},{1,9},{5... | collective-permute-start | bytes 921608 | tf_op jit(solution)/shard_map/ppermute | solution.py:46
  340.3 18.1 %collective-permute-start.35 = (bf16[1,160,960]{2,1,0:T(8,128)(2,1)S(1)}, bf16[1,160,960]{2,1,0:T(8,128)(2,1)S(1)}, u32[]{:S(2)}, u32[]{:S(2)}) collective-permute-start(bf16[1,160,960]{2,1,0:T(8,128)(2,1)S(1)} %fusion.9), channel_id=1, source_target_pairs={{0,8},{4,12},{8,0},{12,4},{16,24},{20,28},{24,16},{28,20},{1,9},{5... | collective-permute-start | bytes 921608 | tf_op jit(solution)/shard_map/ppermute | solution.py:46
  345.1 32.4 %collective-permute-start.24 = (bf16[4,80,960]{2,1,0:T(8,128)(2,1)S(1)}, bf16[4,80,960]{2,1,0:T(8,128)(2,1)S(1)}, u32[]{:S(2)}, u32[]{:S(2)}) collective-permute-start(bf16[4,80,960]{2,1,0:T(8,128)(2,1)S(1)} %bitcast.293), channel_id=1, source_target_pairs={{0,8},{4,12},{8,0},{12,4},{16,24},{20,28},{24,16},{28,20},{1,9},{5... | collective-permute-start | bytes 1843208 | tf_op jit(solution)/shard_map/ppermute | solution.py:46
  347.0 30.6 %collective-permute-start.23 = (bf16[4,80,960]{2,1,0:T(8,128)(2,1)S(1)}, bf16[4,80,960]{2,1,0:T(8,128)(2,1)S(1)}, u32[]{:S(2)}, u32[]{:S(2)}) collective-permute-start(bf16[4,80,960]{2,1,0:T(8,128)(2,1)S(1)} %bitcast.294), channel_id=1, source_target_pairs={{0,4},{4,0},{8,12},{12,8},{16,20},{20,16},{24,28},{28,24},{1,5},{5... | collective-permute-start | bytes 1843208 | tf_op jit(solution)/shard_map/ppermute | solution.py:46
  350.0 30.1 %collective-permute-start.37 = (bf16[80,960]{1,0:T(8,128)(2,1)S(1)}, bf16[80,960]{1,0:T(8,128)(2,1)S(1)}, u32[]{:S(2)}, u32[]{:S(2)}) collective-permute-start(bf16[80,960]{1,0:T(8,128)(2,1)S(1)} %fusion.41), channel_id=1, source_target_pairs={{0,16},{4,20},{8,24},{12,28},{16,0},{20,4},{24,8},{28,12},{1,17},{... | collective-permute-start | bytes 460808 | tf_op jit(solution)/shard_map/ppermute | solution.py:46
  350.8 26.7 %collective-permute-start.25 = (f32[4,960]{1,0:T(4,128)S(1)}, f32[4,960]{1,0:T(4,128)S(1)}, u32[]{:S(2)}, u32[]{:S(2)}) collective-permute-start(f32[4,960]{1,0:T(4,128)S(1)} %fusion.44), channel_id=1, source_target_pairs={{0,8},{4,12},{8,0},{12,4},{16,24},{20,28},{24,16},{28,20},{1,9},{5... | collective-permute-start | bytes 46088 | tf_op jit(solution)/shard_map/ppermute | solution.py:46
  360.7 32.6 %collective-permute-start.36 = (bf16[160,960]{1,0:T(8,128)(2,1)S(1)}, bf16[160,960]{1,0:T(8,128)(2,1)S(1)}, u32[]{:S(2)}, u32[]{:S(2)}) collective-permute-start(bf16[160,960]{1,0:T(8,128)(2,1)S(1)} %fusion.18), channel_id=1, source_target_pairs={{0,16},{4,20},{8,24},{12,28},{16,0},{20,4},{24,8},{28,12},{1,17},{... | collective-permute-start | bytes 921608 | tf_op jit(solution)/shard_map/ppermute | solution.py:46
  377.7 9.4 %collective-permute-start.27 = (bf16[2,80,960]{2,1,0:T(8,128)(2,1)S(1)}, bf16[2,80,960]{2,1,0:T(8,128)(2,1)S(1)}, u32[]{:S(2)}, u32[]{:S(2)}) collective-permute-start(bf16[2,80,960]{2,1,0:T(8,128)(2,1)S(1)} %bitcast.296), channel_id=1, source_target_pairs={{0,4},{4,0},{8,12},{12,8},{16,20},{20,16},{24,28},{28,24},{1,5},{5... | collective-permute-start | bytes 921608 | tf_op jit(solution)/shard_map/ppermute | solution.py:46
  379.5 8.8 %collective-permute-start.26 = (bf16[2,80,960]{2,1,0:T(8,128)(2,1)S(1)}, bf16[2,80,960]{2,1,0:T(8,128)(2,1)S(1)}, u32[]{:S(2)}, u32[]{:S(2)}) collective-permute-start(bf16[2,80,960]{2,1,0:T(8,128)(2,1)S(1)} %bitcast.297), channel_id=1, source_target_pairs={{0,8},{4,12},{8,0},{12,4},{16,24},{20,28},{24,16},{28,20},{1,9},{5... | collective-permute-start | bytes 921608 | tf_op jit(solution)/shard_map/ppermute | solution.py:46
  379.6 7.5 %collective-permute-start.28 = (f32[4,960]{1,0:T(4,128)S(1)}, f32[4,960]{1,0:T(4,128)S(1)}, u32[]{:S(2)}, u32[]{:S(2)}) collective-permute-start(f32[4,960]{1,0:T(4,128)S(1)} %fusion.58), channel_id=1, source_target_pairs={{0,4},{4,0},{8,12},{12,8},{16,20},{20,16},{24,28},{28,24},{1,5},{5... | collective-permute-start | bytes 46088 | tf_op jit(solution)/shard_map/ppermute | solution.py:46
  388.3 8.1 %collective-permute-start.31 = (f32[4,960]{1,0:T(4,128)S(1)}, f32[4,960]{1,0:T(4,128)S(1)}, u32[]{:S(2)}, u32[]{:S(2)}) collective-permute-start(f32[4,960]{1,0:T(4,128)S(1)} %add.656), channel_id=1, source_target_pairs={{0,2},{1,3},{2,0},{3,1},{4,6},{5,7},{6,4},{7,5},{8,10},{9,11},{10,... | collective-permute-start | bytes 46088 | tf_op jit(solution)/shard_map/ppermute | solution.py:46
  391.1 5.7 %collective-permute-start.30 = (bf16[1,80,960]{2,1,0:T(8,128)(2,1)S(1)}, bf16[1,80,960]{2,1,0:T(8,128)(2,1)S(1)}, u32[]{:S(2)}, u32[]{:S(2)}) collective-permute-start(bf16[1,80,960]{2,1,0:T(8,128)(2,1)S(1)} %get-tuple-element.206), channel_id=1, source_target_pairs={{0,2},{1,3},{2,0},{3,1},{4,6},{5,7},{6,4},{7,5},{8,10},{9,11},{10,... | collective-permute-start | bytes 460808 | tf_op jit(solution)/shard_map/ppermute | solution.py:46
  391.6 6.9 %collective-permute-start.29 = (bf16[1,80,960]{2,1,0:T(8,128)(2,1)S(1)}, bf16[1,80,960]{2,1,0:T(8,128)(2,1)S(1)}, u32[]{:S(2)}, u32[]{:S(2)}) collective-permute-start(bf16[1,80,960]{2,1,0:T(8,128)(2,1)S(1)} %get-tuple-element.207), channel_id=1, source_target_pairs={{0,2},{1,3},{2,0},{3,1},{4,6},{5,7},{6,4},{7,5},{8,10},{9,11},{10,... | collective-permute-start | bytes 460808 | tf_op jit(solution)/shard_map/ppermute | solution.py:46
  399.8 6.5 %collective-permute-start.32 = (f32[4,960]{1,0:T(4,128)S(1)}, f32[4,960]{1,0:T(4,128)S(1)}, u32[]{:S(2)}, u32[]{:S(2)}) collective-permute-start(f32[4,960]{1,0:T(4,128)S(1)} %add.670), channel_id=1, source_target_pairs={{0,1},{1,0},{2,3},{3,2},{4,5},{5,4},{6,7},{7,6},{8,9},{9,8},{10,11... | collective-permute-start | bytes 46088 | tf_op jit(solution)/shard_map/ppermute | solution.py:46
  399.9 11.0 %collective-permute-start.33 = (bf16[80,960]{1,0:T(8,128)(2,1)S(1)}, bf16[80,960]{1,0:T(8,128)(2,1)S(1)}, u32[]{:S(2)}, u32[]{:S(2)}) collective-permute-start(bf16[80,960]{1,0:T(8,128)(2,1)S(1)} %get-tuple-element.204), channel_id=1, source_target_pairs={{0,16},{4,20},{8,24},{12,28},{16,0},{20,4},{24,8},{28,12},{1,17},{... | collective-permute-start | bytes 460808 | tf_op jit(solution)/shard_map/ppermute | solution.py:46
Sparse Core Ops, SparseCore 0:
  11.5 130.1 all-gather.2

commit v4 on v3

--- a/solution.py
+++ b/solution.py
@@ -338,13 +338,13 @@
     keys[:ROWS] = key
     vals[:ROWS] = value
     for head in range(PER_KV):
-        q_ref[head] = rotated[head].astype(BF16)
+        q_ref[head] = (rotated[head] * 0.125).astype(BF16)
     lanes = lax.broadcasted_iota(jnp.int32, (1, 128), 1)
     for start, stop, reach in TILES:
         outs = []
         logs = jnp.zeros((stop - start, 128), F32)
         for head in range(PER_KV):
-            scores = nt(q_ref[head, start:stop], keys[:reach]) * 0.125 + bias[start:stop, :reach]
+            scores = nt(q_ref[head, start:stop], keys[:reach]) + bias[start:stop, :reach]
             top = jnp.max(scores, axis=-1, keepdims=True)
             expd = jnp.exp(scores - top)
             total = jnp.sum(expd, axis=-1, keepdims=True)
@@ -714,7 +714,7 @@
         for start, stop, reach in TILES:
             end = start + TILE
             reach = min(reach, ROWS)
-            scores = nt(key[:reach], wide_q[start:end]) * 0.125 + bias[:reach, start:end]
+            scores = nt(key[:reach], wide_q[start:end]) + bias[:reach, start:end]
             probs = jnp.exp(scores - l_ref[0, head : head + 1, start:end])
             d_probs = nt(value[:reach], wide_do[start:end])
             d_scores = (probs * (d_probs - inside[0:1, start:end])).astype(BF16)
@@ -729,7 +729,7 @@
             dq[start:end] = tn(d_scores, key[:reach]) * 0.125
         d_queries.append(dq[:ROWS])
     turned_back = turned(
-        jnp.concatenate(d_queries + [d_key * 0.125], axis=1), cos_ref[...], -sin_ref[...]
+        jnp.concatenate(d_queries + [d_key], axis=1), cos_ref[...], -sin_ref[...]
     )
     d_mixed = jnp.concatenate(turned_back + [d_value], axis=1).astype(BF16)
     stage[: per + 2 * HEAD] = tn(d_mixed, n1_ref[...]).astype(BF16)
@@ -931,7 +931,7 @@
     while attn.step < len(bits):
         start(attn, wide, down, total)
         if attn.step < len(bits):
-            wait([attn, total])
+            out_home = wait([attn, total], out_home)
             take(wide, down)
     grad_home, attn.mine = join(grad_home, attn.mine)
     take(attn, wide, down, total)

time: 428 us -> 426 us (level)
  no operation moved by 1% of the time
where the time goes in v4:
time: 426 us; the launch traced here: 418 us
  Pallas kernels  162 us (38%)
  waiting for transfers between devices  78 us (18%)
  starting transfers between devices  62.8 us (15%)
  other arithmetic  61.9 us (15%)
  local copies, waits for them, and re-layouts  28.4 us (7%)
  between operations  20.3 us (5%)
  matrix products  5.38 us (1%)
    ppermute x38, waiting for transfers between devices, swap(): return lax.ppermute(value, name, pairs)  68.3 us
    pallas_call x2, Pallas kernels, attend_back(): pl.pallas_call(functools.partial(attend_back_kernel, first, final), grid=...  56.7 us
    ppermute x38, starting transfers between devices, swap(): return lax.ppermute(value, name, pairs)  41.8 us
    pallas_call x1, Pallas kernels, feed_back(): pl.pallas_call(feed_back_kernel, grid=(FF // SLAB,), in_specs=[fixed(ROWS...  34.1 us
    pallas_call x1, Pallas kernels, attend(): pl.pallas_call(attend_kernel, grid=(KV_HEADS,), in_specs=[fixed(ROWS, D),...  30.6 us
    pallas_call x1, Pallas kernels, feed(): pl.pallas_call(feed_kernel, grid=(FF // SLAB,), in_specs=[fixed(ROWS, D),...  26.2 us
    convert_element_type x17, other arithmetic, cut(): self.outs.append(self.choose(half, choice).astype(BF16))  24 us
    all_to_all x5, starting transfers between devices, to_sequence(): lax.all_to_all(blocks, 'ctx', split_axis=0, concat_axis=0, tiled=True)  20.9 us
  transfers between devices with their start and end apart: 44, of which 17 were waited for; matrix products, arithmetic and copies ran while one was open for 18% of the time, Pallas kernels for 30%

profile of v4, /device:TPU:0, one launch (start us, length us, event | category | flops | bytes accessed | tf_op | source)
XLA Modules:
  0.0 418.5 jit_solution(9373352520336362499)
XLA Ops:
  7.2 1.9 pad_maximum_fusion.4
  11.1 4.3 %all-to-all-start.1 = ((s32[4,1,256]{2,1,0:T(1,128)}), s32[4,1,256]{2,1,0:T(1,128)S(1)}, u32[]{:S(2)}, u32[]{:S(2)}) async-start(s32[4,1,256]{2,1,0:T(1,128)} %reshape.808), calls=%async_computation.1 | async-start | bytes 8192 | tf_op jit(solution)/shard_map/all_to_all | solution.py:279
  15.4 3.1 collective-permute-start
  19.9 3.8 select_reduce_fusion.1
  24.6 4.6 %all-to-all-start = ((bf16[4,256,960]{1,2,0:T(8,128)(2,1)}), bf16[4,256,960]{1,2,0:T(8,128)(2,1)}, u32[]{:S(2)}, u32[]{:S(2)}) async-start(bf16[4,256,960]{1,2,0:T(8,128)(2,1)} %param.11), calls=%async_computation | async-start | bytes 3932160 | tf_op jit(solution)/shard_map/all_to_all | solution.py:279
  30.9 3.9 collective-permute-start.2
  38.6 2.8 collective-permute-done.2
  41.4 3.2 collective-permute-done.1
  44.6 1.7 collective-permute-start.4
  46.3 1.6 collective-permute-start.3
  49.7 9.6 %all-to-all-done = bf16[4,256,960]{1,2,0:T(8,128)(2,1)} async-done(((bf16[4,256,960]{1,2,0:T(8,128)(2,1)}), bf16[4,256,960]{1,2,0:T(8,128)(2,1)}, u32[]{:S(2)}, u32[]{:S(2)}) %all-to-all-start) | async-done | bytes 1966112 | tf_op jit(solution)/shard_map/all_to_all | solution.py:279
  59.4 1.8 copy.170
  61.2 6.3 %collective-permute-done.4 = bf16[2,80,960]{2,1,0:T(8,128)(2,1)S(1)} collective-permute-done((bf16[2,80,960]{2,1,0:T(8,128)(2,1)S(1)}, bf16[2,80,960]{2,1,0:T(8,128)(2,1)S(1)}, u32[]{:S(2)}, u32[]{:S(2)}) %collective-permute-start.4) | collective-permute-done | bytes 307232 | tf_op jit(solution)/shard_map/ppermute | solution.py:46
  69.5 2.7 convolution_convert_fusion.1.x_ref.rest_3_
  72.2 11.7 %collective-permute-done.6 = bf16[4,80,960]{2,1,0:T(8,128)(2,1)S(1)} collective-permute-done((bf16[4,80,960]{2,1,0:T(8,128)(2,1)S(1)}, bf16[4,80,960]{2,1,0:T(8,128)(2,1)S(1)}, u32[]{:S(2)}, u32[]{:S(2)}) %collective-permute-start.6) | collective-permute-done | bytes 614432 | tf_op jit(solution)/shard_map/ppermute | solution.py:46
  88.8 3.6 collective-permute-done.8.other1
  92.4 2.0 collective-permute-done.7.other0
  94.4 5.9 %order.1 = bf16[2,8,2,80,960]{4,3,2,1,0:T(8,128)(2,1)} custom-call(s32[5]{0:T(128)} %stack.60.own, bf16[8,80,960]{2,1,0:T(8,128)(2,1)} %copy-done.12, bf16[8,80,960]{2,1,0:T(8,128)(2,1)} %collective-permute-done.7.other0, bf16[8,80,960]{2,1,0:T(8,128)(2,1)} %pad_maximum_fusion.1.mine1, bf16[8,80,960]{2,1,0:T(8,128)(2,1)} %collective-permute-done.8.other1), custom_call_target="tpu_custom_call" | custom-call | tf_op jit(solution)/shard_map/order/pallas_call | solution.py:135
  100.3 4.6 %all-to-all-start.2 = ((bf16[4,256,960]{1,2,0:T(8,128)(2,1)}), bf16[4,256,960]{1,2,0:T(8,128)(2,1)}, u32[]{:S(2)}, u32[]{:S(2)}) async-start(bf16[4,256,960]{1,2,0:T(8,128)(2,1)} %param.12), calls=%async_computation.2 | async-start | bytes 3932160 | tf_op jit(solution)/shard_map/all_to_all | solution.py:279
  106.5 30.6 %attend.1 = (bf16[656,960]{1,0:T(8,128)(2,1)}, bf16[15,656,64]{2,1,0:T(8,128)(2,1)}, bf16[5,656,64]{2,1,0:T(8,128)(2,1)}, bf16[5,656,64]{2,1,0:T(8,128)(2,1)}, b...) custom-call(bf16[656,960]{1,0:T(8,128)(2,1)} %convolution_convert_fusion.1.x_ref.rest_3_, ...), custom_call_target="tpu_custom_call" | custom-call | tf_op jit(solution)/shard_map/attend/pallas_call | solution.py:365
  137.2 1.8 copy.171
  139.0 2.7 convolution_convert_fusion.t_ref
  141.7 26.2 %feed.1 = (bf16[656,960]{1,0:T(8,128)(2,1)}, bf16[656,2560]{1,0:T(8,128)(2,1)}, bf16[656,2560]{1,0:T(8,128)(2,1)}, bf16[656,2560]{1,0:T(8,128)(2,1)}, bf16[4,960...) custom-call(f32[656,960]{1,0:T(8,128)} %get-tuple-element.131.h1_ref, ...), custom_call_target="tpu_custom_call" | custom-call | tf_op jit(solution)/shard_map/feed/pallas_call | solution.py:488
  167.9 8.1 %down_grad.1 = (bf16[16,80,960]{2,1,0:T(8,128)(2,1)}, bf16[16,80,960]{2,1,0:T(8,128)(2,1)}) custom-call(bf16[656,2560]{1,0:T(8,128)(2,1)} %get-tuple-element.139.hid_ref, bf16[656,960]{1,0:T(8,128)(2,1)} %get-tuple-element.144.d_ffn_ref, s32[1]{0:T(128)} %bitcast.11.core_ref), custom_call_target="tpu_custom_call" | custom-call | tf_op jit(solution)/shard_map/down_grad/pallas_call | solution.py:552
  176.4 3.6 all-to-all-start.3
  180.0 2.0 fusion.48
  182.1 2.9 fusion.49
  187.5 2.0 collective-permute-start.10
  189.5 1.7 collective-permute-start.11
  191.2 34.1 %feed_back.1 = (bf16[2,8,160,960]{3,2,1,0:T(8,128)(2,1)}, bf16[2,8,160,960]{3,2,1,0:T(8,128)(2,1)}, bf16[656,960]{1,0:T(8,128)(2,1)}, f32[656,960]{1,0:T(8,128)}, f32[8,960]{1,0:T(8,128)}) custom-call(f32[656,960]{1,0:T(8,128)} %get-tuple-element.131.h1_ref, bf16[656,960]{1,0:T(8,128)(2,1)} %get-tuple-element.133.n2_ref, ...), custom_call_target="tpu_custom_call" | custom-call | tf_op jit(solution)/shard_map/feed_back/pallas_call | solution.py:625
  225.4 3.7 fusion.45
  229.2 5.1 %collective-permute-done.12 = bf16[2,8,160,960]{3,2,1,0:T(8,128)(2,1)S(1)} collective-permute-done((bf16[2,8,160,960]{3,2,1,0:T(8,128)(2,1)}, bf16[2,8,160,960]{3,2,1,0:T(8,128)(2,1)S(1)}, u32[]{:S(2)}, u32[]{:S(2)}) %collective-permute-start.12) | collective-permute-done | bytes 4915232 | tf_op jit(solution)/shard_map/ppermute | solution.py:46
  235.1 2.0 fusion.3
  237.1 1.6 add_convert_fusion
  239.2 2.1 fusion.16
  241.2 1.7 collective-permute-start.15
  242.9 2.0 fusion.17
  244.9 1.9 collective-permute-start.16
  246.8 29.4 %attend_back.2 = (bf16[2560,960]{1,0:T(8,128)(2,1)}, f32[656,960]{1,0:T(8,128)}) custom-call(bf16[656,960]{1,0:T(8,128)(2,1)} %get-tuple-element.157.da_ref, bf16[656,960]{1,0:T(8,128)(2,1)} %get-tuple-element.158.n1_ref, f32[656,64]{1,0:T(8,128)} %get-tuple-element.123.cos_ref, f32[656,64]{1,0:T(8,128)} %get-tuple-element.124.sin_ref, ...), custom_call_target="tpu_custom_call" | custom-call | tf_op jit(solution)/shard_map/attend_back/pallas_call | solution.py:767
  276.9 1.8 fusion.30
  278.8 1.8 fusion.27
  280.6 2.7 fusion.5
  283.2 2.7 fusion.6
  286.3 1.7 collective-permute-start.18
  288.0 1.7 collective-permute-start.19
  290.0 27.3 %attend_back.3 = (bf16[2560,960]{1,0:T(8,128)(2,1)}, f32[656,960]{1,0:T(8,128)}, bf16[4,960,256]{2,1,0:T(8,128)(2,1)}, f32[8,960]{1,0:T(8,128)}) custom-call(bf16[656,960]{1,0:T(8,128)(2,1)} %get-tuple-element.157.da_ref, bf16[656,960]{1,0:T(8,128)(2,1)} %get-tuple-element.158.n1_ref, ...), custom_call_target="tpu_custom_call", output_to_operand_aliasing={{0}: (18, {})} | custom-call | tf_op jit(solution)/shard_map/attend_back/pallas_call | solution.py:767
  317.4 3.6 constant_dynamic-slice_fusion.1
  325.9 3.8 all-to-all-start.4
  329.8 2.7 collective-permute-start.22
  337.6 2.0 constant_dynamic-slice_fusion.2
  339.7 2.0 fusion.47
  348.0 7.1 %collective-permute-done.35 = bf16[1,160,960]{2,1,0:T(8,128)(2,1)S(1)} collective-permute-done((bf16[1,160,960]{2,1,0:T(8,128)(2,1)S(1)}, bf16[1,160,960]{2,1,0:T(8,128)(2,1)S(1)}, u32[]{:S(2)}, u32[]{:S(2)}) %collective-permute-start.35) | collective-permute-done | bytes 307232 | tf_op jit(solution)/shard_map/ppermute | solution.py:46
  355.1 2.3 fusion.18
  357.5 16.7 %collective-permute-done.25 = f32[4,960]{1,0:T(4,128)S(1)} collective-permute-done((f32[4,960]{1,0:T(4,128)S(1)}, f32[4,960]{1,0:T(4,128)S(1)}, u32[]{:S(2)}, u32[]{:S(2)}) %collective-permute-start.25) | collective-permute-done | bytes 15392 | tf_op jit(solution)/shard_map/ppermute | solution.py:46
  374.4 1.7 collective-permute-start.27
  376.8 2.3 fusion.31
  379.1 4.7 %collective-permute-done.28 = f32[4,960]{1,0:T(4,128)S(1)} collective-permute-done((f32[4,960]{1,0:T(4,128)S(1)}, f32[4,960]{1,0:T(4,128)S(1)}, u32[]{:S(2)}, u32[]{:S(2)}) %collective-permute-start.28) | collective-permute-done | bytes 15392 | tf_op jit(solution)/shard_map/ppermute | solution.py:46
  385.0 1.6 collective-permute-start.31
  388.3 1.6 collective-permute-start.29
  389.9 3.2 fusion.7
  393.5 1.8 collective-permute-done.29
  396.6 1.6 collective-permute-start.33
  398.3 4.8 %convert_select_fusion = f32[4,256,960]{1,2,0:T(8,128)} fusion(bf16[4,256,960]{1,2,0:T(8,128)(2,1)S(1)} %all-to-all-done.4, bf16[4,256,960]{1,2,0:T(8,128)(2,1)} %param.12, bf16[4,256,960]{1,2,0:T(8,128)(2,1)} %param.11, f32[4,256]{1,0:T(4,128)S(1)} %get-tuple-element.237, pred[4,256]{1,0:T(4,128)(4,1)S(1)} %broadcast_compare_fusion), kind=kLoop, calls=%fused_computation.2 | loop fusion | flops 5898240 | bytes 9835520 | tf_op jit(solution)/shard_map/jit(_where)/select_n | solution.py:942
  403.1 3.0 broadcast_select_fusion
  (167 shorter events, 47.4 us)
Async XLA Ops:
  7.2 134.5 %all-gather.3.cloned.1.call-start = ((), (), s32[]{:S(2)}) async-start(), calls=%async_computation.5 | async-start | bytes 16220160 | tf_op jit(solution)/shard_map/all_gather | solution.py:825
  11.1 13.5 %all-to-all-start.1 = ((s32[4,1,256]{2,1,0:T(1,128)}), s32[4,1,256]{2,1,0:T(1,128)S(1)}, u32[]{:S(2)}, u32[]{:S(2)}) async-start(s32[4,1,256]{2,1,0:T(1,128)} %reshape.808), calls=%async_computation.1 | async-start | bytes 8192 | tf_op jit(solution)/shard_map/all_to_all | solution.py:279
  15.4 13.8 %collective-permute-start = (bf16[1,80,960]{2,1,0:T(8,128)(2,1)}, bf16[1,80,960]{2,1,0:T(8,128)(2,1)S(1)}, u32[]{:S(2)}, u32[]{:S(2)}) collective-permute-start(bf16[1,80,960]{2,1,0:T(8,128)(2,1)} %bitcast.298), channel_id=1, source_target_pairs={{0,16},{4,20},{8,24},{12,28},{16,0},{20,4},{24,8},{28,12},{1,17},{... | collective-permute-start | bytes 460808 | tf_op jit(solution)/shard_map/ppermute | solution.py:46
  24.6 6.2 %copy-start.20 = (bf16[960,80]{0,1:T(8,128)(2,1)S(1)}, bf16[960,80]{0,1:T(8,128)(2,1)}, u32[]{:S(2)}) copy-start(bf16[960,80]{0,1:T(8,128)(2,1)} %param.15) | copy-start | bytes 460804
  24.6 34.8 %all-to-all-start = ((bf16[4,256,960]{1,2,0:T(8,128)(2,1)}), bf16[4,256,960]{1,2,0:T(8,128)(2,1)}, u32[]{:S(2)}, u32[]{:S(2)}) async-start(bf16[4,256,960]{1,2,0:T(8,128)(2,1)} %param.11), calls=%async_computation | async-start | bytes 3932160 | tf_op jit(solution)/shard_map/all_to_all | solution.py:279
  30.9 10.5 %collective-permute-start.2 = (bf16[1,80,960]{2,1,0:T(8,128)(2,1)S(1)}, bf16[1,80,960]{2,1,0:T(8,128)(2,1)S(1)}, u32[]{:S(2)}, u32[]{:S(2)}) collective-permute-start(bf16[1,80,960]{2,1,0:T(8,128)(2,1)S(1)} %get-tuple-element.226), channel_id=1, source_target_pairs={{0,8},{4,12},{8,0},{12,4},{16,24},{20,28},{24,16},{28,20},{1,9},{5... | collective-permute-start | bytes 460808 | tf_op jit(solution)/shard_map/ppermute | solution.py:46
  34.7 9.8 %collective-permute-start.1 = (bf16[1,80,960]{2,1,0:T(8,128)(2,1)S(1)}, bf16[1,80,960]{2,1,0:T(8,128)(2,1)S(1)}, u32[]{:S(2)}, u32[]{:S(2)}) collective-permute-start(bf16[1,80,960]{2,1,0:T(8,128)(2,1)S(1)} %get-tuple-element.227), channel_id=1, source_target_pairs={{0,8},{4,12},{8,0},{12,4},{16,24},{20,28},{24,16},{28,20},{1,9},{5... | collective-permute-start | bytes 460808 | tf_op jit(solution)/shard_map/ppermute | solution.py:46
  44.6 22.9 %collective-permute-start.4 = (bf16[2,80,960]{2,1,0:T(8,128)(2,1)S(1)}, bf16[2,80,960]{2,1,0:T(8,128)(2,1)S(1)}, u32[]{:S(2)}, u32[]{:S(2)}) collective-permute-start(bf16[2,80,960]{2,1,0:T(8,128)(2,1)S(1)} %pad_maximum_fusion.8), channel_id=1, source_target_pairs={{0,2},{1,3},{2,0},{3,1},{4,6},{5,7},{6,4},{7,5},{8,10},{9,11},{10,... | collective-permute-start | bytes 921608 | tf_op jit(solution)/shard_map/ppermute | solution.py:46
  46.3 21.1 %collective-permute-start.3 = (bf16[2,80,960]{2,1,0:T(8,128)(2,1)S(1)}, bf16[2,80,960]{2,1,0:T(8,128)(2,1)S(1)}, u32[]{:S(2)}, u32[]{:S(2)}) collective-permute-start(bf16[2,80,960]{2,1,0:T(8,128)(2,1)S(1)} %pad_maximum_fusion.7), channel_id=1, source_target_pairs={{0,4},{4,0},{8,12},{12,8},{16,20},{20,16},{24,28},{28,24},{1,5},{5... | collective-permute-start | bytes 921608 | tf_op jit(solution)/shard_map/ppermute | solution.py:46
  49.7 89.3 %copy-start = (bf16[656,1024]{1,0:T(8,128)(2,1)}, bf16[656,1024]{1,0:T(8,128)(2,1)S(1)}, u32[]{:S(2)}) copy-start(bf16[656,1024]{1,0:T(8,128)(2,1)S(1)} %fusion.2.pick_ref.rest_5_) | copy-start | bytes 4030468
  67.4 4.8 %copy-start.13 = (bf16[2,80,960]{2,1,0:T(8,128)(2,1)}, bf16[2,80,960]{2,1,0:T(8,128)(2,1)S(1)}, u32[]{:S(2)}) copy-start(bf16[2,80,960]{2,1,0:T(8,128)(2,1)S(1)} %collective-permute-done.4) | copy-start | bytes 921604
  67.4 4.8 %copy-start.15 = (bf16[2,80,960]{2,1,0:T(8,128)(2,1)}, bf16[2,80,960]{2,1,0:T(8,128)(2,1)S(1)}, u32[]{:S(2)}) copy-start(bf16[2,80,960]{2,1,0:T(8,128)(2,1)S(1)} %collective-permute-done.3) | copy-start | bytes 921604
  67.6 16.3 %collective-permute-start.6 = (bf16[4,80,960]{2,1,0:T(8,128)(2,1)S(1)}, bf16[4,80,960]{2,1,0:T(8,128)(2,1)S(1)}, u32[]{:S(2)}, u32[]{:S(2)}) collective-permute-start(bf16[4,80,960]{2,1,0:T(8,128)(2,1)S(1)} %pad_maximum_fusion.3), channel_id=1, source_target_pairs={{0,4},{4,0},{8,12},{12,8},{16,20},{20,16},{24,28},{28,24},{1,5},{5... | collective-permute-start | bytes 1843208 | tf_op jit(solution)/shard_map/ppermute | solution.py:46
  69.1 16.0 %collective-permute-start.5 = (bf16[4,80,960]{2,1,0:T(8,128)(2,1)S(1)}, bf16[4,80,960]{2,1,0:T(8,128)(2,1)S(1)}, u32[]{:S(2)}, u32[]{:S(2)}) collective-permute-start(bf16[4,80,960]{2,1,0:T(8,128)(2,1)S(1)} %pad_maximum_fusion.2), channel_id=1, source_target_pairs={{0,2},{1,3},{2,0},{3,1},{4,6},{5,7},{6,4},{7,5},{8,10},{9,11},{10,... | collective-permute-start | bytes 1843208 | tf_op jit(solution)/shard_map/ppermute | solution.py:46
  83.9 2.4 copy-start.14
  87.7 4.7 %collective-permute-start.8 = (bf16[8,80,960]{2,1,0:T(8,128)(2,1)}, bf16[8,80,960]{2,1,0:T(8,128)(2,1)}, u32[]{:S(2)}, u32[]{:S(2)}) collective-permute-start(bf16[8,80,960]{2,1,0:T(8,128)(2,1)} %pad_maximum_fusion.1.mine1), channel_id=1, source_target_pairs={{0,1},{1,0},{2,3},{3,2},{4,5},{5,4},{6,7},{7,6},{8,9},{9,8},{10,11... | collective-permute-start | bytes 3686408 | tf_op jit(solution)/shard_map/ppermute | solution.py:46
  87.8 6.6 %collective-permute-start.7 = (bf16[8,80,960]{2,1,0:T(8,128)(2,1)S(1)}, bf16[8,80,960]{2,1,0:T(8,128)(2,1)}, u32[]{:S(2)}, u32[]{:S(2)}) collective-permute-start(bf16[8,80,960]{2,1,0:T(8,128)(2,1)S(1)} %pad_maximum_fusion.mine0), channel_id=1, source_target_pairs={{0,1},{1,0},{2,3},{3,2},{4,5},{5,4},{6,7},{7,6},{8,9},{9,8},{10,11... | collective-permute-start | bytes 3686408 | tf_op jit(solution)/shard_map/ppermute | solution.py:46
  100.3 4.7 %copy-start.21 = (f32[2,960]{1,0:T(2,128)S(1)}, f32[2,960]{1,0:T(2,128)}, u32[]{:S(2)}) copy-start(f32[2,960]{1,0:T(2,128)} %param.18) | copy-start | bytes 23044
  100.3 36.8 %all-to-all-start.2 = ((bf16[4,256,960]{1,2,0:T(8,128)(2,1)}), bf16[4,256,960]{1,2,0:T(8,128)(2,1)}, u32[]{:S(2)}, u32[]{:S(2)}) async-start(bf16[4,256,960]{1,2,0:T(8,128)(2,1)} %param.12), calls=%async_computation.2 | async-start | bytes 3932160 | tf_op jit(solution)/shard_map/all_to_all | solution.py:279
  176.0 6.1 %collective-permute-start.9 = (bf16[2,8,80,960]{3,2,1,0:T(8,128)(2,1)}, bf16[2,8,80,960]{3,2,1,0:T(8,128)(2,1)}, u32[]{:S(2)}, u32[]{:S(2)}) collective-permute-start(bf16[2,8,80,960]{3,2,1,0:T(8,128)(2,1)} %bitcast.307), channel_id=1, source_target_pairs={{0,1},{1,0},{2,3},{3,2},{4,5},{5,4},{6,7},{7,6},{8,9},{9,8},{10,11... | collective-permute-start | bytes 7372808 | tf_op jit(solution)/shard_map/ppermute | solution.py:46
  176.4 48.9 %all-to-all-start.3 = ((bf16[4,256,960]{1,2,0:T(8,128)(2,1)}), bf16[4,256,960]{1,2,0:T(8,128)(2,1)S(1)}, u32[]{:S(2)}, u32[]{:S(2)}) async-start(bf16[4,256,960]{1,2,0:T(8,128)(2,1)} %bitcast.288), calls=%async_computation.3 | async-start | bytes 3932160 | tf_op jit(solution)/shard_map/all_to_all | solution.py:279
  182.0 4.3 %copy-start.7 = (bf16[8,80,960]{2,1,0:T(8,128)(2,1)}, bf16[8,80,960]{2,1,0:T(8,128)(2,1)S(1)}, u32[]{:S(2)}) copy-start(bf16[8,80,960]{2,1,0:T(8,128)(2,1)S(1)} %get-tuple-element.222) | copy-start | bytes 3686404
  182.0 5.4 %copy-start.9 = (bf16[8,80,960]{2,1,0:T(8,128)(2,1)}, bf16[8,80,960]{2,1,0:T(8,128)(2,1)S(1)}, u32[]{:S(2)}) copy-start(bf16[8,80,960]{2,1,0:T(8,128)(2,1)S(1)} %get-tuple-element.223) | copy-start | bytes 3686404
  185.0 2.4 copy-start.10
  185.0 2.4 copy-start.11
  187.5 37.9 %collective-permute-start.10 = (bf16[4,80,960]{2,1,0:T(8,128)(2,1)}, bf16[4,80,960]{2,1,0:T(8,128)(2,1)}, u32[]{:S(2)}, u32[]{:S(2)}) collective-permute-start(bf16[4,80,960]{2,1,0:T(8,128)(2,1)} %fusion.4), channel_id=1, source_target_pairs={{0,2},{1,3},{2,0},{3,1},{4,6},{5,7},{6,4},{7,5},{8,10},{9,11},{10,... | collective-permute-start | bytes 1843208 | tf_op jit(solution)/shard_map/ppermute | solution.py:46
  189.5 35.8 %collective-permute-start.11 = (bf16[4,80,960]{2,1,0:T(8,128)(2,1)}, bf16[4,80,960]{2,1,0:T(8,128)(2,1)}, u32[]{:S(2)}, u32[]{:S(2)}) collective-permute-start(bf16[4,80,960]{2,1,0:T(8,128)(2,1)} %bitcast.23), channel_id=1, source_target_pairs={{0,4},{4,0},{8,12},{12,8},{16,20},{20,16},{24,28},{28,24},{1,5},{5... | collective-permute-start | bytes 1843208 | tf_op jit(solution)/shard_map/ppermute | solution.py:46
  225.3 3.9 copy-start.5
  225.3 8.9 %collective-permute-start.12 = (bf16[2,8,160,960]{3,2,1,0:T(8,128)(2,1)}, bf16[2,8,160,960]{3,2,1,0:T(8,128)(2,1)S(1)}, u32[]{:S(2)}, u32[]{:S(2)}) collective-permute-start(bf16[2,8,160,960]{3,2,1,0:T(8,128)(2,1)} %get-tuple-element.153), channel_id=1, source_target_pairs={{0,1},{1,0},{2,3},{3,2},{4,5},{5,4},{6,7},{7,6},{8,9},{9,8},{10,11... | collective-permute-start | bytes 14745608 | tf_op jit(solution)/shard_map/ppermute | solution.py:46
  229.2 5.9 %copy-start.2 = (bf16[1,8,160,960]{3,2,1,0:T(8,128)(2,1)}, bf16[1,8,160,960]{3,2,1,0:T(8,128)(2,1)S(1)}, u32[]{:S(2)}) copy-start(bf16[1,8,160,960]{3,2,1,0:T(8,128)(2,1)S(1)} %get-tuple-element.217) | copy-start | bytes 7372804
  229.2 7.9 %copy-start.1 = (bf16[1,8,160,960]{3,2,1,0:T(8,128)(2,1)}, bf16[1,8,160,960]{3,2,1,0:T(8,128)(2,1)S(1)}, u32[]{:S(2)}) copy-start(bf16[1,8,160,960]{3,2,1,0:T(8,128)(2,1)S(1)} %get-tuple-element.216) | copy-start | bytes 7372804
  235.1 3.7 copy-start.4
  237.1 5.8 %copy-start.8 = (bf16[8,80,960]{2,1,0:T(8,128)(2,1)S(1)}, bf16[8,80,960]{2,1,0:T(8,128)(2,1)}, u32[]{:S(2)}) copy-start(bf16[8,80,960]{2,1,0:T(8,128)(2,1)} %copy-done.7) | copy-start | bytes 3686404
  238.7 38.2 %collective-permute-start.13 = (bf16[4,160,960]{2,1,0:T(8,128)(2,1)}, bf16[4,160,960]{2,1,0:T(8,128)(2,1)}, u32[]{:S(2)}, u32[]{:S(2)}) collective-permute-start(bf16[4,160,960]{2,1,0:T(8,128)(2,1)} %fusion.3), channel_id=1, source_target_pairs={{0,2},{1,3},{2,0},{3,1},{4,6},{5,7},{6,4},{7,5},{8,10},{9,11},{10,... | collective-permute-start | bytes 3686408 | tf_op jit(solution)/shard_map/ppermute | solution.py:46
  238.8 38.1 %collective-permute-start.14 = (bf16[4,160,960]{2,1,0:T(8,128)(2,1)}, bf16[4,160,960]{2,1,0:T(8,128)(2,1)}, u32[]{:S(2)}, u32[]{:S(2)}) collective-permute-start(bf16[4,160,960]{2,1,0:T(8,128)(2,1)} %bitcast.30), channel_id=1, source_target_pairs={{0,4},{4,0},{8,12},{12,8},{16,20},{20,16},{24,28},{28,24},{1,5},{5... | collective-permute-start | bytes 3686408 | tf_op jit(solution)/shard_map/ppermute | solution.py:46
  241.2 35.6 %collective-permute-start.15 = (bf16[2,80,960]{2,1,0:T(8,128)(2,1)}, bf16[2,80,960]{2,1,0:T(8,128)(2,1)S(1)}, u32[]{:S(2)}, u32[]{:S(2)}) collective-permute-start(bf16[2,80,960]{2,1,0:T(8,128)(2,1)} %fusion.16), channel_id=1, source_target_pairs={{0,4},{4,0},{8,12},{12,8},{16,20},{20,16},{24,28},{28,24},{1,5},{5... | collective-permute-start | bytes 921608 | tf_op jit(solution)/shard_map/ppermute | solution.py:46
  244.9 32.0 %collective-permute-start.16 = (bf16[2,80,960]{2,1,0:T(8,128)(2,1)}, bf16[2,80,960]{2,1,0:T(8,128)(2,1)}, u32[]{:S(2)}, u32[]{:S(2)}) collective-permute-start(bf16[2,80,960]{2,1,0:T(8,128)(2,1)} %fusion.17), channel_id=1, source_target_pairs={{0,2},{1,3},{2,0},{3,1},{4,6},{5,7},{6,4},{7,5},{8,10},{9,11},{10,... | collective-permute-start | bytes 921608 | tf_op jit(solution)/shard_map/ppermute | solution.py:46
  276.8 6.4 %copy-start.16 = (bf16[2,80,960]{2,1,0:T(8,128)(2,1)}, bf16[2,80,960]{2,1,0:T(8,128)(2,1)S(1)}, u32[]{:S(2)}) copy-start(bf16[2,80,960]{2,1,0:T(8,128)(2,1)S(1)} %collective-permute-done.15) | copy-start | bytes 921604
  285.9 31.5 %collective-permute-start.17 = (bf16[2,160,960]{2,1,0:T(8,128)(2,1)}, bf16[2,160,960]{2,1,0:T(8,128)(2,1)}, u32[]{:S(2)}, u32[]{:S(2)}) collective-permute-start(bf16[2,160,960]{2,1,0:T(8,128)(2,1)} %fusion.5), channel_id=1, source_target_pairs={{0,4},{4,0},{8,12},{12,8},{16,20},{20,16},{24,28},{28,24},{1,5},{5... | collective-permute-start | bytes 1843208 | tf_op jit(solution)/shard_map/ppermute | solution.py:46
  286.3 31.1 %collective-permute-start.18 = (bf16[2,160,960]{2,1,0:T(8,128)(2,1)}, bf16[2,160,960]{2,1,0:T(8,128)(2,1)}, u32[]{:S(2)}, u32[]{:S(2)}) collective-permute-start(bf16[2,160,960]{2,1,0:T(8,128)(2,1)} %fusion.6), channel_id=1, source_target_pairs={{0,2},{1,3},{2,0},{3,1},{4,6},{5,7},{6,4},{7,5},{8,10},{9,11},{10,... | collective-permute-start | bytes 1843208 | tf_op jit(solution)/shard_map/ppermute | solution.py:46
  288.0 29.4 %collective-permute-start.19 = (bf16[1,80,960]{2,1,0:T(8,128)(2,1)}, bf16[1,80,960]{2,1,0:T(8,128)(2,1)S(1)}, u32[]{:S(2)}, u32[]{:S(2)}) collective-permute-start(bf16[1,80,960]{2,1,0:T(8,128)(2,1)} %fusion.30), channel_id=1, source_target_pairs={{0,8},{4,12},{8,0},{12,4},{16,24},{20,28},{24,16},{28,20},{1,9},{5... | collective-permute-start | bytes 460808 | tf_op jit(solution)/shard_map/ppermute | solution.py:46
  289.7 27.6 %collective-permute-start.20 = (bf16[1,80,960]{2,1,0:T(8,128)(2,1)}, bf16[1,80,960]{2,1,0:T(8,128)(2,1)S(1)}, u32[]{:S(2)}, u32[]{:S(2)}) collective-permute-start(bf16[1,80,960]{2,1,0:T(8,128)(2,1)} %fusion.27), channel_id=1, source_target_pairs={{0,8},{4,12},{8,0},{12,4},{16,24},{20,28},{24,16},{28,20},{1,9},{5... | collective-permute-start | bytes 460808 | tf_op jit(solution)/shard_map/ppermute | solution.py:46
  317.4 3.6 copy-start.18
  321.0 18.6 %collective-permute-start.21 = (bf16[2,8,80,960]{3,2,1,0:T(8,128)(2,1)}, bf16[2,8,80,960]{3,2,1,0:T(8,128)(2,1)}, u32[]{:S(2)}, u32[]{:S(2)}) collective-permute-start(bf16[2,8,80,960]{3,2,1,0:T(8,128)(2,1)} %bitcast.51), channel_id=1, source_target_pairs={{0,1},{1,0},{2,3},{3,2},{4,5},{5,4},{6,7},{7,6},{8,9},{9,8},{10,11... | collective-permute-start | bytes 7372808 | tf_op jit(solution)/shard_map/ppermute | solution.py:46
  325.9 70.7 %all-to-all-start.4 = ((bf16[4,256,960]{1,2,0:T(8,128)(2,1)}), bf16[4,256,960]{1,2,0:T(8,128)(2,1)S(1)}, u32[]{:S(2)}, u32[]{:S(2)}) async-start(bf16[4,256,960]{1,2,0:T(8,128)(2,1)} %bitcast.287), calls=%async_computation.4 | async-start | bytes 3932160 | tf_op jit(solution)/shard_map/all_to_all | solution.py:279
  329.8 9.9 %collective-permute-start.22 = (f32[4,960]{1,0:T(4,128)S(1)}, f32[4,960]{1,0:T(4,128)S(1)}, u32[]{:S(2)}, u32[]{:S(2)}) collective-permute-start(f32[4,960]{1,0:T(4,128)S(1)} %pad_maximum_fusion.9), channel_id=1, source_target_pairs={{0,16},{4,20},{8,24},{12,28},{16,0},{20,4},{24,8},{28,12},{1,17},{... | collective-permute-start | bytes 46088 | tf_op jit(solution)/shard_map/ppermute | solution.py:46
  334.0 13.5 %collective-permute-start.34 = (bf16[1,160,960]{2,1,0:T(8,128)(2,1)S(1)}, bf16[1,160,960]{2,1,0:T(8,128)(2,1)S(1)}, u32[]{:S(2)}, u32[]{:S(2)}) collective-permute-start(bf16[1,160,960]{2,1,0:T(8,128)(2,1)S(1)} %fusion.13), channel_id=1, source_target_pairs={{0,8},{4,12},{8,0},{12,4},{16,24},{20,28},{24,16},{28,20},{1,9},{5... | collective-permute-start | bytes 921608 | tf_op jit(solution)/shard_map/ppermute | solution.py:46
  337.0 18.1 %collective-permute-start.35 = (bf16[1,160,960]{2,1,0:T(8,128)(2,1)S(1)}, bf16[1,160,960]{2,1,0:T(8,128)(2,1)S(1)}, u32[]{:S(2)}, u32[]{:S(2)}) collective-permute-start(bf16[1,160,960]{2,1,0:T(8,128)(2,1)S(1)} %fusion.9), channel_id=1, source_target_pairs={{0,8},{4,12},{8,0},{12,4},{16,24},{20,28},{24,16},{28,20},{1,9},{5... | collective-permute-start | bytes 921608 | tf_op jit(solution)/shard_map/ppermute | solution.py:46
  341.7 3.4 copy-start.17
  341.7 3.4 copy-start.19
  341.9 32.3 %collective-permute-start.24 = (bf16[4,80,960]{2,1,0:T(8,128)(2,1)S(1)}, bf16[4,80,960]{2,1,0:T(8,128)(2,1)S(1)}, u32[]{:S(2)}, u32[]{:S(2)}) collective-permute-start(bf16[4,80,960]{2,1,0:T(8,128)(2,1)S(1)} %bitcast.293), channel_id=1, source_target_pairs={{0,8},{4,12},{8,0},{12,4},{16,24},{20,28},{24,16},{28,20},{1,9},{5... | collective-permute-start | bytes 1843208 | tf_op jit(solution)/shard_map/ppermute | solution.py:46
  343.7 30.5 %collective-permute-start.23 = (bf16[4,80,960]{2,1,0:T(8,128)(2,1)S(1)}, bf16[4,80,960]{2,1,0:T(8,128)(2,1)S(1)}, u32[]{:S(2)}, u32[]{:S(2)}) collective-permute-start(bf16[4,80,960]{2,1,0:T(8,128)(2,1)S(1)} %bitcast.294), channel_id=1, source_target_pairs={{0,4},{4,0},{8,12},{12,8},{16,20},{20,16},{24,28},{28,24},{1,5},{5... | collective-permute-start | bytes 1843208 | tf_op jit(solution)/shard_map/ppermute | solution.py:46
  346.6 30.2 %collective-permute-start.37 = (bf16[80,960]{1,0:T(8,128)(2,1)S(1)}, bf16[80,960]{1,0:T(8,128)(2,1)S(1)}, u32[]{:S(2)}, u32[]{:S(2)}) collective-permute-start(bf16[80,960]{1,0:T(8,128)(2,1)S(1)} %fusion.41), channel_id=1, source_target_pairs={{0,16},{4,20},{8,24},{12,28},{16,0},{20,4},{24,8},{28,12},{1,17},{... | collective-permute-start | bytes 460808 | tf_op jit(solution)/shard_map/ppermute | solution.py:46
  347.4 26.8 %collective-permute-start.25 = (f32[4,960]{1,0:T(4,128)S(1)}, f32[4,960]{1,0:T(4,128)S(1)}, u32[]{:S(2)}, u32[]{:S(2)}) collective-permute-start(f32[4,960]{1,0:T(4,128)S(1)} %fusion.44), channel_id=1, source_target_pairs={{0,8},{4,12},{8,0},{12,4},{16,24},{20,28},{24,16},{28,20},{1,9},{5... | collective-permute-start | bytes 46088 | tf_op jit(solution)/shard_map/ppermute | solution.py:46
  357.4 32.5 %collective-permute-start.36 = (bf16[160,960]{1,0:T(8,128)(2,1)S(1)}, bf16[160,960]{1,0:T(8,128)(2,1)S(1)}, u32[]{:S(2)}, u32[]{:S(2)}) collective-permute-start(bf16[160,960]{1,0:T(8,128)(2,1)S(1)} %fusion.18), channel_id=1, source_target_pairs={{0,16},{4,20},{8,24},{12,28},{16,0},{20,4},{24,8},{28,12},{1,17},{... | collective-permute-start | bytes 921608 | tf_op jit(solution)/shard_map/ppermute | solution.py:46
  374.4 9.4 %collective-permute-start.27 = (bf16[2,80,960]{2,1,0:T(8,128)(2,1)S(1)}, bf16[2,80,960]{2,1,0:T(8,128)(2,1)S(1)}, u32[]{:S(2)}, u32[]{:S(2)}) collective-permute-start(bf16[2,80,960]{2,1,0:T(8,128)(2,1)S(1)} %bitcast.296), channel_id=1, source_target_pairs={{0,4},{4,0},{8,12},{12,8},{16,20},{20,16},{24,28},{28,24},{1,5},{5... | collective-permute-start | bytes 921608 | tf_op jit(solution)/shard_map/ppermute | solution.py:46
  376.2 8.8 %collective-permute-start.26 = (bf16[2,80,960]{2,1,0:T(8,128)(2,1)S(1)}, bf16[2,80,960]{2,1,0:T(8,128)(2,1)S(1)}, u32[]{:S(2)}, u32[]{:S(2)}) collective-permute-start(bf16[2,80,960]{2,1,0:T(8,128)(2,1)S(1)} %bitcast.297), channel_id=1, source_target_pairs={{0,8},{4,12},{8,0},{12,4},{16,24},{20,28},{24,16},{28,20},{1,9},{5... | collective-permute-start | bytes 921608 | tf_op jit(solution)/shard_map/ppermute | solution.py:46
  376.4 7.4 %collective-permute-start.28 = (f32[4,960]{1,0:T(4,128)S(1)}, f32[4,960]{1,0:T(4,128)S(1)}, u32[]{:S(2)}, u32[]{:S(2)}) collective-permute-start(f32[4,960]{1,0:T(4,128)S(1)} %fusion.58), channel_id=1, source_target_pairs={{0,4},{4,0},{8,12},{12,8},{16,20},{20,16},{24,28},{28,24},{1,5},{5... | collective-permute-start | bytes 46088 | tf_op jit(solution)/shard_map/ppermute | solution.py:46
  385.0 8.1 %collective-permute-start.31 = (f32[4,960]{1,0:T(4,128)S(1)}, f32[4,960]{1,0:T(4,128)S(1)}, u32[]{:S(2)}, u32[]{:S(2)}) collective-permute-start(f32[4,960]{1,0:T(4,128)S(1)} %add.669), channel_id=1, source_target_pairs={{0,2},{1,3},{2,0},{3,1},{4,6},{5,7},{6,4},{7,5},{8,10},{9,11},{10,... | collective-permute-start | bytes 46088 | tf_op jit(solution)/shard_map/ppermute | solution.py:46
  387.8 5.7 %collective-permute-start.30 = (bf16[1,80,960]{2,1,0:T(8,128)(2,1)S(1)}, bf16[1,80,960]{2,1,0:T(8,128)(2,1)S(1)}, u32[]{:S(2)}, u32[]{:S(2)}) collective-permute-start(bf16[1,80,960]{2,1,0:T(8,128)(2,1)S(1)} %get-tuple-element.212), channel_id=1, source_target_pairs={{0,2},{1,3},{2,0},{3,1},{4,6},{5,7},{6,4},{7,5},{8,10},{9,11},{10,... | collective-permute-start | bytes 460808 | tf_op jit(solution)/shard_map/ppermute | solution.py:46
  388.3 6.9 %collective-permute-start.29 = (bf16[1,80,960]{2,1,0:T(8,128)(2,1)S(1)}, bf16[1,80,960]{2,1,0:T(8,128)(2,1)S(1)}, u32[]{:S(2)}, u32[]{:S(2)}) collective-permute-start(bf16[1,80,960]{2,1,0:T(8,128)(2,1)S(1)} %get-tuple-element.213), channel_id=1, source_target_pairs={{0,2},{1,3},{2,0},{3,1},{4,6},{5,7},{6,4},{7,5},{8,10},{9,11},{10,... | collective-permute-start | bytes 460808 | tf_op jit(solution)/shard_map/ppermute | solution.py:46
  396.5 9.6 %collective-permute-start.32 = (f32[4,960]{1,0:T(4,128)S(1)}, f32[4,960]{1,0:T(4,128)S(1)}, u32[]{:S(2)}, u32[]{:S(2)}) collective-permute-start(f32[4,960]{1,0:T(4,128)S(1)} %add.670), channel_id=1, source_target_pairs={{0,1},{1,0},{2,3},{3,2},{4,5},{5,4},{6,7},{7,6},{8,9},{9,8},{10,11... | collective-permute-start | bytes 46088 | tf_op jit(solution)/shard_map/ppermute | solution.py:46
  396.6 6.5 %copy-start.6 = (bf16[4,256,960]{1,2,0:T(8,128)(2,1)S(1)}, bf16[4,256,960]{1,2,0:T(8,128)(2,1)}, u32[]{:S(2)}) copy-start(bf16[4,256,960]{1,2,0:T(8,128)(2,1)} %copy-done.5) | copy-start | bytes 5898244
  396.6 12.6 %collective-permute-start.33 = (bf16[80,960]{1,0:T(8,128)(2,1)S(1)}, bf16[80,960]{1,0:T(8,128)(2,1)S(1)}, u32[]{:S(2)}, u32[]{:S(2)}) collective-permute-start(bf16[80,960]{1,0:T(8,128)(2,1)S(1)} %get-tuple-element.210), channel_id=1, source_target_pairs={{0,16},{4,20},{8,24},{12,28},{16,0},{20,4},{24,8},{28,12},{1,17},{... | collective-permute-start | bytes 460808 | tf_op jit(solution)/shard_map/ppermute | solution.py:46
  (2 other events, 3.5 us)
Sparse Core Ops, SparseCore 0:
  11.5 130.1 all-gather.2
